TPU v7x, 128 devices: a whole 4x4x4 slice. The times are simulated.
128 devices in a mesh: dp: 128 (over x, z, y, core).
Axes of the slice: x: 4, y: 4, z: 4, core: 2. Of those that a mesh axis runs over, the one named last changes fastest.
Arguments:
- partials: bfloat16 [128, 256, 16384], P('dp'), may hold values from -96 to 96
- master: float32 [256, 16384], P('dp'), may hold values from -3 to 3
- moment_one: float32 [256, 16384], P('dp'), may hold values from -2 to 2
- moment_two: float32 [256, 16384], P('dp'), may hold values from 0.01 to 1
Outputs:
- master_new: float32 [256, 16384], P('dp')
- moment_one_new: float32 [256, 16384], P('dp')
- moment_two_new: float32 [256, 16384], P('dp')
- reduced_grad: float32 [256, 16384], P('dp')
- weights: bfloat16 [256, 16384], replicated
All inputs are finite; a program needn't handle non-finite values. Where the computation divides by a largest or mean magnitude, that divisor is 1e-20 or more.
Results may differ from a plain program's by a relative error of at most 0.012.
Values may be sent and summed in bfloat16 or wider, within the bound.
No kernel may reach another device: no remote copies, remote signals or barrier semaphores. Data moves between devices by JAX's collectives and lax.ppermute only.
A program may use at most 128 MiB of HBM per device.

v0:
```python
import jax
import jax.numpy as jnp
from jax import lax
from jax.sharding import PartitionSpec as P

BLOCK = 128
MBITS = 7
STEP = 20


def block_scale(amax):
    powers = jnp.asarray([2.0**k for k in range(-20, 13)], jnp.float32)
    doubled = jnp.asarray([2.0 ** (k + 1) for k in range(-20, 13)], jnp.float32)
    inverse = jnp.asarray([2.0 ** (MBITS - k - 1) for k in range(-20, 13)], jnp.float32)
    hit = amax[..., None] >= powers
    scale = jnp.max(jnp.where(hit, doubled, jnp.float32(2.0 ** (-20))), axis=-1)
    mult = jnp.min(jnp.where(hit, inverse, jnp.float32(2.0 ** (MBITS + 20))), axis=-1)
    return (scale, mult)


def per_device(partials, master, moment_one, moment_two):
    devices = lax.axis_size("dp")
    local = partials[0]
    rows = local.shape[0]
    width = local.shape[1]
    nblk = width // BLOCK
    owned = master.shape[0]
    mags = jnp.abs(local.astype(jnp.float32)).reshape(rows, nblk, BLOCK)
    shared = lax.pmax(jnp.max(mags, axis=2).astype(jnp.bfloat16), "dp").astype(jnp.float32)
    scale_all, mult = block_scale(shared)
    vals = local.astype(jnp.float32).reshape(rows, nblk, BLOCK) * mult[:, :, None]
    mant = jnp.floor(vals + 0.5).reshape(rows, width)
    total = lax.psum_scatter(mant, "dp", scatter_dimension=0, tiled=True)
    start = lax.axis_index("dp") * owned
    scale = lax.dynamic_slice_in_dim(scale_all, start, owned, 0)
    total = total.reshape(owned, nblk, BLOCK)
    factor = scale / (2.0**MBITS * devices)
    reduced_grad = (total * factor[:, :, None]).reshape(owned, width)
    moment_one_new = 0.9 * moment_one + 0.1 * reduced_grad
    moment_two_new = 0.95 * moment_two + 0.05 * reduced_grad * reduced_grad
    first = moment_one_new / (1.0 - 0.9**STEP)
    second = moment_two_new / (1.0 - 0.95**STEP)
    update = first / (jnp.sqrt(second) + 1e-08)
    master_new = master - 0.001 * (update + 0.1 * master)
    blocks = master_new.reshape(owned, nblk, BLOCK)
    wscale = jnp.max(jnp.abs(blocks), axis=2) + 1e-06
    wmant = (blocks / wscale[:, :, None]).astype(jnp.bfloat16)
    own_weights = (
        (wmant.astype(jnp.float32) * wscale[:, :, None]).reshape(owned, width).astype(jnp.bfloat16)
    )
    weights = lax.all_gather(own_weights, "dp", axis=0, tiled=True)
    return (master_new, moment_one_new, moment_two_new, reduced_grad, weights)


def solution(mesh):
    in_specs = (P("dp", None, None), P("dp", None), P("dp", None), P("dp", None))
    out_specs = (P("dp", None), P("dp", None), P("dp", None), P("dp", None), P())
    return jax.shard_map(
        per_device, mesh=mesh, in_specs=in_specs, out_specs=out_specs, check_vma=False
    )
```

profile of v0, /device:TPU:1, one launch (start us, length us, event | category | flops | bytes accessed | tf_op | source)
XLA Modules:
  0.0 503.3 jit_solution(18436078014050203146)
XLA Ops:
  7.2 0.0 all-reduce.4.cloned.1.call-start
  7.2 9.6 %fusion.3 = bf16[32,8,128,128]{3,1,2,0:T(8,128)(2,1)} fusion(bf16[1,256,16384]{2,1,0:T(8,128)(2,1)} %param.7), kind=kLoop, calls=%fused_computation.5 | loop fusion | flops 12582912 | bytes 16777216
  16.8 9.2 %copy.12 = bf16[32,8,128,128]{3,2,1,0:T(8,128)(2,1)} copy(bf16[32,8,128,128]{3,1,2,0:T(8,128)(2,1)} %fusion.3) | data formatting | bytes 16777216
  26.0 0.0 copy-start.4
  26.0 0.0 copy-start.5
  26.0 0.0 copy-start.6
  26.0 6.4 %reduce_max.27 = bf16[256,128]{1,0:T(8,128)(2,1)} reduce(bf16[256,128,128]{2,1,0:T(8,128)(2,1)} %bitcast.40, bf16[]{:T(256)} %constant.71), dimensions={2}, to_apply=%region_0.0 | reduce | flops 4161536 | bytes 8454146 | tf_op jit(solution)/shard_map/reduce_max | solution.py:29
  32.3 0.0 all-reduce.4.cloned.1.call-update
  32.4 0.0 all-reduce.6.cloned.1.call-start
  32.4 141.3 %all-reduce.4.cloned.1.call-done = bf16[256,128]{1,0:T(8,128)(2,1)} async-done(((bf16[256,128]{1,0:T(8,128)(2,1)}), bf16[256,128]{1,0:T(8,128)(2,1)}) %all-reduce.4.cloned.1.call-update) | async-done | bytes 65552 | tf_op jit(solution)/shard_map/pmax | solution.py:29
  173.7 0.8 convert_element_type.38
  174.6 0.0 copy-done.4
  174.6 0.0 copy-done.5
  174.6 0.0 copy-done.6
  174.6 0.8 fusion.4
  175.4 4.6 mul.67
  180.0 17.3 %fusion.2 = f32[256,16384]{1,0:T(8,128)} fusion(bf16[1,256,16384]{2,1,0:T(8,128)(2,1)} %param.7, f32[32,8,128,128]{3,2,1,0:T(8,128)S(1)} %bitcast.39), kind=kLoop, calls=%fused_computation.4 | loop fusion | flops 16777216 | bytes 41943040 | tf_op jit(solution)/shard_map/floor | solution.py:32
  197.3 0.0 all-reduce.6.cloned.1.call-update
  197.3 0.0 all-gather.3.cloned.1.call-start
  197.4 0.1 broadcast_bitcast_fusion.1
  197.5 213.8 %all-reduce.6.cloned.1.call-done = f32[256,16384]{1,0:T(8,128)} async-done(((f32[256,16384]{1,0:T(8,128)}), f32[256,16384]{1,0:T(8,128)}) %all-reduce.6.cloned.1.call-update) | async-done | bytes 16777232
  411.3 0.0 copy-done.1
  411.3 0.0 copy-done.2
  411.3 0.0 copy-done.3
  411.3 2.3 abs_bitcast_fusion
  413.6 0.1 bitcast_reduce_fusion
  413.7 0.1 broadcast_bitcast_fusion
  413.8 0.8 fusion.9
  414.6 0.0 all-gather.3.cloned.1.call-update
  414.6 69.1 %all-gather.3.cloned.1.call-done = bf16[128,2,16384]{2,1,0:T(2,128)(2,1)} async-done(((bf16[1,2,16384]{2,1,0:T(2,128)(2,1)}), bf16[128,2,16384]{2,1,0:T(2,128)(2,1)}) %all-gather.3.cloned.1.call-update) | async-done | bytes 8388624 | tf_op jit(solution)/shard_map/all_gather | solution.py:51
  483.7 13.0 %reshape.38 = bf16[256,16384]{1,0:T(8,128)(2,1)} reshape(bf16[128,2,16384]{2,1,0:T(2,128)(2,1)} %all-gather.3.cloned.1.call-done) | data formatting | bytes 16777216
  496.8 0.0 copy-done
  (6 shorter events, 0.0 us)
Async XLA Ops:
  7.2 166.5 %all-reduce.4.cloned.1.call-start = ((), (), s32[]{:S(2)}) async-start(), calls=%async_computation | async-start | bytes 131072 | tf_op jit(solution)/shard_map/pmax | solution.py:29
  26.0 148.6 %copy-start.4 = (f32[33]{0:T(128)S(1)}, f32[33]{0:T(128)}, u32[]{:S(2)}) copy-start(f32[33]{0:T(128)} %constant.49.clone) | copy-start | bytes 400
  26.0 148.6 %copy-start.5 = (f32[33]{0:T(128)S(1)}, f32[33]{0:T(128)}, u32[]{:S(2)}) copy-start(f32[33]{0:T(128)} %constant.50.clone) | copy-start | bytes 400
  26.0 148.6 %copy-start.6 = (f32[33]{0:T(128)S(1)}, f32[33]{0:T(128)}, u32[]{:S(2)}) copy-start(f32[33]{0:T(128)} %constant.51.clone) | copy-start | bytes 400
  32.4 378.9 %all-reduce.6.cloned.1.call-start = ((), (), s32[]{:S(2)}) async-start(), calls=%async_computation.2 | async-start | bytes 33554432
  197.3 214.0 %copy-start.1 = (f32[2,16384]{1,0:T(2,128)S(1)}, f32[2,16384]{1,0:T(2,128)}, u32[]{:S(2)}) copy-start(f32[2,16384]{1,0:T(2,128)} %param.8) | copy-start | bytes 393220
  197.3 214.0 %copy-start.2 = (f32[2,16384]{1,0:T(2,128)S(1)}, f32[2,16384]{1,0:T(2,128)}, u32[]{:S(2)}) copy-start(f32[2,16384]{1,0:T(2,128)} %param.9) | copy-start | bytes 393220
  197.3 214.0 %copy-start.3 = (f32[2,16384]{1,0:T(2,128)S(1)}, f32[2,16384]{1,0:T(2,128)}, u32[]{:S(2)}) copy-start(f32[2,16384]{1,0:T(2,128)} %param.10) | copy-start | bytes 393220
  197.3 286.4 %all-gather.3.cloned.1.call-start = ((), (), s32[]{:S(2)}) async-start(), calls=%async_computation.1 | async-start | bytes 8454144 | tf_op jit(solution)/shard_map/all_gather | solution.py:51
  413.6 83.2 %copy-start = (f32[2,16384]{1,0:T(2,128)}, f32[2,16384]{1,0:T(2,128)S(1)}, u32[]{:S(2)}) copy-start(f32[2,16384]{1,0:T(2,128)S(1)} %get-tuple-element.8) | copy-start | bytes 393220
Sparse Core Ops, SparseCore 0:
  32.5 141.1 all-reduce.3
  197.5 213.7 all-reduce.5
  414.8 68.8 all-gather.2
where the time goes:
time: 504 us; the launch traced here: 503 us
  waiting for transfers between devices  424 us (84%)
  other arithmetic  38.1 us (8%)
  local copies, waits for them, and re-layouts  27.1 us (5%)
  between operations  13.8 us (3%)
    unnamed x4, waiting for transfers between devices  214 us
    pmax x1, waiting for transfers between devices, per_device(): lax.pmax(jnp.max(mags, axis=2).astype(jnp.bfloat16), 'dp')  141 us
    all_gather x1, waiting for transfers between devices, per_device(): weights = lax.all_gather(own_weights, 'dp', axis=0, tiled=True)  69.1 us
    unnamed x18, local copies, waits for them, and re-layouts  22.4 us
    floor x1, other arithmetic, per_device(): mant = jnp.floor(vals + 0.5).reshape(rows, width)  17.3 us
    unnamed x3, other arithmetic  12.6 us
  transfers between devices with their start and end apart: 3, of which 3 were waited for; matrix products, arithmetic and copies ran while one was open for 0% of the time, Pallas kernels for 0%

commit v1 on v0

v1 whole, which is shorter than its diff:
```python
import jax
import jax.numpy as jnp
from jax import lax
from jax.experimental import pallas as pl
from jax.experimental.pallas import tpu as pltpu
from jax.sharding import PartitionSpec as P

BLOCK = 128
MBITS = 7
STEP = 20
ROWS = 256
W = 16384
N_DP = 128
HALF = W // 2
NB = HALF // BLOCK
F32 = jnp.float32
BF16 = jnp.bfloat16

NEAR = {0: ((0, 1), (3, 2)), 1: ((1, 2), (0, 3))}
FAR = {0: ((0, 3), (1, 2)), 1: ((0, 1), (2, 3))}
PLACE = {0: (0, 2, 3, 1), 1: (0, 1, 2, 3)}


def device(x, z, y, core):
    return ((x * 4 + z) * 4 + y) * 2 + core


def groups(pairs):
    return [
        [device(x, z, y, core) for x in px for z in pz for y in py]
        for core in (0, 1)
        for px in pairs[core]
        for pz in pairs[core]
        for py in pairs[core]
    ]


NEAR_GROUPS = groups(NEAR)
FAR_GROUPS = groups(FAR)
SWAP = [(d, d ^ 1) for d in range(N_DP)]


def exchange(x, among):
    return lax.all_to_all(x, "dp", 0, 0, axis_index_groups=among)


def spread(x, among):
    return exchange(jnp.broadcast_to(x[None], (8, *x.shape)), among)


def max_kernel(core_ref, x_ref, amax_ref, send_ref):
    rows = x_ref.shape[1]
    lane = lax.broadcasted_iota(jnp.int32, (rows, 128), 1)
    acc = jnp.zeros((rows, 128), F32)
    for b in range(W // BLOCK):
        v = jnp.abs(x_ref[0, :, b * BLOCK : (b + 1) * BLOCK].astype(F32))
        acc = jnp.where(lane == b, jnp.max(v, axis=1, keepdims=True), acc)
    amax_ref[...] = acc.astype(BF16)
    start = pl.multiple_of((1 - core_ref[0]) * HALF, HALF)
    send_ref[...] = x_ref[0, :, pl.ds(start, HALF)]


def block_max(core, partials, rows=32):
    return pl.pallas_call(
        max_kernel,
        out_shape=(
            jax.ShapeDtypeStruct((ROWS, 128), BF16),
            jax.ShapeDtypeStruct((ROWS, HALF), BF16),
        ),
        grid_spec=pltpu.PrefetchScalarGridSpec(
            num_scalar_prefetch=1,
            grid=(ROWS // rows,),
            in_specs=[pl.BlockSpec((1, rows, W), lambda i, c: (0, i, 0))],
            out_specs=[
                pl.BlockSpec((rows, 128), lambda i, c: (i, 0)),
                pl.BlockSpec((rows, HALF), lambda i, c: (i, 0)),
            ],
        ),
        name="block_max",
    )(core, partials)


def scale_of(amax):
    scale = jnp.full(amax.shape, 2.0**-20, F32)
    for k in range(-20, 13):
        scale = jnp.where(amax >= 2.0**k, F32(2.0 ** (k + 1)), scale)
    return scale


def mult_of(amax):
    mult = jnp.full(amax.shape, 2.0 ** (MBITS + 20), F32)
    for k in range(-20, 13):
        mult = jnp.where(amax >= 2.0**k, F32(2.0 ** (MBITS - k - 1)), mult)
    return mult


def quant_kernel(core_ref, place_ref, own_ref, other_ref, amax_ref, out_ref):
    core = core_ref[0]
    mult = mult_of(jnp.max(amax_ref[...].astype(F32), axis=0))
    mult = jnp.where(core == 0, mult, pltpu.roll(mult, 64, 1))
    top = lax.broadcasted_iota(jnp.int32, (8, 128), 0) < 4
    for b in range(NB):
        cols = slice(b * BLOCK, (b + 1) * BLOCK)
        m = jnp.broadcast_to(mult[:, b : b + 1], (16, BLOCK))
        v = jnp.floor(own_ref[0, :, cols].astype(F32) * m + 0.5)
        v = v + jnp.floor(other_ref[:, cols].astype(F32) * m + 0.5)
        t0, t1 = v[:8], v[8:]
        a = jnp.where(core == 1, t0, jnp.where(top, t0, t1))
        c = jnp.where(core == 1, t1, pltpu.roll(jnp.where(top, t1, t0), 4, 0))
        out_ref[0, 0, 0, 0, 0, :, cols] = a.astype(BF16)
        out_ref[0, 0, 1, 0, 0, :, cols] = c.astype(BF16)


def placed(x, z, place):
    px, pz = place[x], place[z]
    return (px >> 1, pz >> 1, 0, px & 1, pz & 1, 0, 0)


def quantise(core, place, partials, other, amax):
    out = pl.pallas_call(
        quant_kernel,
        out_shape=jax.ShapeDtypeStruct((2, 2, 2, 2, 2, 8, HALF), BF16),
        grid_spec=pltpu.PrefetchScalarGridSpec(
            num_scalar_prefetch=2,
            grid=(4, 4),
            in_specs=[
                pl.BlockSpec((1, 16, HALF), lambda x, z, c, p: (0, x * 4 + z, c[0])),
                pl.BlockSpec((16, HALF), lambda x, z, c, p: (x * 4 + z, 0)),
                pl.BlockSpec((8, 16, 128), lambda x, z, c, p: (0, x * 4 + z, 0)),
            ],
            out_specs=pl.BlockSpec(
                (1, 1, 2, 1, 1, 8, HALF), lambda x, z, c, p: placed(x, z, p)
            ),
        ),
        name="quantise",
    )(core, place, partials, other, amax)
    return out.reshape(8, 32, HALF)


def rows_kernel(core_ref, place_ref, w_ref, *refs):
    out_ref = refs[-1]
    core = core_ref[0]
    top = lax.broadcasted_iota(jnp.int32, (8, 128), 0) < 4
    for b in range(NB):
        cols = slice(b * BLOCK, (b + 1) * BLOCK)
        a = w_ref[0, 0, 0, 0, 0, :, cols].astype(F32)
        c = w_ref[0, 0, 1, 0, 0, :, cols].astype(F32)
        r = pltpu.roll(c, 4, 0)
        out_ref[:8, cols] = jnp.where(core == 1, a, jnp.where(top, a, r)).astype(BF16)
        out_ref[8:, cols] = jnp.where(core == 1, c, jnp.where(top, r, a)).astype(BF16)


def place_rows(core, place, w, before=None):
    w = w.reshape(2, 2, 2, 2, 2, 8, HALF)
    more = () if before is None else (before,)
    return pl.pallas_call(
        rows_kernel,
        out_shape=jax.ShapeDtypeStruct((ROWS, W), BF16),
        grid_spec=pltpu.PrefetchScalarGridSpec(
            num_scalar_prefetch=2,
            grid=(4, 4),
            in_specs=[
                pl.BlockSpec((1, 1, 2, 1, 1, 8, HALF), lambda x, z, c, p: placed(x, z, p)),
                *(pl.BlockSpec(memory_space=pl.ANY) for _ in more),
            ],
            out_specs=pl.BlockSpec((16, HALF), lambda x, z, c, p: (x * 4 + z, c[0])),
        ),
        input_output_aliases={3: 0} if more else {},
        name="place_rows",
    )(core, place, w, *more)


def per_device(partials, master, moment_one, moment_two):
    d = lax.axis_index("dp")
    core, chip = d % 2, d // 2
    places = jnp.asarray([PLACE[0], PLACE[1]], jnp.int32)
    mine = (core.reshape(1), places[core])
    theirs = ((1 - core).reshape(1), places[1 - core])

    amax, send = block_max(mine[0], partials)
    other = lax.ppermute(send, "dp", SWAP)
    amax = jnp.maximum(amax, lax.ppermute(amax, "dp", SWAP))
    amax = jnp.max(spread(amax, FAR_GROUPS), axis=0)
    amax = spread(amax, NEAR_GROUPS)

    state = jnp.stack([master, moment_one, moment_two])
    state_own = lax.dynamic_slice_in_dim(state, core * HALF, HALF, 2)
    state_other = lax.ppermute(
        lax.dynamic_slice_in_dim(state, (1 - core) * HALF, HALF, 2), "dp", SWAP
    )
    first = core == 0
    state = jnp.where(
        first,
        jnp.concatenate([state_own, state_other], axis=1),
        jnp.concatenate([state_other, state_own], axis=1),
    )
    master, moment_one, moment_two = state

    mant = quantise(*mine, partials, other, amax)
    mant = jnp.sum(exchange(mant, NEAR_GROUPS).astype(F32), axis=0).reshape(8, 4, HALF)
    total = jnp.sum(exchange(mant, FAR_GROUPS), axis=0)

    own_amax = lax.dynamic_slice(amax, (0, chip * 4, core * NB), (8, 4, NB))
    scale = scale_of(jnp.max(own_amax.astype(F32), axis=0))
    factor = scale / (2.0**MBITS * N_DP)
    reduced_grad = (total.reshape(4, NB, BLOCK) * factor[:, :, None]).reshape(4, HALF)
    moment_one_new = 0.9 * moment_one + 0.1 * reduced_grad
    moment_two_new = 0.95 * moment_two + 0.05 * reduced_grad * reduced_grad
    update = (moment_one_new / (1.0 - 0.9**STEP)) / (
        jnp.sqrt(moment_two_new / (1.0 - 0.95**STEP)) + 1e-08
    )
    master_new = master - 0.001 * (update + 0.1 * master)
    blocks = master_new.reshape(4, NB, BLOCK)
    wscale = jnp.max(jnp.abs(blocks), axis=2) + 1e-06
    wmant = (blocks / wscale[:, :, None]).astype(BF16)
    weights = (wmant.astype(F32) * wscale[:, :, None]).reshape(4, HALF).astype(BF16)

    out = jnp.stack([master_new, moment_one_new, moment_two_new, reduced_grad])
    out_own = jnp.where(first, out[:, :2], out[:, 2:])
    out_other = lax.ppermute(jnp.where(first, out[:, 2:], out[:, :2]), "dp", SWAP)
    out = jnp.where(
        first,
        jnp.concatenate([out_own, out_other], axis=2),
        jnp.concatenate([out_other, out_own], axis=2),
    )

    weights = spread(weights, FAR_GROUPS).reshape(32, HALF)
    weights = spread(weights, NEAR_GROUPS)
    weights_other = lax.ppermute(weights, "dp", SWAP)
    full = place_rows(*mine, weights)
    full = place_rows(*theirs, weights_other, full)
    return (out[0], out[1], out[2], out[3], full)


def solution(mesh):
    in_specs = (P("dp", None, None), P("dp", None), P("dp", None), P("dp", None))
    out_specs = (P("dp", None), P("dp", None), P("dp", None), P("dp", None), P())
    return jax.shard_map(
        per_device, mesh=mesh, in_specs=in_specs, out_specs=out_specs, check_vma=False
    )
```

time: 504 us -> 198 us (0.39)
  waiting for transfers between devices: 424 us -> 65.2 us
  starting transfers between devices: 0.12 us -> 46.5 us
  Pallas kernels: 0 us -> 46.3 us
  other arithmetic: 38.1 us -> 6.66 us
  blocking collectives: 0 us -> 21.2 us
  local copies, waits for them, and re-layouts: 27.1 us -> 7.5 us
  between operations: 13.8 us -> 0.87 us
    unnamed x4 -> x0, waiting for transfers between devices: 214 us -> none
    pmax x1 -> x0, waiting for transfers between devices: 141 us -> none  [per_device(): lax.pmax(jnp.max(mags, axis=2).astype(jnp.bfloat16), 'dp')]
    all_gather x1 -> x0, waiting for transfers between devices: 69.1 us -> none  [per_device(): weights = lax.all_gather(own_weights, 'dp', axis=0, tiled=True)]
    all_to_all x0 -> x4, waiting for transfers between devices: none -> 59.1 us  [exchange(): return lax.all_to_all(x, 'dp', 0, 0, axis_index_groups=among)]
    pallas_call x0 -> x4, Pallas kernels: none -> 46.3 us  [the longest x2 22.4 us: place_rows(): pl.pallas_call(rows_kernel, out_shape=jax.ShapeDtypeStruct((ROWS, W), BF1...]
    ppermute x0 -> x5, starting transfers between devices: none -> 25.8 us  [the longest x1 10.9 us: per_device(): lax.ppermute(jnp.where(first, out[:, 2:], out[:, :2]), 'dp', SWAP)]
    unnamed x18 -> x10, local copies, waits for them, and re-layouts: 22.4 us -> 0.82 us
    all_to_all x0 -> x2, blocking collectives: none -> 21.2 us  [exchange(): return lax.all_to_all(x, 'dp', 0, 0, axis_index_groups=among)]
  transfers between devices with their start and end apart: 3 -> 9, of which waited for: 3 -> 5; matrix products, arithmetic and copies ran while one was open for 0% -> 5% of each run, Pallas kernels for 0% -> 6%
where the time goes in v1:
time: 198 us; the launch traced here: 194 us
  waiting for transfers between devices  65.2 us (33%)
  starting transfers between devices  46.5 us (23%)
  Pallas kernels  46.3 us (23%)
  blocking collectives  21.2 us (11%)
  local copies, waits for them, and re-layouts  7.5 us (4%)
  other arithmetic  6.66 us (3%)
    all_to_all x4, waiting for transfers between devices, exchange(): return lax.all_to_all(x, 'dp', 0, 0, axis_index_groups=among)  59.1 us
    pallas_call x2, Pallas kernels, place_rows(): pl.pallas_call(rows_kernel, out_shape=jax.ShapeDtypeStruct((ROWS, W), BF1...  22.4 us
    all_to_all x2, blocking collectives, exchange(): return lax.all_to_all(x, 'dp', 0, 0, axis_index_groups=among)  21.2 us
    all_to_all x4, starting transfers between devices, exchange(): return lax.all_to_all(x, 'dp', 0, 0, axis_index_groups=among)  20.8 us
    pallas_call x1, Pallas kernels, quantise(): pl.pallas_call(quant_kernel, out_shape=jax.ShapeDtypeStruct((2, 2, 2, 2,...  14.4 us
    ppermute x1, starting transfers between devices, per_device(): lax.ppermute(jnp.where(first, out[:, 2:], out[:, :2]), 'dp', SWAP)  10.9 us
    pallas_call x1, Pallas kernels, block_max(): pl.pallas_call(max_kernel, out_shape=(jax.ShapeDtypeStruct((ROWS, 128), B...  9.46 us
    ppermute x1, starting transfers between devices, per_device(): weights_other = lax.ppermute(weights, 'dp', SWAP)  9.43 us
  transfers between devices with their start and end apart: 9, of which 5 were waited for; matrix products, arithmetic and copies ran while one was open for 5% of the time, Pallas kernels for 6%

profile of v1, /device:TPU:1, one launch (start us, length us, event | category | flops | bytes accessed | tf_op | source)
XLA Modules:
  0.0 194.4 jit_solution(14309342060422604323)
XLA Ops:
  0.7 9.5 %block_max.1 = (bf16[256,128]{1,0:T(8,128)(2,1)}, bf16[256,8192]{1,0:T(8,128)(2,1)}) custom-call(s32[1]{0:T(128)} %bitcast.3.core_ref, bf16[1,256,16384]{2,1,0:T(8,128)(2,1)} %own_ref.1), custom_call_target="tpu_custom_call" | custom-call | tf_op jit(solution)/shard_map/block_max/pallas_call | solution.py:64
  10.1 1.4 collective-permute-start.1
  11.5 6.1 %collective-permute-done.2 = bf16[256,128]{1,0:T(8,128)(2,1)S(1)} collective-permute-done((bf16[256,128]{1,0:T(8,128)(2,1)}, bf16[256,128]{1,0:T(8,128)(2,1)S(1)}, u32[]{:S(2)}, u32[]{:S(2)}) %collective-permute-start.2) | collective-permute-done | bytes 65568 | tf_op jit(solution)/shard_map/ppermute | solution.py:182
  17.7 0.9 max.3
  18.6 11.6 %all_to_all.30 = bf16[8,256,128]{2,1,0:T(8,128)(2,1)S(1)} all-to-all(bf16[8,256,128]{2,1,0:T(8,128)(2,1)S(1)} %broadcast_in_dim.66), channel_id=1, replica_groups={{0,6,24,30,96,102,120,126},{2,4,26,28,98,100,122,124},{8,14,16,22,104,1..., dimensions={0} | all-to-all | bytes 1048576 | tf_op jit(solution)/shard_map/all_to_all | solution.py:44
  30.3 0.9 broadcast_in_dim.67
  31.2 7.0 %all-to-all-start.1 = ((bf16[8,256,128]{2,1,0:T(8,128)(2,1)}), bf16[8,256,128]{2,1,0:T(8,128)(2,1)S(1)}, u32[]{:S(2)}, u32[]{:S(2)}) async-start(bf16[8,256,128]{2,1,0:T(8,128)(2,1)} %broadcast_in_dim.67), calls=%async_computation.1 | async-start | bytes 1048576 | tf_op jit(solution)/shard_map/all_to_all | solution.py:44
  38.2 0.6 fusion.14
  38.8 9.6 %all-to-all-done.1.amax_ref = bf16[8,256,128]{2,1,0:T(8,128)(2,1)S(1)} async-done(((bf16[8,256,128]{2,1,0:T(8,128)(2,1)}), bf16[8,256,128]{2,1,0:T(8,128)(2,1)S(1)}, u32[]{:S(2)}, u32[]{:S(2)}) %all-to-all-start.1) | async-done | bytes 524320 | tf_op jit(solution)/shard_map/all_to_all | solution.py:44
  48.4 0.8 copy-done
  49.2 14.4 %quantise.1 = bf16[2,2,2,2,2,8,8192]{6,5,4,3,2,1,0:T(8,128)(2,1)} custom-call(s32[1]{0:T(128)} %bitcast.3.core_ref, s32[4]{0:T(128)} %get-tuple-element.26.place_ref, bf16[1,256,16384]{2,1,0:T(8,128)(2,1)} %own_ref.1, bf16[256,8192]{1,0:T(8,128)(2,1)} %collective-permute-done.1.other_ref, bf16[8,256,128]{2,1,0:T(8,128)(2,1)} %copy-done), custom_call_target="tpu_custom_call" | custom-call | tf_op jit(solution)/shard_map/quantise/pallas_call | solution.py:120
  63.6 4.7 %all-to-all-start.2 = ((bf16[8,32,8192]{2,1,0:T(8,128)(2,1)}), bf16[8,32,8192]{2,1,0:T(8,128)(2,1)}, u32[]{:S(2)}, u32[]{:S(2)}) async-start(bf16[8,32,8192]{2,1,0:T(8,128)(2,1)} %bitcast.62), calls=%async_computation.2 | async-start | bytes 8388608 | tf_op jit(solution)/shard_map/all_to_all | solution.py:44
  68.6 4.0 %collective-permute-start = (f32[3,2,8192]{2,1,0:T(2,128)S(1)}, f32[3,2,8192]{2,1,0:T(2,128)S(1)}, u32[]{:S(2)}, u32[]{:S(2)}) collective-permute-start(f32[3,2,8192]{2,1,0:T(2,128)S(1)} %get-tuple-element.24), channel_id=1, source_target_pairs={{0,1},{1,0},{2,3},{3,2},{4,5},{5,4},{6,7},{7,6},{8,9},{9,8},{10,11... | collective-permute-start | bytes 589832 | tf_op jit(solution)/shard_map/ppermute | solution.py:188
  72.6 24.2 %all-to-all-done.2 = bf16[8,32,8192]{2,1,0:T(8,128)(2,1)} async-done(((bf16[8,32,8192]{2,1,0:T(8,128)(2,1)}), bf16[8,32,8192]{2,1,0:T(8,128)(2,1)}, u32[]{:S(2)}, u32[]{:S(2)}) %all-to-all-start.2) | async-done | bytes 4194336 | tf_op jit(solution)/shard_map/all_to_all | solution.py:44
  96.8 2.9 %convert_reduce_fusion = f32[32,8192]{1,0:T(8,128)S(1)} fusion(bf16[8,32,8192]{2,1,0:T(8,128)(2,1)} %all-to-all-done.2), kind=kLoop, calls=%fused_computation | loop fusion | flops 3932160 | bytes 5242880 | tf_op jit(solution)/shard_map/reduce_sum | solution.py:200
  99.7 1.3 reshape.180
  101.0 3.6 %all-to-all-start.3 = ((f32[8,4,8192]{2,1,0:T(4,128)}), f32[8,4,8192]{2,1,0:T(4,128)S(1)}, u32[]{:S(2)}, u32[]{:S(2)}) async-start(f32[8,4,8192]{2,1,0:T(4,128)} %reshape.180), calls=%async_computation.3 | async-start | bytes 2097152 | tf_op jit(solution)/shard_map/all_to_all | solution.py:44
  104.5 0.3 maximum_select_fusion.1
  104.9 0.8 dynamic-slice_reduce_fusion
  105.9 8.0 %all-to-all-done.3 = f32[8,4,8192]{2,1,0:T(4,128)S(1)} async-done(((f32[8,4,8192]{2,1,0:T(4,128)}), f32[8,4,8192]{2,1,0:T(4,128)S(1)}, u32[]{:S(2)}, u32[]{:S(2)}) %all-to-all-start.3) | async-done | bytes 1048608 | tf_op jit(solution)/shard_map/all_to_all | solution.py:44
  114.1 0.3 fusion.9
  114.5 0.3 fusion.12
  115.0 9.6 %all_to_all.31 = bf16[8,4,8192]{2,1,0:T(4,128)(2,1)S(1)} all-to-all(bf16[8,4,8192]{2,1,0:T(4,128)(2,1)S(1)} %broadcast_in_dim.70), channel_id=1, replica_groups={{0,6,24,30,96,102,120,126},{2,4,26,28,98,100,122,124},{8,14,16,22,104,1..., dimensions={0} | all-to-all | bytes 1048576 | tf_op jit(solution)/shard_map/all_to_all | solution.py:44
  124.7 2.5 %broadcast_in_dim.72 = bf16[8,32,8192]{2,1,0:T(8,128)(2,1)} broadcast(bf16[32,8192]{1,0:T(8,128)(2,1)S(1)} %broadcast_in_dim.71), dimensions={1,2} | broadcast | bytes 4718592 | tf_op jit(solution)/shard_map/broadcast_in_dim | solution.py:48
  127.2 5.5 %all-to-all-start.5 = ((bf16[8,32,8192]{2,1,0:T(8,128)(2,1)}), bf16[8,32,8192]{2,1,0:T(8,128)(2,1)}, u32[]{:S(2)}, u32[]{:S(2)}) async-start(bf16[8,32,8192]{2,1,0:T(8,128)(2,1)} %broadcast_in_dim.72), calls=%async_computation.5 | async-start | bytes 8388608 | tf_op jit(solution)/shard_map/all_to_all | solution.py:44
  133.0 10.9 %collective-permute-start.3 = (f32[4,2,8192]{2,1,0:T(2,128)S(1)}, f32[4,2,8192]{2,1,0:T(2,128)S(1)}, u32[]{:S(2)}, u32[]{:S(2)}) collective-permute-start(f32[4,2,8192]{2,1,0:T(2,128)S(1)} %get-tuple-element.19), channel_id=1, source_target_pairs={{0,1},{1,0},{2,3},{3,2},{4,5},{5,4},{6,7},{7,6},{8,9},{9,8},{10,11... | collective-permute-start | bytes 786440 | tf_op jit(solution)/shard_map/ppermute | solution.py:220
  143.9 17.4 %all-to-all-done.5 = bf16[8,32,8192]{2,1,0:T(8,128)(2,1)} async-done(((bf16[8,32,8192]{2,1,0:T(8,128)(2,1)}), bf16[8,32,8192]{2,1,0:T(8,128)(2,1)}, u32[]{:S(2)}, u32[]{:S(2)}) %all-to-all-start.5) | async-done | bytes 4194336 | tf_op jit(solution)/shard_map/all_to_all | solution.py:44
  161.3 9.4 %collective-permute-start.4 = (bf16[8,32,8192]{2,1,0:T(8,128)(2,1)}, bf16[8,32,8192]{2,1,0:T(8,128)(2,1)}, u32[]{:S(2)}, u32[]{:S(2)}) collective-permute-start(bf16[8,32,8192]{2,1,0:T(8,128)(2,1)} %all-to-all-done.5), channel_id=1, source_target_pairs={{0,1},{1,0},{2,3},{3,2},{4,5},{5,4},{6,7},{7,6},{8,9},{9,8},{10,11... | collective-permute-start | bytes 12582920 | tf_op jit(solution)/shard_map/ppermute | solution.py:229
  170.8 0.4 maximum_select_fusion
  171.2 0.8 slice_bitcast_fusion
  172.0 11.2 %place_rows.2.refs_0_ = bf16[256,16384]{1,0:T(8,128)(2,1)} custom-call(s32[1]{0:T(128)} %bitcast.3.core_ref, s32[4]{0:T(128)} %get-tuple-element.26.place_ref, bf16[2,2,2,2,2,8,8192]{6,5,4,3,2,1,0:T(8,128)(2,1)} %bitcast.15.w_ref), custom_call_target="tpu_custom_call" | custom-call | tf_op jit(solution)/shard_map/place_rows/pallas_call | solution.py:156
  183.2 11.2 %place_rows.3 = bf16[256,16384]{1,0:T(8,128)(2,1)} custom-call(s32[1]{0:T(128)} %bitcast.11.core_ref, s32[4]{0:T(128)} %get-tuple-element.25.place_ref, bf16[2,2,2,2,2,8,8192]{6,5,4,3,2,1,0:T(8,128)(2,1)} %bitcast.14.w_ref, bf16[256,16384]{1,0:T(8,128)(2,1)} %place_rows.2.refs_0_), custom_call_target="tpu_custom_call", output_to_operand_aliasing={{}: (3, {})} | custom-call | tf_op jit(solution)/shard_map/place_rows/pallas_call | solution.py:156
  (30 shorter events, 1.5 us)
Async XLA Ops:
  0.6 37.6 %copy-start.4 = (s32[2,4]{1,0:T(2,128)S(1)}, s32[2,4]{1,0:T(2,128)}, u32[]{:S(2)}) copy-start(s32[2,4]{1,0:T(2,128)} %constant.44.clone) | copy-start | bytes 100
  10.1 38.2 %collective-permute-start.1 = (bf16[256,8192]{1,0:T(8,128)(2,1)}, bf16[256,8192]{1,0:T(8,128)(2,1)}, u32[]{:S(2)}, u32[]{:S(2)}) collective-permute-start(bf16[256,8192]{1,0:T(8,128)(2,1)} %get-tuple-element.7), channel_id=1, source_target_pairs={{0,1},{1,0},{2,3},{3,2},{4,5},{5,4},{6,7},{7,6},{8,9},{9,8},{10,11... | collective-permute-start | bytes 12582920 | tf_op jit(solution)/shard_map/ppermute | solution.py:181
  11.5 6.1 %collective-permute-start.2 = (bf16[256,128]{1,0:T(8,128)(2,1)}, bf16[256,128]{1,0:T(8,128)(2,1)S(1)}, u32[]{:S(2)}, u32[]{:S(2)}) collective-permute-start(bf16[256,128]{1,0:T(8,128)(2,1)} %get-tuple-element.8), channel_id=1, source_target_pairs={{0,1},{1,0},{2,3},{3,2},{4,5},{5,4},{6,7},{7,6},{8,9},{9,8},{10,11... | collective-permute-start | bytes 196616 | tf_op jit(solution)/shard_map/ppermute | solution.py:182
  31.2 17.2 %all-to-all-start.1 = ((bf16[8,256,128]{2,1,0:T(8,128)(2,1)}), bf16[8,256,128]{2,1,0:T(8,128)(2,1)S(1)}, u32[]{:S(2)}, u32[]{:S(2)}) async-start(bf16[8,256,128]{2,1,0:T(8,128)(2,1)} %broadcast_in_dim.67), calls=%async_computation.1 | async-start | bytes 1048576 | tf_op jit(solution)/shard_map/all_to_all | solution.py:44
  48.4 0.8 copy-start
  63.6 4.7 %copy-start.1 = (f32[2,16384]{1,0:T(2,128)S(1)}, f32[2,16384]{1,0:T(2,128)}, u32[]{:S(2)}) copy-start(f32[2,16384]{1,0:T(2,128)} %param.8) | copy-start | bytes 393220
  63.6 4.7 %copy-start.2 = (f32[2,16384]{1,0:T(2,128)S(1)}, f32[2,16384]{1,0:T(2,128)}, u32[]{:S(2)}) copy-start(f32[2,16384]{1,0:T(2,128)} %param.7) | copy-start | bytes 393220
  63.6 4.7 %copy-start.3 = (f32[2,16384]{1,0:T(2,128)S(1)}, f32[2,16384]{1,0:T(2,128)}, u32[]{:S(2)}) copy-start(f32[2,16384]{1,0:T(2,128)} %param.6) | copy-start | bytes 393220
  63.6 33.2 %all-to-all-start.2 = ((bf16[8,32,8192]{2,1,0:T(8,128)(2,1)}), bf16[8,32,8192]{2,1,0:T(8,128)(2,1)}, u32[]{:S(2)}, u32[]{:S(2)}) async-start(bf16[8,32,8192]{2,1,0:T(8,128)(2,1)} %bitcast.62), calls=%async_computation.2 | async-start | bytes 8388608 | tf_op jit(solution)/shard_map/all_to_all | solution.py:44
  68.6 36.0 %collective-permute-start = (f32[3,2,8192]{2,1,0:T(2,128)S(1)}, f32[3,2,8192]{2,1,0:T(2,128)S(1)}, u32[]{:S(2)}, u32[]{:S(2)}) collective-permute-start(f32[3,2,8192]{2,1,0:T(2,128)S(1)} %get-tuple-element.24), channel_id=1, source_target_pairs={{0,1},{1,0},{2,3},{3,2},{4,5},{5,4},{6,7},{7,6},{8,9},{9,8},{10,11... | collective-permute-start | bytes 589832 | tf_op jit(solution)/shard_map/ppermute | solution.py:188
  101.0 12.9 %all-to-all-start.3 = ((f32[8,4,8192]{2,1,0:T(4,128)}), f32[8,4,8192]{2,1,0:T(4,128)S(1)}, u32[]{:S(2)}, u32[]{:S(2)}) async-start(f32[8,4,8192]{2,1,0:T(4,128)} %reshape.180), calls=%async_computation.3 | async-start | bytes 2097152 | tf_op jit(solution)/shard_map/all_to_all | solution.py:44
  127.2 34.1 %all-to-all-start.5 = ((bf16[8,32,8192]{2,1,0:T(8,128)(2,1)}), bf16[8,32,8192]{2,1,0:T(8,128)(2,1)}, u32[]{:S(2)}, u32[]{:S(2)}) async-start(bf16[8,32,8192]{2,1,0:T(8,128)(2,1)} %broadcast_in_dim.72), calls=%async_computation.5 | async-start | bytes 8388608 | tf_op jit(solution)/shard_map/all_to_all | solution.py:44
  133.0 37.7 %collective-permute-start.3 = (f32[4,2,8192]{2,1,0:T(2,128)S(1)}, f32[4,2,8192]{2,1,0:T(2,128)S(1)}, u32[]{:S(2)}, u32[]{:S(2)}) collective-permute-start(f32[4,2,8192]{2,1,0:T(2,128)S(1)} %get-tuple-element.19), channel_id=1, source_target_pairs={{0,1},{1,0},{2,3},{3,2},{4,5},{5,4},{6,7},{7,6},{8,9},{9,8},{10,11... | collective-permute-start | bytes 786440 | tf_op jit(solution)/shard_map/ppermute | solution.py:220
  161.3 21.9 %collective-permute-start.4 = (bf16[8,32,8192]{2,1,0:T(8,128)(2,1)}, bf16[8,32,8192]{2,1,0:T(8,128)(2,1)}, u32[]{:S(2)}, u32[]{:S(2)}) collective-permute-start(bf16[8,32,8192]{2,1,0:T(8,128)(2,1)} %all-to-all-done.5), channel_id=1, source_target_pairs={{0,1},{1,0},{2,3},{3,2},{4,5},{5,4},{6,7},{7,6},{8,9},{9,8},{10,11... | collective-permute-start | bytes 12582920 | tf_op jit(solution)/shard_map/ppermute | solution.py:229

commit v2 on v1

v2 whole, which is shorter than its diff:
```python
import jax
import jax.numpy as jnp
from jax import lax
from jax.experimental import pallas as pl
from jax.experimental.pallas import tpu as pltpu
from jax.sharding import PartitionSpec as P

BLOCK = 128
MBITS = 7
STEP = 20
ROWS = 256
W = 16384
N_DP = 128
HALF = W // 2
NB = HALF // BLOCK
F32 = jnp.float32
BF16 = jnp.bfloat16

F16 = jnp.float16

NEAR = {0: ((0, 1), (3, 2)), 1: ((1, 2), (0, 3))}
FAR = {0: ((0, 3), (1, 2)), 1: ((0, 1), (2, 3))}
OWNER = {0: (0, 2, 3, 1), 1: (0, 1, 2, 3)}
ALL = [(x, z, y) for x in range(4) for z in range(4) for y in range(4)]


def device(x, z, y, core):
    return ((x * 4 + z) * 4 + y) * 2 + core


def groups(pairs):
    return [
        [device(x, z, y, core) for x in px for z in pz for y in py]
        for core in (0, 1)
        for px in pairs[core]
        for pz in pairs[core]
        for py in pairs[core]
    ]


def owner(core, at):
    return tuple(OWNER[core][i] for i in at)


NEAR_GROUPS = groups(NEAR)
FAR_GROUPS = groups(FAR)
SWAP = [(d, d ^ 1) for d in range(N_DP)]
TO_SAME = [(device(*owner(c, at), c), device(*at, c)) for c in (0, 1) for at in ALL]
TO_OTHER = [(device(*owner(c, at), 1 - c), device(*at, c)) for c in (0, 1) for at in ALL]
FROM_SAME = [(b, a) for a, b in TO_SAME]
FROM_OTHER = [(b, a) for a, b in TO_OTHER]


def exchange(x, among):
    return lax.all_to_all(x, "dp", 0, 0, axis_index_groups=among)


def spread(x, among):
    return exchange(jnp.broadcast_to(x[None], (8, *x.shape)), among)


def max_kernel(core_ref, x_ref, amax_ref, other_ref, send_ref, buf, own_max, other_max, in_sem, out_sem):
    core = core_ref[0]
    rows = ROWS // in_sem.shape[0]
    theirs = pl.ds(pl.multiple_of((1 - core) * HALF, HALF), HALF)
    chunks = [pl.ds(i * rows, rows) for i in range(ROWS // rows)]
    loads = [
        pltpu.make_async_copy(x_ref.at[0, at], buf.at[at], in_sem.at[i])
        for i, at in enumerate(chunks)
    ]
    stores = [
        pltpu.make_async_copy(buf.at[at, theirs], send_ref.at[at], out_sem.at[i])
        for i, at in enumerate(chunks)
    ]
    for load in loads:
        load.start()
    lane = lax.broadcasted_iota(jnp.int32, (rows, 128), 1)
    low = lane < NB
    for i, at in enumerate(chunks):
        loads[i].wait()
        stores[i].start()
        acc = jnp.zeros((rows, 128), F32)
        for b in range(W // BLOCK):
            v = jnp.abs(buf[at, b * BLOCK : (b + 1) * BLOCK].astype(F32))
            acc = jnp.where(lane == b, jnp.max(v, axis=1, keepdims=True), acc)
        rolled = pltpu.roll(acc, NB, 1)
        mine, rest = jnp.where(core == 0, acc, rolled), jnp.where(core == 0, rolled, acc)
        to = pl.ds(i * rows % 128, rows)
        if i * rows < 128:
            own_max[to, :], other_max[to, :] = mine, rest
        else:
            own_max[to, :] = jnp.where(low, own_max[to, :], rest)
            other_max[to, :] = jnp.where(low, other_max[to, :], mine)
    amax_ref[...] = own_max[...].astype(BF16)
    other_ref[...] = other_max[...].astype(BF16)
    for store in stores:
        store.wait()


SMEM = pl.BlockSpec(memory_space=pltpu.SMEM)
VMEM = pl.BlockSpec(memory_space=pltpu.VMEM)
HBM = pl.BlockSpec(memory_space=pltpu.HBM)
PARAMS = pltpu.CompilerParams(vmem_limit_bytes=60 << 20)


def block_max(core, partials, chunks=4):
    return pl.pallas_call(
        max_kernel,
        out_shape=(
            jax.ShapeDtypeStruct((128, 128), BF16),
            jax.ShapeDtypeStruct((128, 128), BF16),
            jax.ShapeDtypeStruct((ROWS, HALF), BF16),
        ),
        in_specs=[SMEM, HBM],
        out_specs=[VMEM, VMEM, HBM],
        scratch_shapes=[
            pltpu.VMEM((ROWS, W), BF16),
            pltpu.VMEM((128, 128), F32),
            pltpu.VMEM((128, 128), F32),
            pltpu.SemaphoreType.DMA((chunks,)),
            pltpu.SemaphoreType.DMA((chunks,)),
        ],
        compiler_params=PARAMS,
        name="block_max",
    )(core, partials)


def scale_of(amax):
    scale = jnp.full(amax.shape, 2.0**-20, F32)
    for k in range(-20, 13):
        scale = jnp.where(amax >= 2.0**k, F32(2.0 ** (k + 1)), scale)
    return scale


def mult_of(amax):
    mult = jnp.full(amax.shape, 2.0 ** (MBITS + 20), F32)
    for k in range(-20, 13):
        mult = jnp.where(amax >= 2.0**k, F32(2.0 ** (MBITS - k - 1)), mult)
    return mult


def quant_kernel(core_ref, x_ref, other_ref, amax_ref, out_ref, own, other, mant, own_sem, other_sem, out_sem):
    rows = ROWS // own_sem.shape[0]
    mine = pl.ds(pl.multiple_of(core_ref[0] * HALF, HALF), HALF)
    loads = []
    for i in range(ROWS // rows):
        at = pl.ds(i * rows, rows)
        loads.append(
            (
                pltpu.make_async_copy(x_ref.at[0, at, mine], own.at[at], own_sem.at[i]),
                pltpu.make_async_copy(other_ref.at[at], other.at[at], other_sem.at[i]),
            )
        )
        for load in loads[i]:
            load.start()
    stores = []
    for i in range(ROWS // rows):
        at = pl.ds(i * rows, rows)
        low = i * rows % 128
        mult = mult_of(jnp.max(amax_ref[:, low : low + rows, :].astype(F32), axis=0))
        for load in loads[i]:
            load.wait()
        for b in range(NB):
            cols = slice(b * BLOCK, (b + 1) * BLOCK)
            lane = b + (NB if i * rows >= 128 else 0)
            m = jnp.broadcast_to(mult[:, lane : lane + 1], (rows, BLOCK))
            v = jnp.floor(own[at, cols].astype(F32) * m + 0.5)
            v = v + jnp.floor(other[at, cols].astype(F32) * m + 0.5)
            mant[at, cols] = v.astype(BF16)
        for t in range(i * rows // 8, (i + 1) * rows // 8):
            x, z, y = t // 8, t // 2 % 4, t % 2
            stores.append(
                pltpu.make_async_copy(
                    mant.at[pl.ds(t * 8, 8)],
                    out_ref.at[x >> 1, z >> 1, y, x & 1, z & 1],
                    out_sem.at[t],
                )
            )
            stores[t].start()
    for store in stores:
        store.wait()


def quantise(core, partials, other, amax, chunks=8):
    out = pl.pallas_call(
        quant_kernel,
        out_shape=jax.ShapeDtypeStruct((2, 2, 2, 2, 2, 8, HALF), BF16),
        in_specs=[SMEM, HBM, HBM, VMEM],
        out_specs=HBM,
        scratch_shapes=[
            *[pltpu.VMEM((ROWS, HALF), BF16)] * 3,
            pltpu.SemaphoreType.DMA((chunks,)),
            pltpu.SemaphoreType.DMA((chunks,)),
            pltpu.SemaphoreType.DMA((ROWS // 8,)),
        ],
        compiler_params=PARAMS,
        name="quantise",
    )(core, partials, other, amax)
    return out.reshape(8, 32, HALF)


def rows_kernel(half_ref, w_ref, *refs):
    out_ref, buf, in_sem, out_sem = refs[-4:]
    half = pl.ds(pl.multiple_of(half_ref[0] * HALF, HALF), HALF)
    loads, stores = [], []
    for t in range(ROWS // 8):
        x, z, y = t // 8, t // 2 % 4, t % 2
        source = w_ref.at[x >> 1, z >> 1, y, x & 1, z & 1]
        loads.append(pltpu.make_async_copy(source, buf.at[t], in_sem.at[t]))
        target = out_ref.at[pl.ds(t * 8, 8), half]
        stores.append(pltpu.make_async_copy(buf.at[t], target, out_sem.at[t]))
    for load in loads:
        load.start()
    for load, store in zip(loads, stores):
        load.wait()
        store.start()
    for store in stores:
        store.wait()


def place_rows(half, w, before=None):
    more = () if before is None else (before,)
    return pl.pallas_call(
        rows_kernel,
        out_shape=jax.ShapeDtypeStruct((ROWS, W), BF16),
        in_specs=[SMEM, HBM, *(HBM for _ in more)],
        out_specs=HBM,
        scratch_shapes=[
            pltpu.VMEM((ROWS // 8, 8, HALF), BF16),
            pltpu.SemaphoreType.DMA((ROWS // 8,)),
            pltpu.SemaphoreType.DMA((ROWS // 8,)),
        ],
        input_output_aliases={2: 0} if more else {},
        compiler_params=PARAMS,
        name="place_rows",
    )(half, w.reshape(2, 2, 2, 2, 2, 8, HALF), *more)


def per_device(partials, master, moment_one, moment_two):
    d = lax.axis_index("dp")
    core = d & 1
    first = core == 0
    place = [jnp.where((i == 0) | ~first, i, jnp.where(i == 3, 1, i + 1)) for i in (d >> 5, (d >> 3) & 3, (d >> 1) & 3)]
    row = place[0] * 64 + place[1] * 16 + place[2] * 4

    amax, amax_send, send = block_max(core.reshape(1), partials)
    amax_other = lax.ppermute(amax_send, "dp", SWAP)
    send, amax_other = lax.optimization_barrier((send, amax_other))
    other = lax.ppermute(send, "dp", SWAP)
    amax = jnp.max(spread(jnp.maximum(amax, amax_other), FAR_GROUPS), axis=0)
    amax = spread(amax, NEAR_GROUPS)

    state = jnp.stack([master, moment_one, moment_two])
    state_same = lax.dynamic_slice_in_dim(state, core * HALF, HALF, 2)
    state_other = lax.dynamic_slice_in_dim(state, (1 - core) * HALF, HALF, 2)
    state_same = lax.ppermute(state_same, "dp", TO_SAME)
    state_other = lax.ppermute(state_other, "dp", TO_OTHER)
    state = jnp.where(
        first,
        jnp.concatenate([state_same, state_other], axis=1),
        jnp.concatenate([state_other, state_same], axis=1),
    )
    master, moment_one, moment_two = state

    mant = quantise(core.reshape(1), partials, other, amax)
    mant = jnp.sum(exchange(mant, NEAR_GROUPS).astype(F32), axis=0).astype(F16)
    total = jnp.sum(exchange(mant.reshape(8, 4, HALF), FAR_GROUPS).astype(F32), axis=0)

    own_amax = lax.dynamic_slice(amax, (0, row & 127, (row >> 7) * NB), (8, 4, NB))
    scale = scale_of(jnp.max(own_amax.astype(F32), axis=0))
    factor = scale / (2.0**MBITS * N_DP)
    reduced_grad = (total.reshape(4, NB, BLOCK) * factor[:, :, None]).reshape(4, HALF)
    moment_one_new = 0.9 * moment_one + 0.1 * reduced_grad
    moment_two_new = 0.95 * moment_two + 0.05 * reduced_grad * reduced_grad
    update = (moment_one_new / (1.0 - 0.9**STEP)) / (
        jnp.sqrt(moment_two_new / (1.0 - 0.95**STEP)) + 1e-08
    )
    master_new = master - 0.001 * (update + 0.1 * master)
    blocks = master_new.reshape(4, NB, BLOCK)
    wscale = jnp.max(jnp.abs(blocks), axis=2) + 1e-06
    wmant = (blocks / wscale[:, :, None]).astype(BF16)
    weights = (wmant.astype(F32) * wscale[:, :, None]).reshape(4, HALF).astype(BF16)

    out = jnp.stack([master_new, moment_one_new, moment_two_new, reduced_grad])
    out_same = lax.ppermute(jnp.where(first, out[:, :2], out[:, 2:]), "dp", FROM_SAME)
    out_other = lax.ppermute(jnp.where(first, out[:, 2:], out[:, :2]), "dp", FROM_OTHER)
    out = jnp.where(
        first,
        jnp.concatenate([out_same, out_other], axis=2),
        jnp.concatenate([out_other, out_same], axis=2),
    )

    weights = spread(weights, FAR_GROUPS).reshape(32, HALF)
    weights = spread(weights, NEAR_GROUPS)
    weights_other = lax.ppermute(weights, "dp", SWAP)
    full = place_rows(core.reshape(1), weights)
    full = place_rows((1 - core).reshape(1), weights_other, full)
    return (out[0], out[1], out[2], out[3], full)


def solution(mesh):
    in_specs = (P("dp", None, None), P("dp", None), P("dp", None), P("dp", None))
    out_specs = (P("dp", None), P("dp", None), P("dp", None), P("dp", None), P())
    return jax.shard_map(
        per_device, mesh=mesh, in_specs=in_specs, out_specs=out_specs, check_vma=False
    )
```

time: 198 us -> 193 us (0.975)
  the two profiles are of different devices: /device:TPU:1 before, /device:TPU:59 now
where the time goes in v2:
time: 193 us; the launch traced here: 192 us
  starting transfers between devices  108 us (56%)
  waiting for transfers between devices  31 us (16%)
  Pallas kernels  23.2 us (12%)
  blocking collectives  16.1 us (8%)
  other arithmetic  7.04 us (4%)
  local copies, waits for them, and re-layouts  6.35 us (3%)
    ppermute x1, starting transfers between devices, per_device(): lax.ppermute(jnp.where(first, out[:, 2:], out[:, :2]), 'dp', FROM_OTHER)  35.5 us
    ppermute x1, starting transfers between devices, per_device(): weights_other = lax.ppermute(weights, 'dp', SWAP)  29.6 us
    all_to_all x4, starting transfers between devices, exchange(): return lax.all_to_all(x, 'dp', 0, 0, axis_index_groups=among)  28 us
    all_to_all x4, waiting for transfers between devices, exchange(): return lax.all_to_all(x, 'dp', 0, 0, axis_index_groups=among)  19.2 us
    all_to_all x2, blocking collectives, exchange(): return lax.all_to_all(x, 'dp', 0, 0, axis_index_groups=among)  16.1 us
    ppermute x1, starting transfers between devices, per_device(): state_other = lax.ppermute(state_other, 'dp', TO_OTHER)  12 us
    pallas_call x2, Pallas kernels, place_rows(): pl.pallas_call(rows_kernel, out_shape=jax.ShapeDtypeStruct((ROWS, W), BF1...  9.03 us
    pallas_call x1, Pallas kernels, block_max(): pl.pallas_call(max_kernel, out_shape=(jax.ShapeDtypeStruct((128, 128), BF...  7.2 us
  transfers between devices with their start and end apart: 11, of which 6 were waited for; matrix products, arithmetic and copies ran while one was open for 2% of the time, Pallas kernels for 2%

profile of v2, /device:TPU:59, one launch (start us, length us, event | category | flops | bytes accessed | tf_op | source)
XLA Modules:
  0.0 192.3 jit_solution(13826332307504028812)
XLA Ops:
  0.6 7.2 %block_max.1 = (bf16[128,128]{1,0:T(8,128)(2,1)}, bf16[128,128]{1,0:T(8,128)(2,1)}, bf16[256,8192]{1,0:T(8,128)(2,1)}) custom-call(s32[1]{0:T(128)} %bitcast.3.core_ref.half_ref, bf16[1,256,16384]{2,1,0:T(8,128)(2,1)} %x_ref.3), custom_call_target="tpu_custom_call" | custom-call | tf_op jit(solution)/shard_map/block_max/pallas_call | solution.py:107
  7.8 0.8 collective-permute-start.2
  8.6 1.1 collective-permute-done.2
  10.0 0.8 max.3
  10.8 7.2 %all_to_all.30 = bf16[8,128,128]{2,1,0:T(8,128)(2,1)S(1)} all-to-all(bf16[8,128,128]{2,1,0:T(8,128)(2,1)S(1)} %broadcast_in_dim.66), channel_id=1, replica_groups={{0,6,24,30,96,102,120,126},{2,4,26,28,98,100,122,124},{8,14,16,22,104,1..., dimensions={0} | all-to-all | bytes 524288 | tf_op jit(solution)/shard_map/all_to_all | solution.py:55
  18.1 0.7 broadcast_in_dim.67
  18.8 7.5 %all-to-all-start.1 = ((bf16[8,128,128]{2,1,0:T(8,128)(2,1)}), bf16[8,128,128]{2,1,0:T(8,128)(2,1)S(1)}, u32[]{:S(2)}, u32[]{:S(2)}) async-start(bf16[8,128,128]{2,1,0:T(8,128)(2,1)} %broadcast_in_dim.67), calls=%async_computation.1 | async-start | bytes 524288 | tf_op jit(solution)/shard_map/all_to_all | solution.py:55
  26.3 3.9 %all-to-all-done.1.amax_ref = bf16[8,128,128]{2,1,0:T(8,128)(2,1)S(1)} async-done(((bf16[8,128,128]{2,1,0:T(8,128)(2,1)}), bf16[8,128,128]{2,1,0:T(8,128)(2,1)S(1)}, u32[]{:S(2)}, u32[]{:S(2)}) %all-to-all-start.1) | async-done | bytes 262176 | tf_op jit(solution)/shard_map/all_to_all | solution.py:55
  30.3 0.7 copy-done
  30.9 7.0 %quantise.1 = bf16[2,2,2,2,2,8,8192]{6,5,4,3,2,1,0:T(8,128)(2,1)} custom-call(s32[1]{0:T(128)} %bitcast.3.core_ref.half_ref, bf16[1,256,16384]{2,1,0:T(8,128)(2,1)} %x_ref.3, bf16[256,8192]{1,0:T(8,128)(2,1)} %collective-permute-done.3.other_ref, bf16[8,128,128]{2,1,0:T(8,128)(2,1)} %copy-done), custom_call_target="tpu_custom_call" | custom-call | tf_op jit(solution)/shard_map/quantise/pallas_call | solution.py:185
  38.0 7.3 %all-to-all-start.2 = ((bf16[8,32,8192]{2,1,0:T(8,128)(2,1)}), bf16[8,32,8192]{2,1,0:T(8,128)(2,1)}, u32[]{:S(2)}, u32[]{:S(2)}) async-start(bf16[8,32,8192]{2,1,0:T(8,128)(2,1)} %bitcast.58), calls=%async_computation.2 | async-start | bytes 8388608 | tf_op jit(solution)/shard_map/all_to_all | solution.py:55
  45.5 0.7 collective-permute-start
  46.2 12.0 %collective-permute-start.1 = (f32[3,2,8192]{2,1,0:T(2,128)S(1)}, f32[3,2,8192]{2,1,0:T(2,128)S(1)}, u32[]{:S(2)}, u32[]{:S(2)}) collective-permute-start(f32[3,2,8192]{2,1,0:T(2,128)S(1)} %get-tuple-element.30), channel_id=1, source_target_pairs={{1,0},{5,2},{7,4},{3,6},{17,8},{21,10},{23,12},{19,14},{25,16},{29... | collective-permute-start | bytes 589832 | tf_op jit(solution)/shard_map/ppermute | solution.py:257
  58.2 4.8 %collective-permute-done.1 = f32[3,2,8192]{2,1,0:T(2,128)S(1)} collective-permute-done((f32[3,2,8192]{2,1,0:T(2,128)S(1)}, f32[3,2,8192]{2,1,0:T(2,128)S(1)}, u32[]{:S(2)}, u32[]{:S(2)}) %collective-permute-start.1) | collective-permute-done | bytes 196640 | tf_op jit(solution)/shard_map/ppermute | solution.py:257
  63.3 12.1 %all-to-all-done.2 = bf16[8,32,8192]{2,1,0:T(8,128)(2,1)} async-done(((bf16[8,32,8192]{2,1,0:T(8,128)(2,1)}), bf16[8,32,8192]{2,1,0:T(8,128)(2,1)}, u32[]{:S(2)}, u32[]{:S(2)}) %all-to-all-start.2) | async-done | bytes 4194336 | tf_op jit(solution)/shard_map/all_to_all | solution.py:55
  75.4 2.9 %convert_reduce_fusion = f32[32,8192]{1,0:T(8,128)S(1)} fusion(bf16[8,32,8192]{2,1,0:T(8,128)(2,1)} %all-to-all-done.2), kind=kLoop, calls=%fused_computation | loop fusion | flops 3932160 | bytes 5242880 | tf_op jit(solution)/shard_map/reduce_sum | solution.py:266
  78.3 1.0 convert_element_type.30
  79.3 7.9 %all-to-all-start.3 = ((f16[8,4,8192]{2,1,0:T(4,128)(2,1)}), f16[8,4,8192]{2,1,0:T(4,128)(2,1)S(1)}, u32[]{:S(2)}, u32[]{:S(2)}) async-start(f16[8,4,8192]{2,1,0:T(4,128)(2,1)} %convert_element_type.30), calls=%async_computation.3 | async-start | bytes 1048576 | tf_op jit(solution)/shard_map/all_to_all | solution.py:55
  87.3 0.8 dynamic-slice_reduce_fusion
  88.3 3.2 %all-to-all-done.3 = f16[8,4,8192]{2,1,0:T(4,128)(2,1)S(1)} async-done(((f16[8,4,8192]{2,1,0:T(4,128)(2,1)}), f16[8,4,8192]{2,1,0:T(4,128)(2,1)S(1)}, u32[]{:S(2)}, u32[]{:S(2)}) %all-to-all-start.3) | async-done | bytes 524320 | tf_op jit(solution)/shard_map/all_to_all | solution.py:55
  91.5 0.6 convert_reduce_fusion.1
  93.0 8.9 %all_to_all.31 = bf16[8,4,8192]{2,1,0:T(4,128)(2,1)S(1)} all-to-all(bf16[8,4,8192]{2,1,0:T(4,128)(2,1)S(1)} %broadcast_in_dim.70), channel_id=1, replica_groups={{0,6,24,30,96,102,120,126},{2,4,26,28,98,100,122,124},{8,14,16,22,104,1..., dimensions={0} | all-to-all | bytes 1048576 | tf_op jit(solution)/shard_map/all_to_all | solution.py:55
  102.1 2.5 %broadcast_in_dim.72 = bf16[8,32,8192]{2,1,0:T(8,128)(2,1)} broadcast(bf16[32,8192]{1,0:T(8,128)(2,1)S(1)} %broadcast_in_dim.71), dimensions={1,2} | broadcast | bytes 4718592 | tf_op jit(solution)/shard_map/broadcast_in_dim | solution.py:59
  104.6 5.2 %all-to-all-start.5 = ((bf16[8,32,8192]{2,1,0:T(8,128)(2,1)}), bf16[8,32,8192]{2,1,0:T(8,128)(2,1)}, u32[]{:S(2)}, u32[]{:S(2)}) async-start(bf16[8,32,8192]{2,1,0:T(8,128)(2,1)} %broadcast_in_dim.72), calls=%async_computation.5 | async-start | bytes 8388608 | tf_op jit(solution)/shard_map/all_to_all | solution.py:55
  110.1 0.7 collective-permute-start.4
  110.8 35.5 %collective-permute-start.5 = (f32[4,2,8192]{2,1,0:T(2,128)S(1)}, f32[4,2,8192]{2,1,0:T(2,128)S(1)}, u32[]{:S(2)}, u32[]{:S(2)}) collective-permute-start(f32[4,2,8192]{2,1,0:T(2,128)S(1)} %get-tuple-element.25), channel_id=1, source_target_pairs={{0,1},{2,5},{4,7},{6,3},{8,17},{10,21},{12,23},{14,19},{16,25},{18... | collective-permute-start | bytes 786440 | tf_op jit(solution)/shard_map/ppermute | solution.py:286
  146.3 29.6 %collective-permute-start.6 = (bf16[8,32,8192]{2,1,0:T(8,128)(2,1)}, bf16[8,32,8192]{2,1,0:T(8,128)(2,1)}, u32[]{:S(2)}, u32[]{:S(2)}) collective-permute-start(bf16[8,32,8192]{2,1,0:T(8,128)(2,1)} %all-to-all-done.5), channel_id=1, source_target_pairs={{0,1},{1,0},{2,3},{3,2},{4,5},{5,4},{6,7},{7,6},{8,9},{9,8},{10,11... | collective-permute-start | bytes 12582920 | tf_op jit(solution)/shard_map/ppermute | solution.py:295
  175.9 6.0 %collective-permute-done.5 = f32[4,2,8192]{2,1,0:T(2,128)S(1)} collective-permute-done((f32[4,2,8192]{2,1,0:T(2,128)S(1)}, f32[4,2,8192]{2,1,0:T(2,128)S(1)}, u32[]{:S(2)}, u32[]{:S(2)}) %collective-permute-start.5) | collective-permute-done | bytes 262176 | tf_op jit(solution)/shard_map/ppermute | solution.py:286
  181.9 0.4 maximum_select_fusion
  182.3 0.8 slice_bitcast_fusion
  183.1 4.5 %place_rows.2.refs_0_ = bf16[256,16384]{1,0:T(8,128)(2,1)} custom-call(s32[1]{0:T(128)} %bitcast.3.core_ref.half_ref, bf16[2,2,2,2,2,8,8192]{6,5,4,3,2,1,0:T(8,128)(2,1)} %bitcast.13.w_ref), custom_call_target="tpu_custom_call" | custom-call | tf_op jit(solution)/shard_map/place_rows/pallas_call | solution.py:223
  187.6 4.5 %place_rows.3 = bf16[256,16384]{1,0:T(8,128)(2,1)} custom-call(s32[1]{0:T(128)} %bitcast.10.half_ref, bf16[2,2,2,2,2,8,8192]{6,5,4,3,2,1,0:T(8,128)(2,1)} %bitcast.12.w_ref, bf16[256,16384]{1,0:T(8,128)(2,1)} %place_rows.2.refs_0_), custom_call_target="tpu_custom_call", output_to_operand_aliasing={{}: (2, {})} | custom-call | tf_op jit(solution)/shard_map/place_rows/pallas_call | solution.py:223
  (32 shorter events, 2.5 us)
Async XLA Ops:
  7.8 1.8 collective-permute-start.2
  9.7 20.6 %collective-permute-start.3 = (bf16[256,8192]{1,0:T(8,128)(2,1)}, bf16[256,8192]{1,0:T(8,128)(2,1)}, u32[]{:S(2)}, u32[]{:S(2)}) collective-permute-start(bf16[256,8192]{1,0:T(8,128)(2,1)} %get-tuple-element.12), channel_id=1, source_target_pairs={{0,1},{1,0},{2,3},{3,2},{4,5},{5,4},{6,7},{7,6},{8,9},{9,8},{10,11... | collective-permute-start | bytes 12582920 | tf_op jit(solution)/shard_map/ppermute | solution.py:249
  18.8 11.5 %all-to-all-start.1 = ((bf16[8,128,128]{2,1,0:T(8,128)(2,1)}), bf16[8,128,128]{2,1,0:T(8,128)(2,1)S(1)}, u32[]{:S(2)}, u32[]{:S(2)}) async-start(bf16[8,128,128]{2,1,0:T(8,128)(2,1)} %broadcast_in_dim.67), calls=%async_computation.1 | async-start | bytes 524288 | tf_op jit(solution)/shard_map/all_to_all | solution.py:55
  30.3 0.7 copy-start
  37.9 7.3 %copy-start.1 = (f32[2,16384]{1,0:T(2,128)S(1)}, f32[2,16384]{1,0:T(2,128)}, u32[]{:S(2)}) copy-start(f32[2,16384]{1,0:T(2,128)} %param.7) | copy-start | bytes 393220
  37.9 7.3 %copy-start.2 = (f32[2,16384]{1,0:T(2,128)S(1)}, f32[2,16384]{1,0:T(2,128)}, u32[]{:S(2)}) copy-start(f32[2,16384]{1,0:T(2,128)} %param.6) | copy-start | bytes 393220
  38.0 7.3 %copy-start.3 = (f32[2,16384]{1,0:T(2,128)S(1)}, f32[2,16384]{1,0:T(2,128)}, u32[]{:S(2)}) copy-start(f32[2,16384]{1,0:T(2,128)} %param.5) | copy-start | bytes 393220
  38.0 37.4 %all-to-all-start.2 = ((bf16[8,32,8192]{2,1,0:T(8,128)(2,1)}), bf16[8,32,8192]{2,1,0:T(8,128)(2,1)}, u32[]{:S(2)}, u32[]{:S(2)}) async-start(bf16[8,32,8192]{2,1,0:T(8,128)(2,1)} %bitcast.58), calls=%async_computation.2 | async-start | bytes 8388608 | tf_op jit(solution)/shard_map/all_to_all | solution.py:55
  45.5 12.7 %collective-permute-start = (f32[3,2,8192]{2,1,0:T(2,128)S(1)}, f32[3,2,8192]{2,1,0:T(2,128)S(1)}, u32[]{:S(2)}, u32[]{:S(2)}) collective-permute-start(f32[3,2,8192]{2,1,0:T(2,128)S(1)} %get-tuple-element.29), channel_id=1, source_target_pairs={{0,0},{4,2},{6,4},{2,6},{16,8},{20,10},{22,12},{18,14},{24,16},{28... | collective-permute-start | bytes 589832 | tf_op jit(solution)/shard_map/ppermute | solution.py:256
  46.2 16.8 %collective-permute-start.1 = (f32[3,2,8192]{2,1,0:T(2,128)S(1)}, f32[3,2,8192]{2,1,0:T(2,128)S(1)}, u32[]{:S(2)}, u32[]{:S(2)}) collective-permute-start(f32[3,2,8192]{2,1,0:T(2,128)S(1)} %get-tuple-element.30), channel_id=1, source_target_pairs={{1,0},{5,2},{7,4},{3,6},{17,8},{21,10},{23,12},{19,14},{25,16},{29... | collective-permute-start | bytes 589832 | tf_op jit(solution)/shard_map/ppermute | solution.py:257
  79.3 12.2 %all-to-all-start.3 = ((f16[8,4,8192]{2,1,0:T(4,128)(2,1)}), f16[8,4,8192]{2,1,0:T(4,128)(2,1)S(1)}, u32[]{:S(2)}, u32[]{:S(2)}) async-start(f16[8,4,8192]{2,1,0:T(4,128)(2,1)} %convert_element_type.30), calls=%async_computation.3 | async-start | bytes 1048576 | tf_op jit(solution)/shard_map/all_to_all | solution.py:55
  104.6 41.7 %all-to-all-start.5 = ((bf16[8,32,8192]{2,1,0:T(8,128)(2,1)}), bf16[8,32,8192]{2,1,0:T(8,128)(2,1)}, u32[]{:S(2)}, u32[]{:S(2)}) async-start(bf16[8,32,8192]{2,1,0:T(8,128)(2,1)} %broadcast_in_dim.72), calls=%async_computation.5 | async-start | bytes 8388608 | tf_op jit(solution)/shard_map/all_to_all | solution.py:55
  110.1 65.8 %collective-permute-start.4 = (f32[4,2,8192]{2,1,0:T(2,128)S(1)}, f32[4,2,8192]{2,1,0:T(2,128)S(1)}, u32[]{:S(2)}, u32[]{:S(2)}) collective-permute-start(f32[4,2,8192]{2,1,0:T(2,128)S(1)} %get-tuple-element.24), channel_id=1, source_target_pairs={{0,0},{2,4},{4,6},{6,2},{8,16},{10,20},{12,22},{14,18},{16,24},{18... | collective-permute-start | bytes 786440 | tf_op jit(solution)/shard_map/ppermute | solution.py:285
  110.8 71.0 %collective-permute-start.5 = (f32[4,2,8192]{2,1,0:T(2,128)S(1)}, f32[4,2,8192]{2,1,0:T(2,128)S(1)}, u32[]{:S(2)}, u32[]{:S(2)}) collective-permute-start(f32[4,2,8192]{2,1,0:T(2,128)S(1)} %get-tuple-element.25), channel_id=1, source_target_pairs={{0,1},{2,5},{4,7},{6,3},{8,17},{10,21},{12,23},{14,19},{16,25},{18... | collective-permute-start | bytes 786440 | tf_op jit(solution)/shard_map/ppermute | solution.py:286
  146.3 41.3 %collective-permute-start.6 = (bf16[8,32,8192]{2,1,0:T(8,128)(2,1)}, bf16[8,32,8192]{2,1,0:T(8,128)(2,1)}, u32[]{:S(2)}, u32[]{:S(2)}) collective-permute-start(bf16[8,32,8192]{2,1,0:T(8,128)(2,1)} %all-to-all-done.5), channel_id=1, source_target_pairs={{0,1},{1,0},{2,3},{3,2},{4,5},{5,4},{6,7},{7,6},{8,9},{9,8},{10,11... | collective-permute-start | bytes 12582920 | tf_op jit(solution)/shard_map/ppermute | solution.py:295

commit v3 on v2

--- a/solution.py
+++ b/solution.py
@@ -18,8 +18,8 @@
 
 F16 = jnp.float16
 
-NEAR = {0: ((0, 1), (3, 2)), 1: ((1, 2), (0, 3))}
-FAR = {0: ((0, 3), (1, 2)), 1: ((0, 1), (2, 3))}
+NEAR = {0: ((0, 1), (2, 3)), 1: ((1, 2), (0, 3))}
+FAR = {0: ((1, 2), (0, 3)), 1: ((0, 1), (2, 3))}
 OWNER = {0: (0, 2, 3, 1), 1: (0, 1, 2, 3)}
 ALL = [(x, z, y) for x in range(4) for z in range(4) for y in range(4)]
 
@@ -139,9 +139,13 @@
     return mult
 
 
-def quant_kernel(core_ref, x_ref, other_ref, amax_ref, out_ref, own, other, mant, own_sem, other_sem, out_sem):
+def flipped(at_ref, x, z, y):
+    return ((x >> 1) ^ at_ref[1], (z >> 1) ^ at_ref[2], y ^ at_ref[3], x & 1, z & 1)
+
+
+def quant_kernel(at_ref, x_ref, other_ref, amax_ref, out_ref, own, other, mant, own_sem, other_sem, out_sem):
     rows = ROWS // own_sem.shape[0]
-    mine = pl.ds(pl.multiple_of(core_ref[0] * HALF, HALF), HALF)
+    mine = pl.ds(pl.multiple_of(at_ref[0] * HALF, HALF), HALF)
     loads = []
     for i in range(ROWS // rows):
         at = pl.ds(i * rows, rows)
@@ -172,7 +176,7 @@
             stores.append(
                 pltpu.make_async_copy(
                     mant.at[pl.ds(t * 8, 8)],
-                    out_ref.at[x >> 1, z >> 1, y, x & 1, z & 1],
+                    out_ref.at[flipped(at_ref, x, z, y)],
                     out_sem.at[t],
                 )
             )
@@ -181,7 +185,7 @@
         store.wait()
 
 
-def quantise(core, partials, other, amax, chunks=8):
+def quantise(at, partials, other, amax, chunks=8):
     out = pl.pallas_call(
         quant_kernel,
         out_shape=jax.ShapeDtypeStruct((2, 2, 2, 2, 2, 8, HALF), BF16),
@@ -195,17 +199,17 @@
         ],
         compiler_params=PARAMS,
         name="quantise",
-    )(core, partials, other, amax)
+    )(at, partials, other, amax)
     return out.reshape(8, 32, HALF)
 
 
-def rows_kernel(half_ref, w_ref, *refs):
+def rows_kernel(at_ref, w_ref, *refs):
     out_ref, buf, in_sem, out_sem = refs[-4:]
-    half = pl.ds(pl.multiple_of(half_ref[0] * HALF, HALF), HALF)
+    half = pl.ds(pl.multiple_of(at_ref[0] * HALF, HALF), HALF)
     loads, stores = [], []
     for t in range(ROWS // 8):
         x, z, y = t // 8, t // 2 % 4, t % 2
-        source = w_ref.at[x >> 1, z >> 1, y, x & 1, z & 1]
+        source = w_ref.at[flipped(at_ref, x, z, y)]
         loads.append(pltpu.make_async_copy(source, buf.at[t], in_sem.at[t]))
         target = out_ref.at[pl.ds(t * 8, 8), half]
         stores.append(pltpu.make_async_copy(buf.at[t], target, out_sem.at[t]))
@@ -218,7 +222,7 @@
         store.wait()
 
 
-def place_rows(half, w, before=None):
+def place_rows(at, w, before=None):
     more = () if before is None else (before,)
     return pl.pallas_call(
         rows_kernel,
@@ -233,14 +237,16 @@
         input_output_aliases={2: 0} if more else {},
         compiler_params=PARAMS,
         name="place_rows",
-    )(half, w.reshape(2, 2, 2, 2, 2, 8, HALF), *more)
+    )(at, w.reshape(2, 2, 2, 2, 2, 8, HALF), *more)
 
 
 def per_device(partials, master, moment_one, moment_two):
     d = lax.axis_index("dp")
     core = d & 1
     first = core == 0
-    place = [jnp.where((i == 0) | ~first, i, jnp.where(i == 3, 1, i + 1)) for i in (d >> 5, (d >> 3) & 3, (d >> 1) & 3)]
+    chip = (d >> 5, (d >> 3) & 3, (d >> 1) & 3)
+    at = [jnp.stack([c, *((1 - c) * (i >> 1) for i in chip)]) for c in (core, 1 - core)]
+    place = [jnp.where((i == 0) | ~first, i, jnp.where(i == 3, 1, i + 1)) for i in chip]
     row = place[0] * 64 + place[1] * 16 + place[2] * 4
 
     amax, amax_send, send = block_max(core.reshape(1), partials)
@@ -262,7 +268,7 @@
     )
     master, moment_one, moment_two = state
 
-    mant = quantise(core.reshape(1), partials, other, amax)
+    mant = quantise(at[0], partials, other, amax)
     mant = jnp.sum(exchange(mant, NEAR_GROUPS).astype(F32), axis=0).astype(F16)
     total = jnp.sum(exchange(mant.reshape(8, 4, HALF), FAR_GROUPS).astype(F32), axis=0)
 
@@ -293,8 +299,8 @@
     weights = spread(weights, FAR_GROUPS).reshape(32, HALF)
     weights = spread(weights, NEAR_GROUPS)
     weights_other = lax.ppermute(weights, "dp", SWAP)
-    full = place_rows(core.reshape(1), weights)
-    full = place_rows((1 - core).reshape(1), weights_other, full)
+    full = place_rows(at[0], weights)
+    full = place_rows(at[1], weights_other, full)
     return (out[0], out[1], out[2], out[3], full)
 
 

time: 193 us -> 195 us (1.010)
  the two profiles are of different devices: /device:TPU:59 before, /device:TPU:43 now
where the time goes in v3:
time: 195 us; the launch traced here: 194 us
  starting transfers between devices  100 us (51%)
  waiting for transfers between devices  37.1 us (19%)
  Pallas kernels  24.6 us (13%)
  blocking collectives  16.4 us (8%)
  other arithmetic  8.27 us (4%)
  local copies, waits for them, and re-layouts  6.35 us (3%)
    ppermute x1, starting transfers between devices, per_device(): lax.ppermute(jnp.where(first, out[:, 2:], out[:, :2]), 'dp', FROM_OTHER)  34.1 us
    all_to_all x4, starting transfers between devices, exchange(): return lax.all_to_all(x, 'dp', 0, 0, axis_index_groups=among)  27.4 us
    ppermute x1, starting transfers between devices, per_device(): weights_other = lax.ppermute(weights, 'dp', SWAP)  24.1 us
    all_to_all x4, waiting for transfers between devices, exchange(): return lax.all_to_all(x, 'dp', 0, 0, axis_index_groups=among)  18.5 us
    all_to_all x2, blocking collectives, exchange(): return lax.all_to_all(x, 'dp', 0, 0, axis_index_groups=among)  16.4 us
    ppermute x1, waiting for transfers between devices, per_device(): lax.ppermute(jnp.where(first, out[:, 2:], out[:, :2]), 'dp', FROM_OTHER)  12.8 us
    ppermute x1, starting transfers between devices, per_device(): state_other = lax.ppermute(state_other, 'dp', TO_OTHER)  11.9 us
    pallas_call x2, Pallas kernels, place_rows(): pl.pallas_call(rows_kernel, out_shape=jax.ShapeDtypeStruct((ROWS, W), BF1...  10.4 us
  transfers between devices with their start and end apart: 11, of which 6 were waited for; matrix products, arithmetic and copies ran while one was open for 3% of the time, Pallas kernels for 3%

profile of v3, /device:TPU:43, one launch (start us, length us, event | category | flops | bytes accessed | tf_op | source)
XLA Modules:
  0.0 193.8 jit_solution(2699625371468764495)
XLA Ops:
  0.6 7.2 %block_max.1 = (bf16[128,128]{1,0:T(8,128)(2,1)}, bf16[128,128]{1,0:T(8,128)(2,1)}, bf16[256,8192]{1,0:T(8,128)(2,1)}) custom-call(s32[1]{0:T(128)} %bitcast.3.core_ref, bf16[1,256,16384]{2,1,0:T(8,128)(2,1)} %x_ref.3), custom_call_target="tpu_custom_call" | custom-call | tf_op jit(solution)/shard_map/block_max/pallas_call | solution.py:107
  7.8 0.8 collective-permute-start.2
  8.6 1.1 collective-permute-done.2
  10.0 0.8 max.3
  10.8 7.2 %all_to_all.30 = bf16[8,128,128]{2,1,0:T(8,128)(2,1)S(1)} all-to-all(bf16[8,128,128]{2,1,0:T(8,128)(2,1)S(1)} %broadcast_in_dim.66), channel_id=1, replica_groups={{42,44,50,52,74,76,82,84},{40,46,48,54,72,78,80,86},{34,36,58,60,66,68,..., dimensions={0} | all-to-all | bytes 524288 | tf_op jit(solution)/shard_map/all_to_all | solution.py:55
  18.1 0.7 broadcast_in_dim.67
  18.8 6.9 %all-to-all-start.1 = ((bf16[8,128,128]{2,1,0:T(8,128)(2,1)}), bf16[8,128,128]{2,1,0:T(8,128)(2,1)S(1)}, u32[]{:S(2)}, u32[]{:S(2)}) async-start(bf16[8,128,128]{2,1,0:T(8,128)(2,1)} %broadcast_in_dim.67), calls=%async_computation.1 | async-start | bytes 524288 | tf_op jit(solution)/shard_map/all_to_all | solution.py:55
  25.7 0.6 pad_add_fusion.at_ref
  26.4 4.8 %all-to-all-done.1.amax_ref = bf16[8,128,128]{2,1,0:T(8,128)(2,1)S(1)} async-done(((bf16[8,128,128]{2,1,0:T(8,128)(2,1)}), bf16[8,128,128]{2,1,0:T(8,128)(2,1)S(1)}, u32[]{:S(2)}, u32[]{:S(2)}) %all-to-all-start.1) | async-done | bytes 262176 | tf_op jit(solution)/shard_map/all_to_all | solution.py:55
  31.2 0.7 copy-done
  31.9 7.0 %quantise.1 = bf16[2,2,2,2,2,8,8192]{6,5,4,3,2,1,0:T(8,128)(2,1)} custom-call(s32[4]{0:T(128)} %pad_add_fusion.at_ref, bf16[1,256,16384]{2,1,0:T(8,128)(2,1)} %x_ref.3, bf16[256,8192]{1,0:T(8,128)(2,1)} %collective-permute-done.3.other_ref, bf16[8,128,128]{2,1,0:T(8,128)(2,1)} %copy-done), custom_call_target="tpu_custom_call" | custom-call | tf_op jit(solution)/shard_map/quantise/pallas_call | solution.py:189
  38.9 4.7 %all-to-all-start.2 = ((bf16[8,32,8192]{2,1,0:T(8,128)(2,1)}), bf16[8,32,8192]{2,1,0:T(8,128)(2,1)}, u32[]{:S(2)}, u32[]{:S(2)}) async-start(bf16[8,32,8192]{2,1,0:T(8,128)(2,1)} %bitcast.64), calls=%async_computation.2 | async-start | bytes 8388608 | tf_op jit(solution)/shard_map/all_to_all | solution.py:55
  43.9 0.7 collective-permute-start
  44.6 11.9 %collective-permute-start.1 = (f32[3,2,8192]{2,1,0:T(2,128)S(1)}, f32[3,2,8192]{2,1,0:T(2,128)S(1)}, u32[]{:S(2)}, u32[]{:S(2)}) collective-permute-start(f32[3,2,8192]{2,1,0:T(2,128)S(1)} %get-tuple-element.30), channel_id=1, source_target_pairs={{1,0},{5,2},{7,4},{3,6},{17,8},{21,10},{23,12},{19,14},{25,16},{29... | collective-permute-start | bytes 589832 | tf_op jit(solution)/shard_map/ppermute | solution.py:263
  56.5 4.8 %collective-permute-done.1 = f32[3,2,8192]{2,1,0:T(2,128)S(1)} collective-permute-done((f32[3,2,8192]{2,1,0:T(2,128)S(1)}, f32[3,2,8192]{2,1,0:T(2,128)S(1)}, u32[]{:S(2)}, u32[]{:S(2)}) %collective-permute-start.1) | collective-permute-done | bytes 196640 | tf_op jit(solution)/shard_map/ppermute | solution.py:263
  61.5 10.5 %all-to-all-done.2 = bf16[8,32,8192]{2,1,0:T(8,128)(2,1)} async-done(((bf16[8,32,8192]{2,1,0:T(8,128)(2,1)}), bf16[8,32,8192]{2,1,0:T(8,128)(2,1)}, u32[]{:S(2)}, u32[]{:S(2)}) %all-to-all-start.2) | async-done | bytes 4194336 | tf_op jit(solution)/shard_map/all_to_all | solution.py:55
  72.0 2.9 %convert_reduce_fusion = f32[32,8192]{1,0:T(8,128)S(1)} fusion(bf16[8,32,8192]{2,1,0:T(8,128)(2,1)} %all-to-all-done.2), kind=kLoop, calls=%fused_computation | loop fusion | flops 3932160 | bytes 5242880 | tf_op jit(solution)/shard_map/reduce_sum | solution.py:272
  75.0 1.0 convert_element_type.30
  76.0 9.9 %all-to-all-start.3 = ((f16[8,4,8192]{2,1,0:T(4,128)(2,1)}), f16[8,4,8192]{2,1,0:T(4,128)(2,1)S(1)}, u32[]{:S(2)}, u32[]{:S(2)}) async-start(f16[8,4,8192]{2,1,0:T(4,128)(2,1)} %convert_element_type.30), calls=%async_computation.3 | async-start | bytes 1048576 | tf_op jit(solution)/shard_map/all_to_all | solution.py:55
  85.9 0.8 dynamic-slice_reduce_fusion
  87.0 3.1 %all-to-all-done.3 = f16[8,4,8192]{2,1,0:T(4,128)(2,1)S(1)} async-done(((f16[8,4,8192]{2,1,0:T(4,128)(2,1)}), f16[8,4,8192]{2,1,0:T(4,128)(2,1)S(1)}, u32[]{:S(2)}, u32[]{:S(2)}) %all-to-all-start.3) | async-done | bytes 524320 | tf_op jit(solution)/shard_map/all_to_all | solution.py:55
  90.1 0.6 convert_reduce_fusion.1
  91.6 9.2 %all_to_all.31 = bf16[8,4,8192]{2,1,0:T(4,128)(2,1)S(1)} all-to-all(bf16[8,4,8192]{2,1,0:T(4,128)(2,1)S(1)} %broadcast_in_dim.70), channel_id=1, replica_groups={{42,44,50,52,74,76,82,84},{40,46,48,54,72,78,80,86},{34,36,58,60,66,68,..., dimensions={0} | all-to-all | bytes 1048576 | tf_op jit(solution)/shard_map/all_to_all | solution.py:55
  101.0 2.5 %broadcast_in_dim.72 = bf16[8,32,8192]{2,1,0:T(8,128)(2,1)} broadcast(bf16[32,8192]{1,0:T(8,128)(2,1)S(1)} %broadcast_in_dim.71), dimensions={1,2} | broadcast | bytes 4718592 | tf_op jit(solution)/shard_map/broadcast_in_dim | solution.py:59
  103.5 5.9 %all-to-all-start.5 = ((bf16[8,32,8192]{2,1,0:T(8,128)(2,1)}), bf16[8,32,8192]{2,1,0:T(8,128)(2,1)}, u32[]{:S(2)}, u32[]{:S(2)}) async-start(bf16[8,32,8192]{2,1,0:T(8,128)(2,1)} %broadcast_in_dim.72), calls=%async_computation.5 | async-start | bytes 8388608 | tf_op jit(solution)/shard_map/all_to_all | solution.py:55
  109.7 0.7 collective-permute-start.4
  110.4 34.1 %collective-permute-start.5 = (f32[4,2,8192]{2,1,0:T(2,128)S(1)}, f32[4,2,8192]{2,1,0:T(2,128)S(1)}, u32[]{:S(2)}, u32[]{:S(2)}) collective-permute-start(f32[4,2,8192]{2,1,0:T(2,128)S(1)} %get-tuple-element.25), channel_id=1, source_target_pairs={{0,1},{2,5},{4,7},{6,3},{8,17},{10,21},{12,23},{14,19},{16,25},{18... | collective-permute-start | bytes 786440 | tf_op jit(solution)/shard_map/ppermute | solution.py:292
  145.1 24.1 %collective-permute-start.6 = (bf16[8,32,8192]{2,1,0:T(8,128)(2,1)}, bf16[8,32,8192]{2,1,0:T(8,128)(2,1)}, u32[]{:S(2)}, u32[]{:S(2)}) collective-permute-start(bf16[8,32,8192]{2,1,0:T(8,128)(2,1)} %all-to-all-done.5), channel_id=1, source_target_pairs={{0,1},{1,0},{2,3},{3,2},{4,5},{5,4},{6,7},{7,6},{8,9},{9,8},{10,11... | collective-permute-start | bytes 12582920 | tf_op jit(solution)/shard_map/ppermute | solution.py:301
  169.2 12.8 %collective-permute-done.5 = f32[4,2,8192]{2,1,0:T(2,128)S(1)} collective-permute-done((f32[4,2,8192]{2,1,0:T(2,128)S(1)}, f32[4,2,8192]{2,1,0:T(2,128)S(1)}, u32[]{:S(2)}, u32[]{:S(2)}) %collective-permute-start.5) | collective-permute-done | bytes 262176 | tf_op jit(solution)/shard_map/ppermute | solution.py:292
  182.4 0.8 slice_bitcast_fusion
  183.2 5.2 %place_rows.2.refs_0_ = bf16[256,16384]{1,0:T(8,128)(2,1)} custom-call(s32[4]{0:T(128)} %pad_add_fusion.at_ref, bf16[2,2,2,2,2,8,8192]{6,5,4,3,2,1,0:T(8,128)(2,1)} %bitcast.19.w_ref), custom_call_target="tpu_custom_call" | custom-call | tf_op jit(solution)/shard_map/place_rows/pallas_call | solution.py:227
  188.4 5.2 %place_rows.3 = bf16[256,16384]{1,0:T(8,128)(2,1)} custom-call(s32[4]{0:T(128)} %pad_add_fusion.1.at_ref, bf16[2,2,2,2,2,8,8192]{6,5,4,3,2,1,0:T(8,128)(2,1)} %bitcast.18.w_ref, bf16[256,16384]{1,0:T(8,128)(2,1)} %place_rows.2.refs_0_), custom_call_target="tpu_custom_call", output_to_operand_aliasing={{}: (2, {})} | custom-call | tf_op jit(solution)/shard_map/place_rows/pallas_call | solution.py:227
  (34 shorter events, 3.5 us)
Async XLA Ops:
  7.8 1.8 collective-permute-start.2
  9.7 21.5 %collective-permute-start.3 = (bf16[256,8192]{1,0:T(8,128)(2,1)}, bf16[256,8192]{1,0:T(8,128)(2,1)}, u32[]{:S(2)}, u32[]{:S(2)}) collective-permute-start(bf16[256,8192]{1,0:T(8,128)(2,1)} %get-tuple-element.12), channel_id=1, source_target_pairs={{0,1},{1,0},{2,3},{3,2},{4,5},{5,4},{6,7},{7,6},{8,9},{9,8},{10,11... | collective-permute-start | bytes 12582920 | tf_op jit(solution)/shard_map/ppermute | solution.py:255
  18.8 12.4 %all-to-all-start.1 = ((bf16[8,128,128]{2,1,0:T(8,128)(2,1)}), bf16[8,128,128]{2,1,0:T(8,128)(2,1)S(1)}, u32[]{:S(2)}, u32[]{:S(2)}) async-start(bf16[8,128,128]{2,1,0:T(8,128)(2,1)} %broadcast_in_dim.67), calls=%async_computation.1 | async-start | bytes 524288 | tf_op jit(solution)/shard_map/all_to_all | solution.py:55
  31.2 0.7 copy-start
  38.9 4.7 %copy-start.1 = (f32[2,16384]{1,0:T(2,128)S(1)}, f32[2,16384]{1,0:T(2,128)}, u32[]{:S(2)}) copy-start(f32[2,16384]{1,0:T(2,128)} %param.7) | copy-start | bytes 393220
  38.9 4.7 %copy-start.2 = (f32[2,16384]{1,0:T(2,128)S(1)}, f32[2,16384]{1,0:T(2,128)}, u32[]{:S(2)}) copy-start(f32[2,16384]{1,0:T(2,128)} %param.6) | copy-start | bytes 393220
  38.9 4.7 %copy-start.3 = (f32[2,16384]{1,0:T(2,128)S(1)}, f32[2,16384]{1,0:T(2,128)}, u32[]{:S(2)}) copy-start(f32[2,16384]{1,0:T(2,128)} %param.5) | copy-start | bytes 393220
  38.9 33.1 %all-to-all-start.2 = ((bf16[8,32,8192]{2,1,0:T(8,128)(2,1)}), bf16[8,32,8192]{2,1,0:T(8,128)(2,1)}, u32[]{:S(2)}, u32[]{:S(2)}) async-start(bf16[8,32,8192]{2,1,0:T(8,128)(2,1)} %bitcast.64), calls=%async_computation.2 | async-start | bytes 8388608 | tf_op jit(solution)/shard_map/all_to_all | solution.py:55
  43.9 12.6 %collective-permute-start = (f32[3,2,8192]{2,1,0:T(2,128)S(1)}, f32[3,2,8192]{2,1,0:T(2,128)S(1)}, u32[]{:S(2)}, u32[]{:S(2)}) collective-permute-start(f32[3,2,8192]{2,1,0:T(2,128)S(1)} %get-tuple-element.29), channel_id=1, source_target_pairs={{0,0},{4,2},{6,4},{2,6},{16,8},{20,10},{22,12},{18,14},{24,16},{28... | collective-permute-start | bytes 589832 | tf_op jit(solution)/shard_map/ppermute | solution.py:262
  44.6 16.7 %collective-permute-start.1 = (f32[3,2,8192]{2,1,0:T(2,128)S(1)}, f32[3,2,8192]{2,1,0:T(2,128)S(1)}, u32[]{:S(2)}, u32[]{:S(2)}) collective-permute-start(f32[3,2,8192]{2,1,0:T(2,128)S(1)} %get-tuple-element.30), channel_id=1, source_target_pairs={{1,0},{5,2},{7,4},{3,6},{17,8},{21,10},{23,12},{19,14},{25,16},{29... | collective-permute-start | bytes 589832 | tf_op jit(solution)/shard_map/ppermute | solution.py:263
  76.0 14.1 %all-to-all-start.3 = ((f16[8,4,8192]{2,1,0:T(4,128)(2,1)}), f16[8,4,8192]{2,1,0:T(4,128)(2,1)S(1)}, u32[]{:S(2)}, u32[]{:S(2)}) async-start(f16[8,4,8192]{2,1,0:T(4,128)(2,1)} %convert_element_type.30), calls=%async_computation.3 | async-start | bytes 1048576 | tf_op jit(solution)/shard_map/all_to_all | solution.py:55
  103.5 41.6 %all-to-all-start.5 = ((bf16[8,32,8192]{2,1,0:T(8,128)(2,1)}), bf16[8,32,8192]{2,1,0:T(8,128)(2,1)}, u32[]{:S(2)}, u32[]{:S(2)}) async-start(bf16[8,32,8192]{2,1,0:T(8,128)(2,1)} %broadcast_in_dim.72), calls=%async_computation.5 | async-start | bytes 8388608 | tf_op jit(solution)/shard_map/all_to_all | solution.py:55
  109.7 59.5 %collective-permute-start.4 = (f32[4,2,8192]{2,1,0:T(2,128)S(1)}, f32[4,2,8192]{2,1,0:T(2,128)S(1)}, u32[]{:S(2)}, u32[]{:S(2)}) collective-permute-start(f32[4,2,8192]{2,1,0:T(2,128)S(1)} %get-tuple-element.24), channel_id=1, source_target_pairs={{0,0},{2,4},{4,6},{6,2},{8,16},{10,20},{12,22},{14,18},{16,24},{18... | collective-permute-start | bytes 786440 | tf_op jit(solution)/shard_map/ppermute | solution.py:291
  110.4 71.7 %collective-permute-start.5 = (f32[4,2,8192]{2,1,0:T(2,128)S(1)}, f32[4,2,8192]{2,1,0:T(2,128)S(1)}, u32[]{:S(2)}, u32[]{:S(2)}) collective-permute-start(f32[4,2,8192]{2,1,0:T(2,128)S(1)} %get-tuple-element.25), channel_id=1, source_target_pairs={{0,1},{2,5},{4,7},{6,3},{8,17},{10,21},{12,23},{14,19},{16,25},{18... | collective-permute-start | bytes 786440 | tf_op jit(solution)/shard_map/ppermute | solution.py:292
  145.1 43.3 %collective-permute-start.6 = (bf16[8,32,8192]{2,1,0:T(8,128)(2,1)}, bf16[8,32,8192]{2,1,0:T(8,128)(2,1)}, u32[]{:S(2)}, u32[]{:S(2)}) collective-permute-start(bf16[8,32,8192]{2,1,0:T(8,128)(2,1)} %all-to-all-done.5), channel_id=1, source_target_pairs={{0,1},{1,0},{2,3},{3,2},{4,5},{5,4},{6,7},{7,6},{8,9},{9,8},{10,11... | collective-permute-start | bytes 12582920 | tf_op jit(solution)/shard_map/ppermute | solution.py:301

commit v4 on v2

--- a/solution.py
+++ b/solution.py
@@ -15,13 +15,9 @@
 NB = HALF // BLOCK
 F32 = jnp.float32
 BF16 = jnp.bfloat16
-
-F16 = jnp.float16
-
-NEAR = {0: ((0, 1), (3, 2)), 1: ((1, 2), (0, 3))}
-FAR = {0: ((0, 3), (1, 2)), 1: ((0, 1), (2, 3))}
-OWNER = {0: (0, 2, 3, 1), 1: (0, 1, 2, 3)}
-ALL = [(x, z, y) for x in range(4) for z in range(4) for y in range(4)]
+CHIPS = 64
+
+PAIRS = (((0, 1), (2, 3)), ((1, 2), (0, 3)))
 
 
 def device(x, z, y, core):
@@ -32,23 +28,15 @@
     return [
         [device(x, z, y, core) for x in px for z in pz for y in py]
         for core in (0, 1)
-        for px in pairs[core]
-        for pz in pairs[core]
-        for py in pairs[core]
+        for px in pairs
+        for pz in pairs
+        for py in pairs
     ]
 
 
-def owner(core, at):
-    return tuple(OWNER[core][i] for i in at)
-
-
-NEAR_GROUPS = groups(NEAR)
-FAR_GROUPS = groups(FAR)
+CUBES = [groups(pairs) for pairs in PAIRS]
+SAME_CORE = [[2 * chip + core for chip in range(CHIPS)] for core in (0, 1)]
 SWAP = [(d, d ^ 1) for d in range(N_DP)]
-TO_SAME = [(device(*owner(c, at), c), device(*at, c)) for c in (0, 1) for at in ALL]
-TO_OTHER = [(device(*owner(c, at), 1 - c), device(*at, c)) for c in (0, 1) for at in ALL]
-FROM_SAME = [(b, a) for a, b in TO_SAME]
-FROM_OTHER = [(b, a) for a, b in TO_OTHER]
 
 
 def exchange(x, among):
@@ -56,7 +44,7 @@
 
 
 def spread(x, among):
-    return exchange(jnp.broadcast_to(x[None], (8, *x.shape)), among)
+    return exchange(jnp.broadcast_to(x[None], (len(among[0]), *x.shape)), among)
 
 
 def max_kernel(core_ref, x_ref, amax_ref, other_ref, send_ref, buf, own_max, other_max, in_sem, out_sem):
@@ -139,11 +127,19 @@
     return mult
 
 
+PART = HALF // 2
+
+
+def top_rows():
+    return lax.broadcasted_iota(jnp.int32, (8, BLOCK), 0) < 4
+
+
 def quant_kernel(core_ref, x_ref, other_ref, amax_ref, out_ref, own, other, mant, own_sem, other_sem, out_sem):
-    rows = ROWS // own_sem.shape[0]
+    chunks = own_sem.shape[0]
+    rows = ROWS // chunks
     mine = pl.ds(pl.multiple_of(core_ref[0] * HALF, HALF), HALF)
-    loads = []
-    for i in range(ROWS // rows):
+    loads, stores = [], []
+    for i in range(chunks):
         at = pl.ds(i * rows, rows)
         loads.append(
             (
@@ -153,72 +149,84 @@
         )
         for load in loads[i]:
             load.start()
-    stores = []
-    for i in range(ROWS // rows):
+    top = top_rows()
+    for i in range(chunks):
         at = pl.ds(i * rows, rows)
         low = i * rows % 128
         mult = mult_of(jnp.max(amax_ref[:, low : low + rows, :].astype(F32), axis=0))
-        for load in loads[i]:
-            load.wait()
-        for b in range(NB):
+
+        def mantissas(b):
             cols = slice(b * BLOCK, (b + 1) * BLOCK)
             lane = b + (NB if i * rows >= 128 else 0)
             m = jnp.broadcast_to(mult[:, lane : lane + 1], (rows, BLOCK))
             v = jnp.floor(own[at, cols].astype(F32) * m + 0.5)
-            v = v + jnp.floor(other[at, cols].astype(F32) * m + 0.5)
-            mant[at, cols] = v.astype(BF16)
-        for t in range(i * rows // 8, (i + 1) * rows // 8):
-            x, z, y = t // 8, t // 2 % 4, t % 2
-            stores.append(
-                pltpu.make_async_copy(
-                    mant.at[pl.ds(t * 8, 8)],
-                    out_ref.at[x >> 1, z >> 1, y, x & 1, z & 1],
-                    out_sem.at[t],
-                )
-            )
-            stores[t].start()
+            return v + jnp.floor(other[at, cols].astype(F32) * m + 0.5)
+
+        for load in loads[i]:
+            load.wait()
+        for b in range(NB // 2):
+            left, right = mantissas(b), mantissas(b + NB // 2)
+            cols = slice(b * BLOCK, (b + 1) * BLOCK)
+            for t in range(rows // 8):
+                l, r = left[t * 8 : t * 8 + 8], right[t * 8 : t * 8 + 8]
+                chip = (i * rows // 8 + t) * 2
+                mant[chip, :, cols] = jnp.where(top, l, pltpu.roll(r, 4, 0)).astype(BF16)
+                mant[chip + 1, :, cols] = jnp.where(top, pltpu.roll(l, 4, 0), r).astype(BF16)
+        at = pl.ds(i * rows // 4, rows // 4)
+        stores.append(pltpu.make_async_copy(mant.at[at], out_ref.at[at], out_sem.at[i]))
+        stores[i].start()
     for store in stores:
         store.wait()
 
 
 def quantise(core, partials, other, amax, chunks=8):
-    out = pl.pallas_call(
+    return pl.pallas_call(
         quant_kernel,
-        out_shape=jax.ShapeDtypeStruct((2, 2, 2, 2, 2, 8, HALF), BF16),
+        out_shape=jax.ShapeDtypeStruct((CHIPS, 8, PART), BF16),
         in_specs=[SMEM, HBM, HBM, VMEM],
         out_specs=HBM,
         scratch_shapes=[
-            *[pltpu.VMEM((ROWS, HALF), BF16)] * 3,
-            pltpu.SemaphoreType.DMA((chunks,)),
-            pltpu.SemaphoreType.DMA((chunks,)),
-            pltpu.SemaphoreType.DMA((ROWS // 8,)),
+            pltpu.VMEM((ROWS, HALF), BF16),
+            pltpu.VMEM((ROWS, HALF), BF16),
+            pltpu.VMEM((CHIPS, 8, PART), BF16),
+            pltpu.SemaphoreType.DMA((chunks,)),
+            pltpu.SemaphoreType.DMA((chunks,)),
+            pltpu.SemaphoreType.DMA((chunks,)),
         ],
         compiler_params=PARAMS,
         name="quantise",
     )(core, partials, other, amax)
-    return out.reshape(8, 32, HALF)
 
 
 def rows_kernel(half_ref, w_ref, *refs):
-    out_ref, buf, in_sem, out_sem = refs[-4:]
+    out_ref, got, full, in_sem, out_sem = refs[-5:]
+    chunks = in_sem.shape[0]
+    rows = ROWS // chunks
     half = pl.ds(pl.multiple_of(half_ref[0] * HALF, HALF), HALF)
     loads, stores = [], []
-    for t in range(ROWS // 8):
-        x, z, y = t // 8, t // 2 % 4, t % 2
-        source = w_ref.at[x >> 1, z >> 1, y, x & 1, z & 1]
-        loads.append(pltpu.make_async_copy(source, buf.at[t], in_sem.at[t]))
-        target = out_ref.at[pl.ds(t * 8, 8), half]
-        stores.append(pltpu.make_async_copy(buf.at[t], target, out_sem.at[t]))
-    for load in loads:
-        load.start()
-    for load, store in zip(loads, stores):
-        load.wait()
-        store.start()
+    for i in range(chunks):
+        at = pl.ds(i * rows // 4, rows // 4)
+        loads.append(pltpu.make_async_copy(w_ref.at[at], got.at[at], in_sem.at[i]))
+        at = pl.ds(i * rows, rows)
+        stores.append(pltpu.make_async_copy(full.at[at], out_ref.at[at, half], out_sem.at[i]))
+        loads[i].start()
+    top = top_rows()
+    for i in range(chunks):
+        loads[i].wait()
+        for t in range(i * rows // 8, (i + 1) * rows // 8):
+            for b in range(NB // 2):
+                cols = slice(b * BLOCK, (b + 1) * BLOCK)
+                u = got[2 * t, :, cols].astype(F32)
+                v = got[2 * t + 1, :, cols].astype(F32)
+                full[t * 8 : t * 8 + 8, cols] = jnp.where(top, u, pltpu.roll(v, 4, 0)).astype(BF16)
+                cols = slice(PART + b * BLOCK, PART + (b + 1) * BLOCK)
+                full[t * 8 : t * 8 + 8, cols] = jnp.where(top, pltpu.roll(u, 4, 0), v).astype(BF16)
+        stores[i].start()
     for store in stores:
         store.wait()
 
 
-def place_rows(half, w, before=None):
+def place_rows(half, w, before=None, chunks=8):
     more = () if before is None else (before,)
     return pl.pallas_call(
         rows_kernel,
@@ -226,45 +234,44 @@
         in_specs=[SMEM, HBM, *(HBM for _ in more)],
         out_specs=HBM,
         scratch_shapes=[
-            pltpu.VMEM((ROWS // 8, 8, HALF), BF16),
-            pltpu.SemaphoreType.DMA((ROWS // 8,)),
-            pltpu.SemaphoreType.DMA((ROWS // 8,)),
+            pltpu.VMEM((CHIPS, 8, PART), BF16),
+            pltpu.VMEM((ROWS, HALF), BF16),
+            pltpu.SemaphoreType.DMA((chunks,)),
+            pltpu.SemaphoreType.DMA((chunks,)),
         ],
         input_output_aliases={2: 0} if more else {},
         compiler_params=PARAMS,
         name="place_rows",
-    )(half, w.reshape(2, 2, 2, 2, 2, 8, HALF), *more)
+    )(half, w, *more)
 
 
 def per_device(partials, master, moment_one, moment_two):
     d = lax.axis_index("dp")
-    core = d & 1
+    core, chip = d & 1, d >> 1
     first = core == 0
-    place = [jnp.where((i == 0) | ~first, i, jnp.where(i == 3, 1, i + 1)) for i in (d >> 5, (d >> 3) & 3, (d >> 1) & 3)]
-    row = place[0] * 64 + place[1] * 16 + place[2] * 4
+    row = chip * 4
 
     amax, amax_send, send = block_max(core.reshape(1), partials)
     amax_other = lax.ppermute(amax_send, "dp", SWAP)
     send, amax_other = lax.optimization_barrier((send, amax_other))
     other = lax.ppermute(send, "dp", SWAP)
-    amax = jnp.max(spread(jnp.maximum(amax, amax_other), FAR_GROUPS), axis=0)
-    amax = spread(amax, NEAR_GROUPS)
+    amax = jnp.max(spread(jnp.maximum(amax, amax_other), CUBES[0]), axis=0)
+    amax = spread(amax, CUBES[1])
 
     state = jnp.stack([master, moment_one, moment_two])
-    state_same = lax.dynamic_slice_in_dim(state, core * HALF, HALF, 2)
+    state_own = lax.dynamic_slice_in_dim(state, core * HALF, HALF, 2)
     state_other = lax.dynamic_slice_in_dim(state, (1 - core) * HALF, HALF, 2)
-    state_same = lax.ppermute(state_same, "dp", TO_SAME)
-    state_other = lax.ppermute(state_other, "dp", TO_OTHER)
+    state_other = lax.ppermute(state_other, "dp", SWAP)
     state = jnp.where(
         first,
-        jnp.concatenate([state_same, state_other], axis=1),
-        jnp.concatenate([state_other, state_same], axis=1),
+        jnp.concatenate([state_own, state_other], axis=1),
+        jnp.concatenate([state_other, state_own], axis=1),
     )
     master, moment_one, moment_two = state
 
-    mant = quantise(core.reshape(1), partials, other, amax)
-    mant = jnp.sum(exchange(mant, NEAR_GROUPS).astype(F32), axis=0).astype(F16)
-    total = jnp.sum(exchange(mant.reshape(8, 4, HALF), FAR_GROUPS).astype(F32), axis=0)
+    mant = exchange(quantise(core.reshape(1), partials, other, amax), SAME_CORE)
+    total = jnp.sum(mant.astype(F32), axis=0)
+    total = total.reshape(2, 4, PART).transpose(1, 0, 2).reshape(4, HALF)
 
     own_amax = lax.dynamic_slice(amax, (0, row & 127, (row >> 7) * NB), (8, 4, NB))
     scale = scale_of(jnp.max(own_amax.astype(F32), axis=0))
@@ -282,16 +289,16 @@
     weights = (wmant.astype(F32) * wscale[:, :, None]).reshape(4, HALF).astype(BF16)
 
     out = jnp.stack([master_new, moment_one_new, moment_two_new, reduced_grad])
-    out_same = lax.ppermute(jnp.where(first, out[:, :2], out[:, 2:]), "dp", FROM_SAME)
-    out_other = lax.ppermute(jnp.where(first, out[:, 2:], out[:, :2]), "dp", FROM_OTHER)
+    out_own = jnp.where(first, out[:, :2], out[:, 2:])
+    out_other = lax.ppermute(jnp.where(first, out[:, 2:], out[:, :2]), "dp", SWAP)
     out = jnp.where(
         first,
-        jnp.concatenate([out_same, out_other], axis=2),
-        jnp.concatenate([out_other, out_same], axis=2),
+        jnp.concatenate([out_own, out_other], axis=2),
+        jnp.concatenate([out_other, out_own], axis=2),
     )
 
-    weights = spread(weights, FAR_GROUPS).reshape(32, HALF)
-    weights = spread(weights, NEAR_GROUPS)
+    weights = weights.reshape(4, 2, PART).transpose(1, 0, 2).reshape(8, PART)
+    weights = spread(weights, SAME_CORE)
     weights_other = lax.ppermute(weights, "dp", SWAP)
     full = place_rows(core.reshape(1), weights)
     full = place_rows((1 - core).reshape(1), weights_other, full)

time: 193 us -> 196 us (1.016)
  the two profiles are of different devices: /device:TPU:59 before, /device:TPU:103 now
where the time goes in v4:
time: 196 us
  waiting for transfers between devices  118 us (60%)
  starting transfers between devices  22.8 us (12%)
  blocking collectives  21.9 us (11%)
  Pallas kernels  20.9 us (11%)
  other arithmetic  6.55 us (3%)
  local copies, waits for them, and re-layouts  4.1 us (2%)
    all_to_all x2, waiting for transfers between devices, exchange(): return lax.all_to_all(x, 'dp', 0, 0, axis_index_groups=among)  114 us
    all_to_all x2, blocking collectives, exchange(): return lax.all_to_all(x, 'dp', 0, 0, axis_index_groups=among)  21.9 us
    all_to_all x2, starting transfers between devices, exchange(): return lax.all_to_all(x, 'dp', 0, 0, axis_index_groups=among)  16.8 us
    pallas_call x1, Pallas kernels, block_max(): pl.pallas_call(max_kernel, out_shape=(jax.ShapeDtypeStruct((128, 128), BF...  7.2 us
    pallas_call x1, Pallas kernels, quantise(): pl.pallas_call(quant_kernel, out_shape=jax.ShapeDtypeStruct((CHIPS, 8, PA...  6.95 us
    pallas_call x2, Pallas kernels, place_rows(): pl.pallas_call(rows_kernel, out_shape=jax.ShapeDtypeStruct((ROWS, W), BF1...  6.76 us
  transfers between devices with their start and end apart: 7, of which 5 were waited for; matrix products, arithmetic and copies ran while one was open for 2% of the time, Pallas kernels for 2%

profile of v4, /device:TPU:103, one launch (start us, length us, event | category | flops | bytes accessed | tf_op | source)
XLA Modules:
  0.0 195.7 jit_solution(14588656534024977395)
XLA Ops:
  0.6 7.2 %block_max.1 = (bf16[128,128]{1,0:T(8,128)(2,1)}, bf16[128,128]{1,0:T(8,128)(2,1)}, bf16[256,8192]{1,0:T(8,128)(2,1)}) custom-call(s32[1]{0:T(128)} %bitcast.3.core_ref.half_ref, bf16[1,256,16384]{2,1,0:T(8,128)(2,1)} %x_ref.3), custom_call_target="tpu_custom_call" | custom-call | tf_op jit(solution)/shard_map/block_max/pallas_call | solution.py:95
  7.8 0.8 collective-permute-start.1
  8.6 1.1 collective-permute-done.1
  9.7 0.3 collective-permute-start.2
  10.0 0.8 max.3
  10.8 9.2 %all_to_all.20 = bf16[8,128,128]{2,1,0:T(8,128)(2,1)S(1)} all-to-all(bf16[8,128,128]{2,1,0:T(8,128)(2,1)S(1)} %broadcast_in_dim.58), channel_id=1, replica_groups={{0,2,8,10,32,34,40,42},{4,6,12,14,36,38,44,46},{16,18,24,26,48,50,56,58..., dimensions={0} | all-to-all | bytes 524288 | tf_op jit(solution)/shard_map/all_to_all | solution.py:43
  20.1 12.7 %all_to_all.21.amax_ref = bf16[8,128,128]{2,1,0:T(8,128)(2,1)} all-to-all(bf16[8,128,128]{2,1,0:T(8,128)(2,1)S(1)} %broadcast_in_dim.59), channel_id=1, replica_groups={{42,44,50,52,74,76,82,84},{40,46,48,54,72,78,80,86},{34,36,58,60,66,68,..., dimensions={0} | all-to-all | bytes 524288 | tf_op jit(solution)/shard_map/all_to_all | solution.py:43
  32.8 6.9 %quantise.1 = bf16[64,8,4096]{2,1,0:T(8,128)(2,1)} custom-call(s32[1]{0:T(128)} %bitcast.3.core_ref.half_ref, bf16[1,256,16384]{2,1,0:T(8,128)(2,1)} %x_ref.3, bf16[256,8192]{1,0:T(8,128)(2,1)} %collective-permute-done.2.other_ref, bf16[8,128,128]{2,1,0:T(8,128)(2,1)} %all_to_all.21.amax_ref), custom_call_target="tpu_custom_call" | custom-call | tf_op jit(solution)/shard_map/quantise/pallas_call | solution.py:183
  39.8 9.7 %all-to-all-start.2 = ((bf16[64,8,4096]{2,1,0:T(8,128)(2,1)}), bf16[64,8,4096]{2,1,0:T(8,128)(2,1)}, u32[]{:S(2)}, u32[]{:S(2)}) async-start(bf16[64,8,4096]{2,1,0:T(8,128)(2,1)} %quantise.1), calls=%async_computation.2 | async-start | bytes 8388608 | tf_op jit(solution)/shard_map/all_to_all | solution.py:43
  49.6 0.2 pad_maximum_fusion.1
  49.8 2.7 %collective-permute-start = (f32[3,2,8192]{2,1,0:T(2,128)S(1)}, f32[3,2,8192]{2,1,0:T(2,128)S(1)}, u32[]{:S(2)}, u32[]{:S(2)}) collective-permute-start(f32[3,2,8192]{2,1,0:T(2,128)S(1)} %get-tuple-element.36), channel_id=1, source_target_pairs={{0,1},{1,0},{2,3},{3,2},{4,5},{5,4},{6,7},{7,6},{8,9},{9,8},{10,11... | collective-permute-start | bytes 589832 | tf_op jit(solution)/shard_map/ppermute | solution.py:264
  52.5 1.1 collective-permute-done
  53.6 0.3 maximum_select_fusion.1
  53.9 0.8 dynamic-slice_reduce_fusion
  55.0 54.2 %all-to-all-done.2 = bf16[64,8,4096]{2,1,0:T(8,128)(2,1)} async-done(((bf16[64,8,4096]{2,1,0:T(8,128)(2,1)}), bf16[64,8,4096]{2,1,0:T(8,128)(2,1)}, u32[]{:S(2)}, u32[]{:S(2)}) %all-to-all-start.2) | async-done | bytes 4194336 | tf_op jit(solution)/shard_map/all_to_all | solution.py:43
  109.2 2.8 %convert_reduce_fusion = f32[8,4096]{1,0:T(8,128)S(1)} fusion(bf16[64,8,4096]{2,1,0:T(8,128)(2,1)} %all-to-all-done.2), kind=kLoop, calls=%fused_computation | loop fusion | flops 4161536 | bytes 4325376 | tf_op jit(solution)/shard_map/reduce_sum | solution.py:273
  112.2 0.1 reshape_reshape.6
  112.3 0.3 slice_multiply_fusion.1
  112.6 0.3 fusion.14
  113.1 0.3 fusion.16
  113.4 2.5 %broadcast_in_dim.62 = bf16[64,8,4096]{2,1,0:T(8,128)(2,1)} broadcast(bf16[8,4096]{1,0:T(8,128)(2,1)S(1)} %broadcast_in_dim.61), dimensions={1,2} | broadcast | bytes 4259840 | tf_op jit(solution)/shard_map/broadcast_in_dim | solution.py:47
  115.9 7.1 %all-to-all-start.3 = ((bf16[64,8,4096]{2,1,0:T(8,128)(2,1)}), bf16[64,8,4096]{2,1,0:T(8,128)(2,1)}, u32[]{:S(2)}, u32[]{:S(2)}) async-start(bf16[64,8,4096]{2,1,0:T(8,128)(2,1)} %broadcast_in_dim.62), calls=%async_computation.3 | async-start | bytes 8388608 | tf_op jit(solution)/shard_map/all_to_all | solution.py:43
  123.0 0.1 pad_maximum_fusion
  123.2 0.2 broadcast_select_fusion.1
  123.4 1.5 collective-permute-start.3
  124.9 59.5 %all-to-all-done.3.w_ref = bf16[64,8,4096]{2,1,0:T(8,128)(2,1)} async-done(((bf16[64,8,4096]{2,1,0:T(8,128)(2,1)}), bf16[64,8,4096]{2,1,0:T(8,128)(2,1)}, u32[]{:S(2)}, u32[]{:S(2)}) %all-to-all-start.3) | async-done | bytes 4194336 | tf_op jit(solution)/shard_map/all_to_all | solution.py:43
  184.4 0.7 collective-permute-start.4
  185.1 0.4 maximum_select_fusion
  185.5 0.8 slice_bitcast_fusion
  186.3 3.4 %place_rows.2.refs_0_ = bf16[256,16384]{1,0:T(8,128)(2,1)} custom-call(s32[1]{0:T(128)} %bitcast.3.core_ref.half_ref, bf16[64,8,4096]{2,1,0:T(8,128)(2,1)} %all-to-all-done.3.w_ref), custom_call_target="tpu_custom_call" | custom-call | tf_op jit(solution)/shard_map/place_rows/pallas_call | solution.py:231
  189.7 2.5 %collective-permute-done.4.w_ref = bf16[64,8,4096]{2,1,0:T(8,128)(2,1)} collective-permute-done((bf16[64,8,4096]{2,1,0:T(8,128)(2,1)}, bf16[64,8,4096]{2,1,0:T(8,128)(2,1)}, u32[]{:S(2)}, u32[]{:S(2)}) %collective-permute-start.4) | collective-permute-done | bytes 4194336 | tf_op jit(solution)/shard_map/ppermute | solution.py:302
  192.2 3.4 %place_rows.3 = bf16[256,16384]{1,0:T(8,128)(2,1)} custom-call(s32[1]{0:T(128)} %bitcast.10.half_ref, bf16[64,8,4096]{2,1,0:T(8,128)(2,1)} %collective-permute-done.4.w_ref, bf16[256,16384]{1,0:T(8,128)(2,1)} %place_rows.2.refs_0_), custom_call_target="tpu_custom_call", output_to_operand_aliasing={{}: (2, {})} | custom-call | tf_op jit(solution)/shard_map/place_rows/pallas_call | solution.py:231
  (22 shorter events, 0.7 us)
Async XLA Ops:
  7.8 1.8 collective-permute-start.1
  9.7 23.1 %collective-permute-start.2 = (bf16[256,8192]{1,0:T(8,128)(2,1)}, bf16[256,8192]{1,0:T(8,128)(2,1)}, u32[]{:S(2)}, u32[]{:S(2)}) collective-permute-start(bf16[256,8192]{1,0:T(8,128)(2,1)} %get-tuple-element.12), channel_id=1, source_target_pairs={{0,1},{1,0},{2,3},{3,2},{4,5},{5,4},{6,7},{7,6},{8,9},{9,8},{10,11... | collective-permute-start | bytes 12582920 | tf_op jit(solution)/shard_map/ppermute | solution.py:257
  39.8 9.8 %copy-start = (f32[2,16384]{1,0:T(2,128)S(1)}, f32[2,16384]{1,0:T(2,128)}, u32[]{:S(2)}) copy-start(f32[2,16384]{1,0:T(2,128)} %param.7) | copy-start | bytes 393220
  39.8 9.8 %copy-start.1 = (f32[2,16384]{1,0:T(2,128)S(1)}, f32[2,16384]{1,0:T(2,128)}, u32[]{:S(2)}) copy-start(f32[2,16384]{1,0:T(2,128)} %param.6) | copy-start | bytes 393220
  39.8 9.8 %copy-start.2 = (f32[2,16384]{1,0:T(2,128)S(1)}, f32[2,16384]{1,0:T(2,128)}, u32[]{:S(2)}) copy-start(f32[2,16384]{1,0:T(2,128)} %param.5) | copy-start | bytes 393220
  39.8 69.4 %all-to-all-start.2 = ((bf16[64,8,4096]{2,1,0:T(8,128)(2,1)}), bf16[64,8,4096]{2,1,0:T(8,128)(2,1)}, u32[]{:S(2)}, u32[]{:S(2)}) async-start(bf16[64,8,4096]{2,1,0:T(8,128)(2,1)} %quantise.1), calls=%async_computation.2 | async-start | bytes 8388608 | tf_op jit(solution)/shard_map/all_to_all | solution.py:43
  49.8 3.8 %collective-permute-start = (f32[3,2,8192]{2,1,0:T(2,128)S(1)}, f32[3,2,8192]{2,1,0:T(2,128)S(1)}, u32[]{:S(2)}, u32[]{:S(2)}) collective-permute-start(f32[3,2,8192]{2,1,0:T(2,128)S(1)} %get-tuple-element.36), channel_id=1, source_target_pairs={{0,1},{1,0},{2,3},{3,2},{4,5},{5,4},{6,7},{7,6},{8,9},{9,8},{10,11... | collective-permute-start | bytes 589832 | tf_op jit(solution)/shard_map/ppermute | solution.py:264
  115.9 68.4 %all-to-all-start.3 = ((bf16[64,8,4096]{2,1,0:T(8,128)(2,1)}), bf16[64,8,4096]{2,1,0:T(8,128)(2,1)}, u32[]{:S(2)}, u32[]{:S(2)}) async-start(bf16[64,8,4096]{2,1,0:T(8,128)(2,1)} %broadcast_in_dim.62), calls=%async_computation.3 | async-start | bytes 8388608 | tf_op jit(solution)/shard_map/all_to_all | solution.py:43
  123.4 61.7 %collective-permute-start.3 = (f32[4,2,8192]{2,1,0:T(2,128)S(1)}, f32[4,2,8192]{2,1,0:T(2,128)S(1)}, u32[]{:S(2)}, u32[]{:S(2)}) collective-permute-start(f32[4,2,8192]{2,1,0:T(2,128)S(1)} %get-tuple-element.24), channel_id=1, source_target_pairs={{0,1},{1,0},{2,3},{3,2},{4,5},{5,4},{6,7},{7,6},{8,9},{9,8},{10,11... | collective-permute-start | bytes 786440 | tf_op jit(solution)/shard_map/ppermute | solution.py:293
  184.4 7.8 %collective-permute-start.4 = (bf16[64,8,4096]{2,1,0:T(8,128)(2,1)}, bf16[64,8,4096]{2,1,0:T(8,128)(2,1)}, u32[]{:S(2)}, u32[]{:S(2)}) collective-permute-start(bf16[64,8,4096]{2,1,0:T(8,128)(2,1)} %all-to-all-done.3.w_ref), channel_id=1, source_target_pairs={{0,1},{1,0},{2,3},{3,2},{4,5},{5,4},{6,7},{7,6},{8,9},{9,8},{10,11... | collective-permute-start | bytes 12582920 | tf_op jit(solution)/shard_map/ppermute | solution.py:302

commit v5 on v3

--- a/solution.py
+++ b/solution.py
@@ -15,13 +15,12 @@
 NB = HALF // BLOCK
 F32 = jnp.float32
 BF16 = jnp.bfloat16
-
 F16 = jnp.float16
 
-NEAR = {0: ((0, 1), (2, 3)), 1: ((1, 2), (0, 3))}
-FAR = {0: ((1, 2), (0, 3)), 1: ((0, 1), (2, 3))}
-OWNER = {0: (0, 2, 3, 1), 1: (0, 1, 2, 3)}
-ALL = [(x, z, y) for x in range(4) for z in range(4) for y in range(4)]
+NEAR = {0: ((0, 1), (3, 2)), 1: ((1, 2), (0, 3))}
+FAR = {0: ((0, 3), (1, 2)), 1: ((0, 1), (2, 3))}
+PLACE = {0: (0, 2, 3, 1), 1: (0, 1, 2, 3)}
+CUBES = ({0: FAR[1], 1: FAR[1]}, {0: NEAR[1], 1: NEAR[1]})
 
 
 def device(x, z, y, core):
@@ -38,17 +37,9 @@
     ]
 
 
-def owner(core, at):
-    return tuple(OWNER[core][i] for i in at)
-
-
 NEAR_GROUPS = groups(NEAR)
 FAR_GROUPS = groups(FAR)
 SWAP = [(d, d ^ 1) for d in range(N_DP)]
-TO_SAME = [(device(*owner(c, at), c), device(*at, c)) for c in (0, 1) for at in ALL]
-TO_OTHER = [(device(*owner(c, at), 1 - c), device(*at, c)) for c in (0, 1) for at in ALL]
-FROM_SAME = [(b, a) for a, b in TO_SAME]
-FROM_OTHER = [(b, a) for a, b in TO_OTHER]
 
 
 def exchange(x, among):
@@ -56,7 +47,7 @@
 
 
 def spread(x, among):
-    return exchange(jnp.broadcast_to(x[None], (8, *x.shape)), among)
+    return exchange(jnp.broadcast_to(x[None], (len(among[0]), *x.shape)), among)
 
 
 def max_kernel(core_ref, x_ref, amax_ref, other_ref, send_ref, buf, own_max, other_max, in_sem, out_sem):
@@ -139,15 +130,22 @@
     return mult
 
 
-def flipped(at_ref, x, z, y):
-    return ((x >> 1) ^ at_ref[1], (z >> 1) ^ at_ref[2], y ^ at_ref[3], x & 1, z & 1)
+def block_of(at_ref, x, z, y):
+    px, pz = at_ref[1 + x], at_ref[1 + z]
+    return (px >> 1, pz >> 1, y, px & 1, pz & 1)
+
+
+def tile_mask(at_ref):
+    row = lax.broadcasted_iota(jnp.int32, (8, BLOCK), 0)
+    return row < 4 + 4 * at_ref[0], 4 * (1 - at_ref[0])
 
 
 def quant_kernel(at_ref, x_ref, other_ref, amax_ref, out_ref, own, other, mant, own_sem, other_sem, out_sem):
-    rows = ROWS // own_sem.shape[0]
+    chunks = own_sem.shape[0]
+    rows = ROWS // chunks
     mine = pl.ds(pl.multiple_of(at_ref[0] * HALF, HALF), HALF)
-    loads = []
-    for i in range(ROWS // rows):
+    loads, stores = [], []
+    for i in range(chunks):
         at = pl.ds(i * rows, rows)
         loads.append(
             (
@@ -157,8 +155,8 @@
         )
         for load in loads[i]:
             load.start()
-    stores = []
-    for i in range(ROWS // rows):
+    keep, turn = tile_mask(at_ref)
+    for i in range(chunks):
         at = pl.ds(i * rows, rows)
         low = i * rows % 128
         mult = mult_of(jnp.max(amax_ref[:, low : low + rows, :].astype(F32), axis=0))
@@ -170,16 +168,14 @@
             m = jnp.broadcast_to(mult[:, lane : lane + 1], (rows, BLOCK))
             v = jnp.floor(own[at, cols].astype(F32) * m + 0.5)
             v = v + jnp.floor(other[at, cols].astype(F32) * m + 0.5)
-            mant[at, cols] = v.astype(BF16)
+            for t in range(0, rows // 8, 2):
+                p, q = v[t * 8 : t * 8 + 8], v[t * 8 + 8 : t * 8 + 16]
+                tile = i * rows // 8 + t
+                mant[tile, :, cols] = jnp.where(keep, p, q).astype(BF16)
+                mant[tile + 1, :, cols] = pltpu.roll(jnp.where(keep, q, p), turn, 0).astype(BF16)
         for t in range(i * rows // 8, (i + 1) * rows // 8):
-            x, z, y = t // 8, t // 2 % 4, t % 2
-            stores.append(
-                pltpu.make_async_copy(
-                    mant.at[pl.ds(t * 8, 8)],
-                    out_ref.at[flipped(at_ref, x, z, y)],
-                    out_sem.at[t],
-                )
-            )
+            target = out_ref.at[block_of(at_ref, t // 8, t // 2 % 4, t % 2)]
+            stores.append(pltpu.make_async_copy(mant.at[t], target, out_sem.at[t]))
             stores[t].start()
     for store in stores:
         store.wait()
@@ -192,7 +188,9 @@
         in_specs=[SMEM, HBM, HBM, VMEM],
         out_specs=HBM,
         scratch_shapes=[
-            *[pltpu.VMEM((ROWS, HALF), BF16)] * 3,
+            pltpu.VMEM((ROWS, HALF), BF16),
+            pltpu.VMEM((ROWS, HALF), BF16),
+            pltpu.VMEM((ROWS // 8, 8, HALF), BF16),
             pltpu.SemaphoreType.DMA((chunks,)),
             pltpu.SemaphoreType.DMA((chunks,)),
             pltpu.SemaphoreType.DMA((ROWS // 8,)),
@@ -204,25 +202,35 @@
 
 
 def rows_kernel(at_ref, w_ref, *refs):
-    out_ref, buf, in_sem, out_sem = refs[-4:]
+    out_ref, got, full, in_sem, out_sem = refs[-5:]
+    chunks = out_sem.shape[0]
+    rows = ROWS // chunks
     half = pl.ds(pl.multiple_of(at_ref[0] * HALF, HALF), HALF)
     loads, stores = [], []
     for t in range(ROWS // 8):
-        x, z, y = t // 8, t // 2 % 4, t % 2
-        source = w_ref.at[flipped(at_ref, x, z, y)]
-        loads.append(pltpu.make_async_copy(source, buf.at[t], in_sem.at[t]))
-        target = out_ref.at[pl.ds(t * 8, 8), half]
-        stores.append(pltpu.make_async_copy(buf.at[t], target, out_sem.at[t]))
-    for load in loads:
-        load.start()
-    for load, store in zip(loads, stores):
-        load.wait()
-        store.start()
+        source = w_ref.at[block_of(at_ref, t // 8, t // 2 % 4, t % 2)]
+        loads.append(pltpu.make_async_copy(source, got.at[t], in_sem.at[t]))
+        loads[t].start()
+    for i in range(chunks):
+        at = pl.ds(i * rows, rows)
+        stores.append(pltpu.make_async_copy(full.at[at], out_ref.at[at, half], out_sem.at[i]))
+    keep, turn = tile_mask(at_ref)
+    for i in range(chunks):
+        for t in range(i * rows // 8, (i + 1) * rows // 8, 2):
+            loads[t].wait()
+            loads[t + 1].wait()
+            for b in range(NB):
+                cols = slice(b * BLOCK, (b + 1) * BLOCK)
+                p = got[t, :, cols].astype(F32)
+                q = pltpu.roll(got[t + 1, :, cols].astype(F32), turn, 0)
+                full[t * 8 : t * 8 + 8, cols] = jnp.where(keep, p, q).astype(BF16)
+                full[t * 8 + 8 : t * 8 + 16, cols] = jnp.where(keep, q, p).astype(BF16)
+        stores[i].start()
     for store in stores:
         store.wait()
 
 
-def place_rows(at, w, before=None):
+def place_rows(at, w, before=None, chunks=8):
     more = () if before is None else (before,)
     return pl.pallas_call(
         rows_kernel,
@@ -231,8 +239,9 @@
         out_specs=HBM,
         scratch_shapes=[
             pltpu.VMEM((ROWS // 8, 8, HALF), BF16),
+            pltpu.VMEM((ROWS, HALF), BF16),
             pltpu.SemaphoreType.DMA((ROWS // 8,)),
-            pltpu.SemaphoreType.DMA((ROWS // 8,)),
+            pltpu.SemaphoreType.DMA((chunks,)),
         ],
         input_output_aliases={2: 0} if more else {},
         compiler_params=PARAMS,
@@ -242,35 +251,34 @@
 
 def per_device(partials, master, moment_one, moment_two):
     d = lax.axis_index("dp")
-    core = d & 1
+    core, chip = d & 1, d >> 1
     first = core == 0
-    chip = (d >> 5, (d >> 3) & 3, (d >> 1) & 3)
-    at = [jnp.stack([c, *((1 - c) * (i >> 1) for i in chip)]) for c in (core, 1 - core)]
-    place = [jnp.where((i == 0) | ~first, i, jnp.where(i == 3, 1, i + 1)) for i in chip]
-    row = place[0] * 64 + place[1] * 16 + place[2] * 4
+    row = chip * 4
+    places = [jnp.where(first, PLACE[0][i], PLACE[1][i]) for i in range(4)]
+    others = [jnp.where(first, PLACE[1][i], PLACE[0][i]) for i in range(4)]
+    mine, theirs = jnp.stack([core, *places]), jnp.stack([1 - core, *others])
 
     amax, amax_send, send = block_max(core.reshape(1), partials)
     amax_other = lax.ppermute(amax_send, "dp", SWAP)
     send, amax_other = lax.optimization_barrier((send, amax_other))
     other = lax.ppermute(send, "dp", SWAP)
-    amax = jnp.max(spread(jnp.maximum(amax, amax_other), FAR_GROUPS), axis=0)
-    amax = spread(amax, NEAR_GROUPS)
+    amax = jnp.max(spread(jnp.maximum(amax, amax_other), groups(CUBES[0])), axis=0)
+    amax = spread(amax, groups(CUBES[1]))
 
     state = jnp.stack([master, moment_one, moment_two])
-    state_same = lax.dynamic_slice_in_dim(state, core * HALF, HALF, 2)
+    state_own = lax.dynamic_slice_in_dim(state, core * HALF, HALF, 2)
     state_other = lax.dynamic_slice_in_dim(state, (1 - core) * HALF, HALF, 2)
-    state_same = lax.ppermute(state_same, "dp", TO_SAME)
-    state_other = lax.ppermute(state_other, "dp", TO_OTHER)
+    state_other = lax.ppermute(state_other, "dp", SWAP)
     state = jnp.where(
         first,
-        jnp.concatenate([state_same, state_other], axis=1),
-        jnp.concatenate([state_other, state_same], axis=1),
+        jnp.concatenate([state_own, state_other], axis=1),
+        jnp.concatenate([state_other, state_own], axis=1),
     )
     master, moment_one, moment_two = state
 
-    mant = quantise(at[0], partials, other, amax)
-    mant = jnp.sum(exchange(mant, NEAR_GROUPS).astype(F32), axis=0).astype(F16)
-    total = jnp.sum(exchange(mant.reshape(8, 4, HALF), FAR_GROUPS).astype(F32), axis=0)
+    mant = exchange(quantise(mine, partials, other, amax), NEAR_GROUPS)
+    mant = jnp.sum(mant.astype(F32), axis=0).astype(F16).reshape(8, 4, HALF)
+    total = jnp.sum(exchange(mant, FAR_GROUPS).astype(F32), axis=0)
 
     own_amax = lax.dynamic_slice(amax, (0, row & 127, (row >> 7) * NB), (8, 4, NB))
     scale = scale_of(jnp.max(own_amax.astype(F32), axis=0))
@@ -288,19 +296,19 @@
     weights = (wmant.astype(F32) * wscale[:, :, None]).reshape(4, HALF).astype(BF16)
 
     out = jnp.stack([master_new, moment_one_new, moment_two_new, reduced_grad])
-    out_same = lax.ppermute(jnp.where(first, out[:, :2], out[:, 2:]), "dp", FROM_SAME)
-    out_other = lax.ppermute(jnp.where(first, out[:, 2:], out[:, :2]), "dp", FROM_OTHER)
+    out_own = jnp.where(first, out[:, :2], out[:, 2:])
+    out_other = lax.ppermute(jnp.where(first, out[:, 2:], out[:, :2]), "dp", SWAP)
     out = jnp.where(
         first,
-        jnp.concatenate([out_same, out_other], axis=2),
-        jnp.concatenate([out_other, out_same], axis=2),
+        jnp.concatenate([out_own, out_other], axis=2),
+        jnp.concatenate([out_other, out_own], axis=2),
     )
 
     weights = spread(weights, FAR_GROUPS).reshape(32, HALF)
     weights = spread(weights, NEAR_GROUPS)
     weights_other = lax.ppermute(weights, "dp", SWAP)
-    full = place_rows(at[0], weights)
-    full = place_rows(at[1], weights_other, full)
+    full = place_rows(mine, weights)
+    full = place_rows(theirs, weights_other, full)
     return (out[0], out[1], out[2], out[3], full)
 
 

time: 195 us -> 165 us (0.85)
  the two profiles are of different devices: /device:TPU:43 before, /device:TPU:1 now
where the time goes in v5:
time: 165 us; the launch traced here: 162 us
  waiting for transfers between devices  60.1 us (36%)
  starting transfers between devices  43.2 us (26%)
  Pallas kernels  23.3 us (14%)
  blocking collectives  19.8 us (12%)
  local copies, waits for them, and re-layouts  7.66 us (5%)
  other arithmetic  7.04 us (4%)
    all_to_all x4, waiting for transfers between devices, exchange(): return lax.all_to_all(x, 'dp', 0, 0, axis_index_groups=among)  56.6 us
    all_to_all x4, starting transfers between devices, exchange(): return lax.all_to_all(x, 'dp', 0, 0, axis_index_groups=among)  21.8 us
    all_to_all x2, blocking collectives, exchange(): return lax.all_to_all(x, 'dp', 0, 0, axis_index_groups=among)  19.8 us
    ppermute x1, starting transfers between devices, per_device(): lax.ppermute(jnp.where(first, out[:, 2:], out[:, :2]), 'dp', SWAP)  9.29 us
    pallas_call x2, Pallas kernels, place_rows(): pl.pallas_call(rows_kernel, out_shape=jax.ShapeDtypeStruct((ROWS, W), BF1...  9.06 us
    ppermute x1, starting transfers between devices, per_device(): weights_other = lax.ppermute(weights, 'dp', SWAP)  7.83 us
    pallas_call x1, Pallas kernels, block_max(): pl.pallas_call(max_kernel, out_shape=(jax.ShapeDtypeStruct((128, 128), BF...  7.2 us
    pallas_call x1, Pallas kernels, quantise(): pl.pallas_call(quant_kernel, out_shape=jax.ShapeDtypeStruct((2, 2, 2, 2,...  7.05 us
  transfers between devices with their start and end apart: 9, of which 7 were waited for; matrix products, arithmetic and copies ran while one was open for 4% of the time, Pallas kernels for 3%

profile of v5, /device:TPU:1, one launch (start us, length us, event | category | flops | bytes accessed | tf_op | source)
XLA Modules:
  0.0 162.2 jit_solution(789198501243288284)
XLA Ops:
  0.6 7.2 %block_max.1 = (bf16[128,128]{1,0:T(8,128)(2,1)}, bf16[128,128]{1,0:T(8,128)(2,1)}, bf16[256,8192]{1,0:T(8,128)(2,1)}) custom-call(s32[1]{0:T(128)} %bitcast.3.core_ref, bf16[1,256,16384]{2,1,0:T(8,128)(2,1)} %x_ref.3), custom_call_target="tpu_custom_call" | custom-call | tf_op jit(solution)/shard_map/block_max/pallas_call | solution.py:98
  7.8 1.5 collective-permute-start.1
  9.3 1.1 collective-permute-done.1
  10.8 0.8 max.3
  11.6 10.6 %all_to_all.30 = bf16[8,128,128]{2,1,0:T(8,128)(2,1)S(1)} all-to-all(bf16[8,128,128]{2,1,0:T(8,128)(2,1)S(1)} %broadcast_in_dim.66), channel_id=1, replica_groups={{0,2,8,10,32,34,40,42},{4,6,12,14,36,38,44,46},{16,18,24,26,48,50,56,58..., dimensions={0} | all-to-all | bytes 524288 | tf_op jit(solution)/shard_map/all_to_all | solution.py:46
  22.2 0.7 broadcast_in_dim.67
  22.9 7.7 %all-to-all-start.1 = ((bf16[8,128,128]{2,1,0:T(8,128)(2,1)}), bf16[8,128,128]{2,1,0:T(8,128)(2,1)S(1)}, u32[]{:S(2)}, u32[]{:S(2)}) async-start(bf16[8,128,128]{2,1,0:T(8,128)(2,1)} %broadcast_in_dim.67), calls=%async_computation.1 | async-start | bytes 524288 | tf_op jit(solution)/shard_map/all_to_all | solution.py:46
  30.6 0.6 stack.58.at_ref
  31.3 8.5 %all-to-all-done.1.amax_ref = bf16[8,128,128]{2,1,0:T(8,128)(2,1)S(1)} async-done(((bf16[8,128,128]{2,1,0:T(8,128)(2,1)}), bf16[8,128,128]{2,1,0:T(8,128)(2,1)S(1)}, u32[]{:S(2)}, u32[]{:S(2)}) %all-to-all-start.1) | async-done | bytes 262176 | tf_op jit(solution)/shard_map/all_to_all | solution.py:46
  39.7 0.7 copy-done
  40.4 7.1 %quantise.1 = bf16[2,2,2,2,2,8,8192]{6,5,4,3,2,1,0:T(8,128)(2,1)} custom-call(s32[5]{0:T(128)} %stack.58.at_ref, bf16[1,256,16384]{2,1,0:T(8,128)(2,1)} %x_ref.3, bf16[256,8192]{1,0:T(8,128)(2,1)} %collective-permute-done.2.other_ref, bf16[8,128,128]{2,1,0:T(8,128)(2,1)} %copy-done), custom_call_target="tpu_custom_call" | custom-call | tf_op jit(solution)/shard_map/quantise/pallas_call | solution.py:185
  47.5 4.7 %all-to-all-start.2 = ((bf16[8,32,8192]{2,1,0:T(8,128)(2,1)}), bf16[8,32,8192]{2,1,0:T(8,128)(2,1)}, u32[]{:S(2)}, u32[]{:S(2)}) async-start(bf16[8,32,8192]{2,1,0:T(8,128)(2,1)} %bitcast.64), calls=%async_computation.2 | async-start | bytes 8388608 | tf_op jit(solution)/shard_map/all_to_all | solution.py:46
  52.5 2.5 %collective-permute-start = (f32[3,2,8192]{2,1,0:T(2,128)S(1)}, f32[3,2,8192]{2,1,0:T(2,128)S(1)}, u32[]{:S(2)}, u32[]{:S(2)}) collective-permute-start(f32[3,2,8192]{2,1,0:T(2,128)S(1)} %get-tuple-element.30), channel_id=1, source_target_pairs={{0,1},{1,0},{2,3},{3,2},{4,5},{5,4},{6,7},{7,6},{8,9},{9,8},{10,11... | collective-permute-start | bytes 589832 | tf_op jit(solution)/shard_map/ppermute | solution.py:271
  55.0 1.1 collective-permute-done
  56.3 24.4 %all-to-all-done.2 = bf16[8,32,8192]{2,1,0:T(8,128)(2,1)} async-done(((bf16[8,32,8192]{2,1,0:T(8,128)(2,1)}), bf16[8,32,8192]{2,1,0:T(8,128)(2,1)}, u32[]{:S(2)}, u32[]{:S(2)}) %all-to-all-start.2) | async-done | bytes 4194336 | tf_op jit(solution)/shard_map/all_to_all | solution.py:46
  80.7 2.9 %convert_reduce_fusion = f32[32,8192]{1,0:T(8,128)S(1)} fusion(bf16[8,32,8192]{2,1,0:T(8,128)(2,1)} %all-to-all-done.2), kind=kLoop, calls=%fused_computation | loop fusion | flops 3932160 | bytes 5242880 | tf_op jit(solution)/shard_map/reduce_sum | solution.py:280
  83.7 1.0 convert_element_type.30
  84.7 3.5 %all-to-all-start.3 = ((f16[8,4,8192]{2,1,0:T(4,128)(2,1)}), f16[8,4,8192]{2,1,0:T(4,128)(2,1)S(1)}, u32[]{:S(2)}, u32[]{:S(2)}) async-start(f16[8,4,8192]{2,1,0:T(4,128)(2,1)} %convert_element_type.30), calls=%async_computation.3 | async-start | bytes 1048576 | tf_op jit(solution)/shard_map/all_to_all | solution.py:46
  88.3 0.8 dynamic-slice_reduce_fusion
  89.3 5.4 %all-to-all-done.3 = f16[8,4,8192]{2,1,0:T(4,128)(2,1)S(1)} async-done(((f16[8,4,8192]{2,1,0:T(4,128)(2,1)}), f16[8,4,8192]{2,1,0:T(4,128)(2,1)S(1)}, u32[]{:S(2)}, u32[]{:S(2)}) %all-to-all-start.3) | async-done | bytes 524320 | tf_op jit(solution)/shard_map/all_to_all | solution.py:46
  94.7 0.6 convert_reduce_fusion.1
  96.2 9.3 %all_to_all.31 = bf16[8,4,8192]{2,1,0:T(4,128)(2,1)S(1)} all-to-all(bf16[8,4,8192]{2,1,0:T(4,128)(2,1)S(1)} %broadcast_in_dim.70), channel_id=1, replica_groups={{0,6,24,30,96,102,120,126},{2,4,26,28,98,100,122,124},{8,14,16,22,104,1..., dimensions={0} | all-to-all | bytes 1048576 | tf_op jit(solution)/shard_map/all_to_all | solution.py:46
  105.6 2.5 %broadcast_in_dim.72 = bf16[8,32,8192]{2,1,0:T(8,128)(2,1)} broadcast(bf16[32,8192]{1,0:T(8,128)(2,1)S(1)} %broadcast_in_dim.71), dimensions={1,2} | broadcast | bytes 4718592 | tf_op jit(solution)/shard_map/broadcast_in_dim | solution.py:50
  108.1 5.9 %all-to-all-start.5 = ((bf16[8,32,8192]{2,1,0:T(8,128)(2,1)}), bf16[8,32,8192]{2,1,0:T(8,128)(2,1)}, u32[]{:S(2)}, u32[]{:S(2)}) async-start(bf16[8,32,8192]{2,1,0:T(8,128)(2,1)} %broadcast_in_dim.72), calls=%async_computation.5 | async-start | bytes 8388608 | tf_op jit(solution)/shard_map/all_to_all | solution.py:46
  114.3 9.3 %collective-permute-start.3 = (f32[4,2,8192]{2,1,0:T(2,128)S(1)}, f32[4,2,8192]{2,1,0:T(2,128)S(1)}, u32[]{:S(2)}, u32[]{:S(2)}) collective-permute-start(f32[4,2,8192]{2,1,0:T(2,128)S(1)} %get-tuple-element.25), channel_id=1, source_target_pairs={{0,1},{1,0},{2,3},{3,2},{4,5},{5,4},{6,7},{7,6},{8,9},{9,8},{10,11... | collective-permute-start | bytes 786440 | tf_op jit(solution)/shard_map/ppermute | solution.py:300
  123.5 0.7 stack.64.at_ref
  124.2 18.3 %all-to-all-done.5 = bf16[8,32,8192]{2,1,0:T(8,128)(2,1)} async-done(((bf16[8,32,8192]{2,1,0:T(8,128)(2,1)}), bf16[8,32,8192]{2,1,0:T(8,128)(2,1)}, u32[]{:S(2)}, u32[]{:S(2)}) %all-to-all-start.5) | async-done | bytes 4194336 | tf_op jit(solution)/shard_map/all_to_all | solution.py:46
  142.5 7.8 %collective-permute-start.4 = (bf16[8,32,8192]{2,1,0:T(8,128)(2,1)}, bf16[8,32,8192]{2,1,0:T(8,128)(2,1)}, u32[]{:S(2)}, u32[]{:S(2)}) collective-permute-start(bf16[8,32,8192]{2,1,0:T(8,128)(2,1)} %all-to-all-done.5), channel_id=1, source_target_pairs={{0,1},{1,0},{2,3},{3,2},{4,5},{5,4},{6,7},{7,6},{8,9},{9,8},{10,11... | collective-permute-start | bytes 12582920 | tf_op jit(solution)/shard_map/ppermute | solution.py:309
  150.8 0.8 slice_bitcast_fusion
  151.6 4.5 %place_rows.2.refs_0_ = bf16[256,16384]{1,0:T(8,128)(2,1)} custom-call(s32[5]{0:T(128)} %stack.58.at_ref, bf16[2,2,2,2,2,8,8192]{6,5,4,3,2,1,0:T(8,128)(2,1)} %bitcast.19.w_ref), custom_call_target="tpu_custom_call" | custom-call | tf_op jit(solution)/shard_map/place_rows/pallas_call | solution.py:235
  156.1 1.4 collective-permute-done.4
  157.5 4.5 %place_rows.3 = bf16[256,16384]{1,0:T(8,128)(2,1)} custom-call(s32[5]{0:T(128)} %stack.64.at_ref, bf16[2,2,2,2,2,8,8192]{6,5,4,3,2,1,0:T(8,128)(2,1)} %bitcast.18.w_ref, bf16[256,16384]{1,0:T(8,128)(2,1)} %place_rows.2.refs_0_), custom_call_target="tpu_custom_call", output_to_operand_aliasing={{}: (2, {})} | custom-call | tf_op jit(solution)/shard_map/place_rows/pallas_call | solution.py:235
  (30 shorter events, 2.9 us)
Async XLA Ops:
  7.8 2.6 %collective-permute-start.1 = (bf16[128,128]{1,0:T(8,128)(2,1)}, bf16[128,128]{1,0:T(8,128)(2,1)S(1)}, u32[]{:S(2)}, u32[]{:S(2)}) collective-permute-start(bf16[128,128]{1,0:T(8,128)(2,1)} %get-tuple-element.11), channel_id=1, source_target_pairs={{0,1},{1,0},{2,3},{3,2},{4,5},{5,4},{6,7},{7,6},{8,9},{9,8},{10,11... | collective-permute-start | bytes 98312 | tf_op jit(solution)/shard_map/ppermute | solution.py:262
  10.4 29.3 %collective-permute-start.2 = (bf16[256,8192]{1,0:T(8,128)(2,1)}, bf16[256,8192]{1,0:T(8,128)(2,1)}, u32[]{:S(2)}, u32[]{:S(2)}) collective-permute-start(bf16[256,8192]{1,0:T(8,128)(2,1)} %get-tuple-element.12), channel_id=1, source_target_pairs={{0,1},{1,0},{2,3},{3,2},{4,5},{5,4},{6,7},{7,6},{8,9},{9,8},{10,11... | collective-permute-start | bytes 12582920 | tf_op jit(solution)/shard_map/ppermute | solution.py:264
  22.9 16.8 %all-to-all-start.1 = ((bf16[8,128,128]{2,1,0:T(8,128)(2,1)}), bf16[8,128,128]{2,1,0:T(8,128)(2,1)S(1)}, u32[]{:S(2)}, u32[]{:S(2)}) async-start(bf16[8,128,128]{2,1,0:T(8,128)(2,1)} %broadcast_in_dim.67), calls=%async_computation.1 | async-start | bytes 524288 | tf_op jit(solution)/shard_map/all_to_all | solution.py:46
  39.7 0.7 copy-start
  47.5 4.8 %copy-start.1 = (f32[2,16384]{1,0:T(2,128)S(1)}, f32[2,16384]{1,0:T(2,128)}, u32[]{:S(2)}) copy-start(f32[2,16384]{1,0:T(2,128)} %param.7) | copy-start | bytes 393220
  47.5 4.7 %copy-start.2 = (f32[2,16384]{1,0:T(2,128)S(1)}, f32[2,16384]{1,0:T(2,128)}, u32[]{:S(2)}) copy-start(f32[2,16384]{1,0:T(2,128)} %param.6) | copy-start | bytes 393220
  47.5 4.7 %copy-start.3 = (f32[2,16384]{1,0:T(2,128)S(1)}, f32[2,16384]{1,0:T(2,128)}, u32[]{:S(2)}) copy-start(f32[2,16384]{1,0:T(2,128)} %param.5) | copy-start | bytes 393220
  47.5 33.2 %all-to-all-start.2 = ((bf16[8,32,8192]{2,1,0:T(8,128)(2,1)}), bf16[8,32,8192]{2,1,0:T(8,128)(2,1)}, u32[]{:S(2)}, u32[]{:S(2)}) async-start(bf16[8,32,8192]{2,1,0:T(8,128)(2,1)} %bitcast.64), calls=%async_computation.2 | async-start | bytes 8388608 | tf_op jit(solution)/shard_map/all_to_all | solution.py:46
  52.5 3.5 %collective-permute-start = (f32[3,2,8192]{2,1,0:T(2,128)S(1)}, f32[3,2,8192]{2,1,0:T(2,128)S(1)}, u32[]{:S(2)}, u32[]{:S(2)}) collective-permute-start(f32[3,2,8192]{2,1,0:T(2,128)S(1)} %get-tuple-element.30), channel_id=1, source_target_pairs={{0,1},{1,0},{2,3},{3,2},{4,5},{5,4},{6,7},{7,6},{8,9},{9,8},{10,11... | collective-permute-start | bytes 589832 | tf_op jit(solution)/shard_map/ppermute | solution.py:271
  84.7 10.0 %all-to-all-start.3 = ((f16[8,4,8192]{2,1,0:T(4,128)(2,1)}), f16[8,4,8192]{2,1,0:T(4,128)(2,1)S(1)}, u32[]{:S(2)}, u32[]{:S(2)}) async-start(f16[8,4,8192]{2,1,0:T(4,128)(2,1)} %convert_element_type.30), calls=%async_computation.3 | async-start | bytes 1048576 | tf_op jit(solution)/shard_map/all_to_all | solution.py:46
  108.1 34.5 %all-to-all-start.5 = ((bf16[8,32,8192]{2,1,0:T(8,128)(2,1)}), bf16[8,32,8192]{2,1,0:T(8,128)(2,1)}, u32[]{:S(2)}, u32[]{:S(2)}) async-start(bf16[8,32,8192]{2,1,0:T(8,128)(2,1)} %broadcast_in_dim.72), calls=%async_computation.5 | async-start | bytes 8388608 | tf_op jit(solution)/shard_map/all_to_all | solution.py:46
  114.3 36.1 %collective-permute-start.3 = (f32[4,2,8192]{2,1,0:T(2,128)S(1)}, f32[4,2,8192]{2,1,0:T(2,128)S(1)}, u32[]{:S(2)}, u32[]{:S(2)}) collective-permute-start(f32[4,2,8192]{2,1,0:T(2,128)S(1)} %get-tuple-element.25), channel_id=1, source_target_pairs={{0,1},{1,0},{2,3},{3,2},{4,5},{5,4},{6,7},{7,6},{8,9},{9,8},{10,11... | collective-permute-start | bytes 786440 | tf_op jit(solution)/shard_map/ppermute | solution.py:300
  142.5 15.0 %collective-permute-start.4 = (bf16[8,32,8192]{2,1,0:T(8,128)(2,1)}, bf16[8,32,8192]{2,1,0:T(8,128)(2,1)}, u32[]{:S(2)}, u32[]{:S(2)}) collective-permute-start(bf16[8,32,8192]{2,1,0:T(8,128)(2,1)} %all-to-all-done.5), channel_id=1, source_target_pairs={{0,1},{1,0},{2,3},{3,2},{4,5},{5,4},{6,7},{7,6},{8,9},{9,8},{10,11... | collective-permute-start | bytes 12582920 | tf_op jit(solution)/shard_map/ppermute | solution.py:309

commit v6 on v5

--- a/solution.py
+++ b/solution.py
@@ -20,7 +20,7 @@
 NEAR = {0: ((0, 1), (3, 2)), 1: ((1, 2), (0, 3))}
 FAR = {0: ((0, 3), (1, 2)), 1: ((0, 1), (2, 3))}
 PLACE = {0: (0, 2, 3, 1), 1: (0, 1, 2, 3)}
-CUBES = ({0: FAR[1], 1: FAR[1]}, {0: NEAR[1], 1: NEAR[1]})
+ORDER = {0: (0, 3, 1, 2), 1: (0, 1, 2, 3)}
 
 
 def device(x, z, y, core):
@@ -39,6 +39,8 @@
 
 NEAR_GROUPS = groups(NEAR)
 FAR_GROUPS = groups(FAR)
+Y_CORES = [[device(x, z, y, core) for core in (0, 1) for y in range(4)] for x in range(4) for z in range(4)]
+X_Z = [[device(x, z, y, core) for x in range(4) for z in range(4)] for y in range(4) for core in (0, 1)]
 SWAP = [(d, d ^ 1) for d in range(N_DP)]
 
 
@@ -50,7 +52,7 @@
     return exchange(jnp.broadcast_to(x[None], (len(among[0]), *x.shape)), among)
 
 
-def max_kernel(core_ref, x_ref, amax_ref, other_ref, send_ref, buf, own_max, other_max, in_sem, out_sem):
+def max_kernel(core_ref, x_ref, amax_ref, send_ref, buf, left, right, in_sem, out_sem):
     core = core_ref[0]
     rows = ROWS // in_sem.shape[0]
     theirs = pl.ds(pl.multiple_of((1 - core) * HALF, HALF), HALF)
@@ -75,15 +77,14 @@
             v = jnp.abs(buf[at, b * BLOCK : (b + 1) * BLOCK].astype(F32))
             acc = jnp.where(lane == b, jnp.max(v, axis=1, keepdims=True), acc)
         rolled = pltpu.roll(acc, NB, 1)
-        mine, rest = jnp.where(core == 0, acc, rolled), jnp.where(core == 0, rolled, acc)
         to = pl.ds(i * rows % 128, rows)
         if i * rows < 128:
-            own_max[to, :], other_max[to, :] = mine, rest
+            left[to, :], right[to, :] = acc, rolled
         else:
-            own_max[to, :] = jnp.where(low, own_max[to, :], rest)
-            other_max[to, :] = jnp.where(low, other_max[to, :], mine)
-    amax_ref[...] = own_max[...].astype(BF16)
-    other_ref[...] = other_max[...].astype(BF16)
+            left[to, :] = jnp.where(low, left[to, :], rolled)
+            right[to, :] = jnp.where(low, right[to, :], acc)
+    amax_ref[0] = left[...].astype(BF16)
+    amax_ref[1] = right[...].astype(BF16)
     for store in stores:
         store.wait()
 
@@ -98,12 +99,11 @@
     return pl.pallas_call(
         max_kernel,
         out_shape=(
-            jax.ShapeDtypeStruct((128, 128), BF16),
-            jax.ShapeDtypeStruct((128, 128), BF16),
+            jax.ShapeDtypeStruct((2, 128, 128), BF16),
             jax.ShapeDtypeStruct((ROWS, HALF), BF16),
         ),
         in_specs=[SMEM, HBM],
-        out_specs=[VMEM, VMEM, HBM],
+        out_specs=[VMEM, HBM],
         scratch_shapes=[
             pltpu.VMEM((ROWS, W), BF16),
             pltpu.VMEM((128, 128), F32),
@@ -159,7 +159,7 @@
     for i in range(chunks):
         at = pl.ds(i * rows, rows)
         low = i * rows % 128
-        mult = mult_of(jnp.max(amax_ref[:, low : low + rows, :].astype(F32), axis=0))
+        mult = mult_of(amax_ref[low : low + rows, :].astype(F32))
         for load in loads[i]:
             load.wait()
         for b in range(NB):
@@ -203,34 +203,33 @@
 
 def rows_kernel(at_ref, w_ref, *refs):
     out_ref, got, full, in_sem, out_sem = refs[-5:]
-    chunks = out_sem.shape[0]
-    rows = ROWS // chunks
     half = pl.ds(pl.multiple_of(at_ref[0] * HALF, HALF), HALF)
+    keep, turn = tile_mask(at_ref)
+    chunks = [(i >> 2, i >> 1 & 1, i & 1) for i in range(8)]
     loads, stores = [], []
-    for t in range(ROWS // 8):
-        source = w_ref.at[block_of(at_ref, t // 8, t // 2 % 4, t % 2)]
-        loads.append(pltpu.make_async_copy(source, got.at[t], in_sem.at[t]))
-        loads[t].start()
-    for i in range(chunks):
-        at = pl.ds(i * rows, rows)
-        stores.append(pltpu.make_async_copy(full.at[at], out_ref.at[at, half], out_sem.at[i]))
-    keep, turn = tile_mask(at_ref)
-    for i in range(chunks):
-        for t in range(i * rows // 8, (i + 1) * rows // 8, 2):
-            loads[t].wait()
-            loads[t + 1].wait()
+    for i, (jx, jz, ox) in enumerate(chunks):
+        source, target = w_ref.at[jx, jz, :, ox], got.at[i]
+        loads.append(pltpu.make_async_copy(source, target, in_sem.at[i]))
+        loads[i].start()
+    for i, (jx, jz, ox) in enumerate(chunks):
+        loads[i].wait()
+        for oz in (0, 1):
+            n = 2 * i + oz
             for b in range(NB):
                 cols = slice(b * BLOCK, (b + 1) * BLOCK)
-                p = got[t, :, cols].astype(F32)
-                q = pltpu.roll(got[t + 1, :, cols].astype(F32), turn, 0)
-                full[t * 8 : t * 8 + 8, cols] = jnp.where(keep, p, q).astype(BF16)
-                full[t * 8 + 8 : t * 8 + 16, cols] = jnp.where(keep, q, p).astype(BF16)
-        stores[i].start()
+                p = got[i, 0, oz, :, cols].astype(F32)
+                q = pltpu.roll(got[i, 1, oz, :, cols].astype(F32), turn, 0)
+                full[n, :8, cols] = jnp.where(keep, p, q).astype(BF16)
+                full[n, 8:, cols] = jnp.where(keep, q, p).astype(BF16)
+            x, z = at_ref[5 + 2 * jx + ox], at_ref[5 + 2 * jz + oz]
+            at = pl.ds(pl.multiple_of(x * 64 + z * 16, 16), 16)
+            stores.append(pltpu.make_async_copy(full.at[n], out_ref.at[at, half], out_sem.at[n]))
+            stores[n].start()
     for store in stores:
         store.wait()
 
 
-def place_rows(at, w, before=None, chunks=8):
+def place_rows(at, w, before=None):
     more = () if before is None else (before,)
     return pl.pallas_call(
         rows_kernel,
@@ -238,10 +237,10 @@
         in_specs=[SMEM, HBM, *(HBM for _ in more)],
         out_specs=HBM,
         scratch_shapes=[
-            pltpu.VMEM((ROWS // 8, 8, HALF), BF16),
-            pltpu.VMEM((ROWS, HALF), BF16),
-            pltpu.SemaphoreType.DMA((ROWS // 8,)),
-            pltpu.SemaphoreType.DMA((chunks,)),
+            pltpu.VMEM((8, 2, 2, 8, HALF), BF16),
+            pltpu.VMEM((16, 16, HALF), BF16),
+            pltpu.SemaphoreType.DMA((8,)),
+            pltpu.SemaphoreType.DMA((16,)),
         ],
         input_output_aliases={2: 0} if more else {},
         compiler_params=PARAMS,
@@ -254,16 +253,14 @@
     core, chip = d & 1, d >> 1
     first = core == 0
     row = chip * 4
-    places = [jnp.where(first, PLACE[0][i], PLACE[1][i]) for i in range(4)]
-    others = [jnp.where(first, PLACE[1][i], PLACE[0][i]) for i in range(4)]
-    mine, theirs = jnp.stack([core, *places]), jnp.stack([1 - core, *others])
-
-    amax, amax_send, send = block_max(core.reshape(1), partials)
-    amax_other = lax.ppermute(amax_send, "dp", SWAP)
-    send, amax_other = lax.optimization_barrier((send, amax_other))
+    tables = [[c, *(jnp.where(c == 0, t[0][i], t[1][i]) for t in (PLACE, ORDER) for i in range(4))] for c in (core, 1 - core)]
+    mine, theirs = (jnp.stack(table) for table in tables)
+
+    amax, send = block_max(core.reshape(1), partials)
     other = lax.ppermute(send, "dp", SWAP)
-    amax = jnp.max(spread(jnp.maximum(amax, amax_other), groups(CUBES[0])), axis=0)
-    amax = spread(amax, groups(CUBES[1]))
+    amax = jnp.broadcast_to(amax[:, None], (2, 4, 128, 128)).reshape(8, 128, 128)
+    amax = jnp.max(exchange(amax, Y_CORES), axis=0)
+    amax = jnp.max(spread(amax, X_Z), axis=0)
 
     state = jnp.stack([master, moment_one, moment_two])
     state_own = lax.dynamic_slice_in_dim(state, core * HALF, HALF, 2)
@@ -280,8 +277,8 @@
     mant = jnp.sum(mant.astype(F32), axis=0).astype(F16).reshape(8, 4, HALF)
     total = jnp.sum(exchange(mant, FAR_GROUPS).astype(F32), axis=0)
 
-    own_amax = lax.dynamic_slice(amax, (0, row & 127, (row >> 7) * NB), (8, 4, NB))
-    scale = scale_of(jnp.max(own_amax.astype(F32), axis=0))
+    own_amax = lax.dynamic_slice(amax, (row & 127, (row >> 7) * NB), (4, NB))
+    scale = scale_of(own_amax.astype(F32))
     factor = scale / (2.0**MBITS * N_DP)
     reduced_grad = (total.reshape(4, NB, BLOCK) * factor[:, :, None]).reshape(4, HALF)
     moment_one_new = 0.9 * moment_one + 0.1 * reduced_grad

time: 165 us -> 164 us (level)
    all_to_all x4, waiting for transfers between devices: 56.6 us -> 59.2 us  [exchange(): return lax.all_to_all(x, 'dp', 0, 0, axis_index_groups=among)]
    broadcast_in_dim x5 -> x4, local copies, waits for them, and re-layouts: 3.52 us -> 3.65 us  [spread(): return exchange(jnp.broadcast_to(x[None], (len(among[0]), *x.shape)), among)]
  transfers between devices with their start and end apart: 9 -> 8, of which waited for: 7 -> 5; matrix products, arithmetic and copies ran while one was open for 4% -> 7% of each run, Pallas kernels for 3% -> 3%
where the time goes in v6:
time: 164 us; the launch traced here: 162 us
  waiting for transfers between devices  60.9 us (37%)
  starting transfers between devices  42.4 us (26%)
  Pallas kernels  22.5 us (14%)
  blocking collectives  20.3 us (12%)
  local copies, waits for them, and re-layouts  7.96 us (5%)
  other arithmetic  6.91 us (4%)
    all_to_all x4, waiting for transfers between devices, exchange(): return lax.all_to_all(x, 'dp', 0, 0, axis_index_groups=among)  59.2 us
    all_to_all x4, starting transfers between devices, exchange(): return lax.all_to_all(x, 'dp', 0, 0, axis_index_groups=among)  21.8 us
    all_to_all x2, blocking collectives, exchange(): return lax.all_to_all(x, 'dp', 0, 0, axis_index_groups=among)  20.3 us
    ppermute x1, starting transfers between devices, per_device(): lax.ppermute(jnp.where(first, out[:, 2:], out[:, :2]), 'dp', SWAP)  9.17 us
    pallas_call x2, Pallas kernels, place_rows(): pl.pallas_call(rows_kernel, out_shape=jax.ShapeDtypeStruct((ROWS, W), BF1...  8.45 us
    ppermute x1, starting transfers between devices, per_device(): weights_other = lax.ppermute(weights, 'dp', SWAP)  7.72 us
    pallas_call x1, Pallas kernels, block_max(): pl.pallas_call(max_kernel, out_shape=(jax.ShapeDtypeStruct((2, 128, 128),...  7.2 us
    pallas_call x1, Pallas kernels, quantise(): pl.pallas_call(quant_kernel, out_shape=jax.ShapeDtypeStruct((2, 2, 2, 2,...  6.86 us
  transfers between devices with their start and end apart: 8, of which 5 were waited for; matrix products, arithmetic and copies ran while one was open for 7% of the time, Pallas kernels for 3%

profile of v6, /device:TPU:1, one launch (start us, length us, event | category | flops | bytes accessed | tf_op | source)
XLA Modules:
  0.0 162.0 jit_solution(8227892865591446247)
XLA Ops:
  0.6 7.2 %block_max.1 = (bf16[2,128,128]{2,1,0:T(8,128)(2,1)}, bf16[256,8192]{1,0:T(8,128)(2,1)}) custom-call(s32[1]{0:T(128)} %bitcast.3.core_ref, bf16[1,256,16384]{2,1,0:T(8,128)(2,1)} %x_ref.3), custom_call_target="tpu_custom_call" | custom-call | tf_op jit(solution)/shard_map/block_max/pallas_call | solution.py:99
  7.8 1.5 collective-permute-start.1
  9.3 0.9 broadcast_in_dim.66
  10.2 11.0 %all_to_all.30 = bf16[8,128,128]{2,1,0:T(8,128)(2,1)S(1)} all-to-all(bf16[8,128,128]{2,1,0:T(8,128)(2,1)S(1)} %bitcast.73), channel_id=1, replica_groups={{0,2,4,6,1,3,5,7},{8,10,12,14,9,11,13,15},{16,18,20,22,17,19,21,23},{24..., dimensions={0} | all-to-all | bytes 524288 | tf_op jit(solution)/shard_map/all_to_all | solution.py:48
  21.3 0.9 broadcast_in_dim.67
  22.2 7.6 %all-to-all-start.1 = ((bf16[16,128,128]{2,1,0:T(8,128)(2,1)}), bf16[16,128,128]{2,1,0:T(8,128)(2,1)S(1)}, u32[]{:S(2)}, u32[]{:S(2)}) async-start(bf16[16,128,128]{2,1,0:T(8,128)(2,1)} %broadcast_in_dim.67), calls=%async_computation.1 | async-start | bytes 1048576 | tf_op jit(solution)/shard_map/all_to_all | solution.py:48
  29.8 0.6 stack.81.at_ref
  30.4 9.7 %all-to-all-done.1 = bf16[16,128,128]{2,1,0:T(8,128)(2,1)S(1)} async-done(((bf16[16,128,128]{2,1,0:T(8,128)(2,1)}), bf16[16,128,128]{2,1,0:T(8,128)(2,1)S(1)}, u32[]{:S(2)}, u32[]{:S(2)}) %all-to-all-start.1) | async-done | bytes 524320 | tf_op jit(solution)/shard_map/all_to_all | solution.py:48
  40.2 0.7 reduce_max.28.amax_ref
  40.9 6.9 %quantise.1 = bf16[2,2,2,2,2,8,8192]{6,5,4,3,2,1,0:T(8,128)(2,1)} custom-call(s32[9]{0:T(128)} %stack.81.at_ref, bf16[1,256,16384]{2,1,0:T(8,128)(2,1)} %x_ref.3, bf16[256,8192]{1,0:T(8,128)(2,1)} %collective-permute-done.1.other_ref, bf16[128,128]{1,0:T(8,128)(2,1)} %reduce_max.28.amax_ref), custom_call_target="tpu_custom_call" | custom-call | tf_op jit(solution)/shard_map/quantise/pallas_call | solution.py:185
  47.8 4.7 %all-to-all-start.2 = ((bf16[8,32,8192]{2,1,0:T(8,128)(2,1)}), bf16[8,32,8192]{2,1,0:T(8,128)(2,1)}, u32[]{:S(2)}, u32[]{:S(2)}) async-start(bf16[8,32,8192]{2,1,0:T(8,128)(2,1)} %bitcast.71), calls=%async_computation.2 | async-start | bytes 8388608 | tf_op jit(solution)/shard_map/all_to_all | solution.py:48
  52.7 2.2 %collective-permute-start = (f32[3,2,8192]{2,1,0:T(2,128)S(1)}, f32[3,2,8192]{2,1,0:T(2,128)S(1)}, u32[]{:S(2)}, u32[]{:S(2)}) collective-permute-start(f32[3,2,8192]{2,1,0:T(2,128)S(1)} %get-tuple-element.24), channel_id=1, source_target_pairs={{0,1},{1,0},{2,3},{3,2},{4,5},{5,4},{6,7},{7,6},{8,9},{9,8},{10,11... | collective-permute-start | bytes 589832 | tf_op jit(solution)/shard_map/ppermute | solution.py:268
  54.9 26.1 %all-to-all-done.2 = bf16[8,32,8192]{2,1,0:T(8,128)(2,1)} async-done(((bf16[8,32,8192]{2,1,0:T(8,128)(2,1)}), bf16[8,32,8192]{2,1,0:T(8,128)(2,1)}, u32[]{:S(2)}, u32[]{:S(2)}) %all-to-all-start.2) | async-done | bytes 4194336 | tf_op jit(solution)/shard_map/all_to_all | solution.py:48
  81.0 2.9 %convert_reduce_fusion = f32[32,8192]{1,0:T(8,128)S(1)} fusion(bf16[8,32,8192]{2,1,0:T(8,128)(2,1)} %all-to-all-done.2), kind=kLoop, calls=%fused_computation | loop fusion | flops 3932160 | bytes 5242880 | tf_op jit(solution)/shard_map/reduce_sum | solution.py:277
  83.9 1.0 convert_element_type.32
  84.9 3.7 %all-to-all-start.3 = ((f16[8,4,8192]{2,1,0:T(4,128)(2,1)}), f16[8,4,8192]{2,1,0:T(4,128)(2,1)S(1)}, u32[]{:S(2)}, u32[]{:S(2)}) async-start(f16[8,4,8192]{2,1,0:T(4,128)(2,1)} %convert_element_type.32), calls=%async_computation.3 | async-start | bytes 1048576 | tf_op jit(solution)/shard_map/all_to_all | solution.py:48
  88.6 0.3 maximum_select_fusion.1
  89.0 0.8 select_multiply_fusion
  89.9 5.0 %all-to-all-done.3 = f16[8,4,8192]{2,1,0:T(4,128)(2,1)S(1)} async-done(((f16[8,4,8192]{2,1,0:T(4,128)(2,1)}), f16[8,4,8192]{2,1,0:T(4,128)(2,1)S(1)}, u32[]{:S(2)}, u32[]{:S(2)}) %all-to-all-start.3) | async-done | bytes 524320 | tf_op jit(solution)/shard_map/all_to_all | solution.py:48
  94.9 0.6 convert_reduce_fusion.1
  96.4 9.3 %all_to_all.31 = bf16[8,4,8192]{2,1,0:T(4,128)(2,1)S(1)} all-to-all(bf16[8,4,8192]{2,1,0:T(4,128)(2,1)S(1)} %broadcast_in_dim.70), channel_id=1, replica_groups={{0,6,24,30,96,102,120,126},{2,4,26,28,98,100,122,124},{8,14,16,22,104,1..., dimensions={0} | all-to-all | bytes 1048576 | tf_op jit(solution)/shard_map/all_to_all | solution.py:48
  105.8 2.5 %broadcast_in_dim.72 = bf16[8,32,8192]{2,1,0:T(8,128)(2,1)} broadcast(bf16[32,8192]{1,0:T(8,128)(2,1)S(1)} %broadcast_in_dim.71), dimensions={1,2} | broadcast | bytes 4718592 | tf_op jit(solution)/shard_map/broadcast_in_dim | solution.py:52
  108.3 5.9 %all-to-all-start.5 = ((bf16[8,32,8192]{2,1,0:T(8,128)(2,1)}), bf16[8,32,8192]{2,1,0:T(8,128)(2,1)}, u32[]{:S(2)}, u32[]{:S(2)}) async-start(bf16[8,32,8192]{2,1,0:T(8,128)(2,1)} %broadcast_in_dim.72), calls=%async_computation.5 | async-start | bytes 8388608 | tf_op jit(solution)/shard_map/all_to_all | solution.py:48
  114.5 9.2 %collective-permute-start.2 = (f32[4,2,8192]{2,1,0:T(2,128)S(1)}, f32[4,2,8192]{2,1,0:T(2,128)S(1)}, u32[]{:S(2)}, u32[]{:S(2)}) collective-permute-start(f32[4,2,8192]{2,1,0:T(2,128)S(1)} %get-tuple-element.19), channel_id=1, source_target_pairs={{0,1},{1,0},{2,3},{3,2},{4,5},{5,4},{6,7},{7,6},{8,9},{9,8},{10,11... | collective-permute-start | bytes 786440 | tf_op jit(solution)/shard_map/ppermute | solution.py:297
  123.6 0.7 stack.90.at_ref
  124.3 18.4 %all-to-all-done.5 = bf16[8,32,8192]{2,1,0:T(8,128)(2,1)} async-done(((bf16[8,32,8192]{2,1,0:T(8,128)(2,1)}), bf16[8,32,8192]{2,1,0:T(8,128)(2,1)}, u32[]{:S(2)}, u32[]{:S(2)}) %all-to-all-start.5) | async-done | bytes 4194336 | tf_op jit(solution)/shard_map/all_to_all | solution.py:48
  142.8 7.7 %collective-permute-start.3 = (bf16[8,32,8192]{2,1,0:T(8,128)(2,1)}, bf16[8,32,8192]{2,1,0:T(8,128)(2,1)}, u32[]{:S(2)}, u32[]{:S(2)}) collective-permute-start(bf16[8,32,8192]{2,1,0:T(8,128)(2,1)} %all-to-all-done.5), channel_id=1, source_target_pairs={{0,1},{1,0},{2,3},{3,2},{4,5},{5,4},{6,7},{7,6},{8,9},{9,8},{10,11... | collective-permute-start | bytes 12582920 | tf_op jit(solution)/shard_map/ppermute | solution.py:306
  150.5 0.4 maximum_select_fusion
  150.9 0.8 slice_bitcast_fusion
  151.7 4.2 %place_rows.2.refs_0_ = bf16[256,16384]{1,0:T(8,128)(2,1)} custom-call(s32[9]{0:T(128)} %stack.81.at_ref, bf16[2,2,2,2,2,8,8192]{6,5,4,3,2,1,0:T(8,128)(2,1)} %bitcast.26.w_ref), custom_call_target="tpu_custom_call" | custom-call | tf_op jit(solution)/shard_map/place_rows/pallas_call | solution.py:234
  155.9 1.7 %collective-permute-done.3 = bf16[8,32,8192]{2,1,0:T(8,128)(2,1)} collective-permute-done((bf16[8,32,8192]{2,1,0:T(8,128)(2,1)}, bf16[8,32,8192]{2,1,0:T(8,128)(2,1)}, u32[]{:S(2)}, u32[]{:S(2)}) %collective-permute-start.3) | collective-permute-done | bytes 4194336 | tf_op jit(solution)/shard_map/ppermute | solution.py:306
  157.6 4.2 %place_rows.3 = bf16[256,16384]{1,0:T(8,128)(2,1)} custom-call(s32[9]{0:T(128)} %stack.90.at_ref, bf16[2,2,2,2,2,8,8192]{6,5,4,3,2,1,0:T(8,128)(2,1)} %bitcast.25.w_ref, bf16[256,16384]{1,0:T(8,128)(2,1)} %place_rows.2.refs_0_), custom_call_target="tpu_custom_call", output_to_operand_aliasing={{}: (2, {})} | custom-call | tf_op jit(solution)/shard_map/place_rows/pallas_call | solution.py:234
  (25 shorter events, 1.8 us)
Async XLA Ops:
  7.8 33.0 %collective-permute-start.1 = (bf16[256,8192]{1,0:T(8,128)(2,1)}, bf16[256,8192]{1,0:T(8,128)(2,1)}, u32[]{:S(2)}, u32[]{:S(2)}) collective-permute-start(bf16[256,8192]{1,0:T(8,128)(2,1)} %get-tuple-element.7), channel_id=1, source_target_pairs={{0,1},{1,0},{2,3},{3,2},{4,5},{5,4},{6,7},{7,6},{8,9},{9,8},{10,11... | collective-permute-start | bytes 12582920 | tf_op jit(solution)/shard_map/ppermute | solution.py:260
  22.2 18.0 %all-to-all-start.1 = ((bf16[16,128,128]{2,1,0:T(8,128)(2,1)}), bf16[16,128,128]{2,1,0:T(8,128)(2,1)S(1)}, u32[]{:S(2)}, u32[]{:S(2)}) async-start(bf16[16,128,128]{2,1,0:T(8,128)(2,1)} %broadcast_in_dim.67), calls=%async_computation.1 | async-start | bytes 1048576 | tf_op jit(solution)/shard_map/all_to_all | solution.py:48
  47.7 4.7 %copy-start = (f32[2,16384]{1,0:T(2,128)S(1)}, f32[2,16384]{1,0:T(2,128)}, u32[]{:S(2)}) copy-start(f32[2,16384]{1,0:T(2,128)} %param.7) | copy-start | bytes 393220
  47.7 4.7 %copy-start.1 = (f32[2,16384]{1,0:T(2,128)S(1)}, f32[2,16384]{1,0:T(2,128)}, u32[]{:S(2)}) copy-start(f32[2,16384]{1,0:T(2,128)} %param.6) | copy-start | bytes 393220
  47.7 4.7 %copy-start.2 = (f32[2,16384]{1,0:T(2,128)S(1)}, f32[2,16384]{1,0:T(2,128)}, u32[]{:S(2)}) copy-start(f32[2,16384]{1,0:T(2,128)} %param.5) | copy-start | bytes 393220
  47.8 33.2 %all-to-all-start.2 = ((bf16[8,32,8192]{2,1,0:T(8,128)(2,1)}), bf16[8,32,8192]{2,1,0:T(8,128)(2,1)}, u32[]{:S(2)}, u32[]{:S(2)}) async-start(bf16[8,32,8192]{2,1,0:T(8,128)(2,1)} %bitcast.71), calls=%async_computation.2 | async-start | bytes 8388608 | tf_op jit(solution)/shard_map/all_to_all | solution.py:48
  52.7 35.9 %collective-permute-start = (f32[3,2,8192]{2,1,0:T(2,128)S(1)}, f32[3,2,8192]{2,1,0:T(2,128)S(1)}, u32[]{:S(2)}, u32[]{:S(2)}) collective-permute-start(f32[3,2,8192]{2,1,0:T(2,128)S(1)} %get-tuple-element.24), channel_id=1, source_target_pairs={{0,1},{1,0},{2,3},{3,2},{4,5},{5,4},{6,7},{7,6},{8,9},{9,8},{10,11... | collective-permute-start | bytes 589832 | tf_op jit(solution)/shard_map/ppermute | solution.py:268
  84.9 10.0 %all-to-all-start.3 = ((f16[8,4,8192]{2,1,0:T(4,128)(2,1)}), f16[8,4,8192]{2,1,0:T(4,128)(2,1)S(1)}, u32[]{:S(2)}, u32[]{:S(2)}) async-start(f16[8,4,8192]{2,1,0:T(4,128)(2,1)} %convert_element_type.32), calls=%async_computation.3 | async-start | bytes 1048576 | tf_op jit(solution)/shard_map/all_to_all | solution.py:48
  108.3 34.5 %all-to-all-start.5 = ((bf16[8,32,8192]{2,1,0:T(8,128)(2,1)}), bf16[8,32,8192]{2,1,0:T(8,128)(2,1)}, u32[]{:S(2)}, u32[]{:S(2)}) async-start(bf16[8,32,8192]{2,1,0:T(8,128)(2,1)} %broadcast_in_dim.72), calls=%async_computation.5 | async-start | bytes 8388608 | tf_op jit(solution)/shard_map/all_to_all | solution.py:48
  114.5 36.0 %collective-permute-start.2 = (f32[4,2,8192]{2,1,0:T(2,128)S(1)}, f32[4,2,8192]{2,1,0:T(2,128)S(1)}, u32[]{:S(2)}, u32[]{:S(2)}) collective-permute-start(f32[4,2,8192]{2,1,0:T(2,128)S(1)} %get-tuple-element.19), channel_id=1, source_target_pairs={{0,1},{1,0},{2,3},{3,2},{4,5},{5,4},{6,7},{7,6},{8,9},{9,8},{10,11... | collective-permute-start | bytes 786440 | tf_op jit(solution)/shard_map/ppermute | solution.py:297
  142.8 14.8 %collective-permute-start.3 = (bf16[8,32,8192]{2,1,0:T(8,128)(2,1)}, bf16[8,32,8192]{2,1,0:T(8,128)(2,1)}, u32[]{:S(2)}, u32[]{:S(2)}) collective-permute-start(bf16[8,32,8192]{2,1,0:T(8,128)(2,1)} %all-to-all-done.5), channel_id=1, source_target_pairs={{0,1},{1,0},{2,3},{3,2},{4,5},{5,4},{6,7},{7,6},{8,9},{9,8},{10,11... | collective-permute-start | bytes 12582920 | tf_op jit(solution)/shard_map/ppermute | solution.py:306

commit v7 on v6

--- a/solution.py
+++ b/solution.py
@@ -20,7 +20,8 @@
 NEAR = {0: ((0, 1), (3, 2)), 1: ((1, 2), (0, 3))}
 FAR = {0: ((0, 3), (1, 2)), 1: ((0, 1), (2, 3))}
 PLACE = {0: (0, 2, 3, 1), 1: (0, 1, 2, 3)}
-ORDER = {0: (0, 3, 1, 2), 1: (0, 1, 2, 3)}
+BACK = {0: ((0, 3), (1, 2)), 1: ((0, 1), (3, 2))}
+ARRIVE = {0: (0, 1, 3, 2), 1: (0, 3, 1, 2)}
 
 
 def device(x, z, y, core):
@@ -39,6 +40,7 @@
 
 NEAR_GROUPS = groups(NEAR)
 FAR_GROUPS = groups(FAR)
+BACK_GROUPS = groups(BACK)
 Y_CORES = [[device(x, z, y, core) for core in (0, 1) for y in range(4)] for x in range(4) for z in range(4)]
 X_Z = [[device(x, z, y, core) for x in range(4) for z in range(4)] for y in range(4) for core in (0, 1)]
 SWAP = [(d, d ^ 1) for d in range(N_DP)]
@@ -83,8 +85,9 @@
         else:
             left[to, :] = jnp.where(low, left[to, :], rolled)
             right[to, :] = jnp.where(low, right[to, :], acc)
-    amax_ref[0] = left[...].astype(BF16)
-    amax_ref[1] = right[...].astype(BF16)
+    for j in range(4):
+        amax_ref[j] = left[...].astype(BF16)
+        amax_ref[4 + j] = right[...].astype(BF16)
     for store in stores:
         store.wait()
 
@@ -99,7 +102,7 @@
     return pl.pallas_call(
         max_kernel,
         out_shape=(
-            jax.ShapeDtypeStruct((2, 128, 128), BF16),
+            jax.ShapeDtypeStruct((8, 128, 128), BF16),
             jax.ShapeDtypeStruct((ROWS, HALF), BF16),
         ),
         in_specs=[SMEM, HBM],
@@ -130,20 +133,23 @@
     return mult
 
 
-def block_of(at_ref, x, z, y):
-    px, pz = at_ref[1 + x], at_ref[1 + z]
+def pick(core, table, i):
+    return jnp.where(core == 0, table[0][i], table[1][i])
+
+
+def block_of(core, x, z, y):
+    px, pz = pick(core, PLACE, x), pick(core, PLACE, z)
     return (px >> 1, pz >> 1, y, px & 1, pz & 1)
 
 
-def tile_mask(at_ref):
-    row = lax.broadcasted_iota(jnp.int32, (8, BLOCK), 0)
-    return row < 4 + 4 * at_ref[0], 4 * (1 - at_ref[0])
-
-
-def quant_kernel(at_ref, x_ref, other_ref, amax_ref, out_ref, own, other, mant, own_sem, other_sem, out_sem):
+def rows_below(limit):
+    return lax.broadcasted_iota(jnp.int32, (8, BLOCK), 0) < limit
+
+
+def quant_kernel(core_ref, x_ref, other_ref, amax_ref, out_ref, own, other, mant, own_sem, other_sem, out_sem):
     chunks = own_sem.shape[0]
     rows = ROWS // chunks
-    mine = pl.ds(pl.multiple_of(at_ref[0] * HALF, HALF), HALF)
+    mine = pl.ds(pl.multiple_of(core_ref[0] * HALF, HALF), HALF)
     loads, stores = [], []
     for i in range(chunks):
         at = pl.ds(i * rows, rows)
@@ -155,7 +161,7 @@
         )
         for load in loads[i]:
             load.start()
-    keep, turn = tile_mask(at_ref)
+    keep, turn = rows_below(4 + 4 * core_ref[0]), 4 * (1 - core_ref[0])
     for i in range(chunks):
         at = pl.ds(i * rows, rows)
         low = i * rows % 128
@@ -174,14 +180,14 @@
                 mant[tile, :, cols] = jnp.where(keep, p, q).astype(BF16)
                 mant[tile + 1, :, cols] = pltpu.roll(jnp.where(keep, q, p), turn, 0).astype(BF16)
         for t in range(i * rows // 8, (i + 1) * rows // 8):
-            target = out_ref.at[block_of(at_ref, t // 8, t // 2 % 4, t % 2)]
+            target = out_ref.at[block_of(core_ref[0], t // 8, t // 2 % 4, t % 2)]
             stores.append(pltpu.make_async_copy(mant.at[t], target, out_sem.at[t]))
             stores[t].start()
     for store in stores:
         store.wait()
 
 
-def quantise(at, partials, other, amax, chunks=8):
+def quantise(core, partials, other, amax, chunks=8):
     out = pl.pallas_call(
         quant_kernel,
         out_shape=jax.ShapeDtypeStruct((2, 2, 2, 2, 2, 8, HALF), BF16),
@@ -197,31 +203,32 @@
         ],
         compiler_params=PARAMS,
         name="quantise",
-    )(at, partials, other, amax)
+    )(core, partials, other, amax)
     return out.reshape(8, 32, HALF)
 
 
-def rows_kernel(at_ref, w_ref, *refs):
+def rows_kernel(core_ref, w_ref, *refs):
     out_ref, got, full, in_sem, out_sem = refs[-5:]
-    half = pl.ds(pl.multiple_of(at_ref[0] * HALF, HALF), HALF)
-    keep, turn = tile_mask(at_ref)
+    half = pl.ds(pl.multiple_of(core_ref[0] * HALF, HALF), HALF)
+    keep = rows_below(8 - 4 * core_ref[0])
     chunks = [(i >> 2, i >> 1 & 1, i & 1) for i in range(8)]
     loads, stores = [], []
-    for i, (jx, jz, ox) in enumerate(chunks):
-        source, target = w_ref.at[jx, jz, :, ox], got.at[i]
+    for i, (ox, oz, jx) in enumerate(chunks):
+        source, target = w_ref.at[ox, oz, :, jx], got.at[i]
         loads.append(pltpu.make_async_copy(source, target, in_sem.at[i]))
         loads[i].start()
-    for i, (jx, jz, ox) in enumerate(chunks):
+    for i, (ox, oz, jx) in enumerate(chunks):
         loads[i].wait()
-        for oz in (0, 1):
-            n = 2 * i + oz
+        for jz in (0, 1):
+            n = 2 * i + jz
             for b in range(NB):
                 cols = slice(b * BLOCK, (b + 1) * BLOCK)
-                p = got[i, 0, oz, :, cols].astype(F32)
-                q = pltpu.roll(got[i, 1, oz, :, cols].astype(F32), turn, 0)
+                p = got[i, 0, jz, :, cols].astype(F32)
+                q = pltpu.roll(got[i, 1, jz, :, cols].astype(F32), 4, 0)
                 full[n, :8, cols] = jnp.where(keep, p, q).astype(BF16)
                 full[n, 8:, cols] = jnp.where(keep, q, p).astype(BF16)
-            x, z = at_ref[5 + 2 * jx + ox], at_ref[5 + 2 * jz + oz]
+            x = pick(core_ref[0], ARRIVE, 2 * ox + jx)
+            z = pick(core_ref[0], ARRIVE, 2 * oz + jz)
             at = pl.ds(pl.multiple_of(x * 64 + z * 16, 16), 16)
             stores.append(pltpu.make_async_copy(full.at[n], out_ref.at[at, half], out_sem.at[n]))
             stores[n].start()
@@ -229,7 +236,7 @@
         store.wait()
 
 
-def place_rows(at, w, before=None):
+def place_rows(core, w, before=None):
     more = () if before is None else (before,)
     return pl.pallas_call(
         rows_kernel,
@@ -245,7 +252,7 @@
         input_output_aliases={2: 0} if more else {},
         compiler_params=PARAMS,
         name="place_rows",
-    )(at, w.reshape(2, 2, 2, 2, 2, 8, HALF), *more)
+    )(core, w.reshape(2, 2, 2, 2, 2, 8, HALF), *more)
 
 
 def per_device(partials, master, moment_one, moment_two):
@@ -253,12 +260,10 @@
     core, chip = d & 1, d >> 1
     first = core == 0
     row = chip * 4
-    tables = [[c, *(jnp.where(c == 0, t[0][i], t[1][i]) for t in (PLACE, ORDER) for i in range(4))] for c in (core, 1 - core)]
-    mine, theirs = (jnp.stack(table) for table in tables)
-
-    amax, send = block_max(core.reshape(1), partials)
+    mine, theirs = core.reshape(1), (1 - core).reshape(1)
+
+    amax, send = block_max(mine, partials)
     other = lax.ppermute(send, "dp", SWAP)
-    amax = jnp.broadcast_to(amax[:, None], (2, 4, 128, 128)).reshape(8, 128, 128)
     amax = jnp.max(exchange(amax, Y_CORES), axis=0)
     amax = jnp.max(spread(amax, X_Z), axis=0)
 
@@ -301,8 +306,8 @@
         jnp.concatenate([out_other, out_own], axis=2),
     )
 
-    weights = spread(weights, FAR_GROUPS).reshape(32, HALF)
-    weights = spread(weights, NEAR_GROUPS)
+    weights = spread(weights, NEAR_GROUPS).reshape(32, HALF)
+    weights = spread(weights, BACK_GROUPS)
     weights_other = lax.ppermute(weights, "dp", SWAP)
     full = place_rows(mine, weights)
     full = place_rows(theirs, weights_other, full)

time: 164 us -> 161 us (0.982)
  blocking collectives: 20.3 us -> 45.5 us
  starting transfers between devices: 42.4 us -> 21.9 us
  local copies, waits for them, and re-layouts: 7.96 us -> 4.98 us
  waiting for transfers between devices: 60.9 us -> 58.4 us
    all_to_all x2 -> x3, blocking collectives: 20.3 us -> 45.5 us  [exchange(): return lax.all_to_all(x, 'dp', 0, 0, axis_index_groups=among)]
    all_to_all x4 -> x3, starting transfers between devices: 21.8 us -> 12.9 us  [exchange(): return lax.all_to_all(x, 'dp', 0, 0, axis_index_groups=among)]
    ppermute x1, starting transfers between devices: 9.17 us -> 1.01 us  [per_device(): lax.ppermute(jnp.where(first, out[:, 2:], out[:, :2]), 'dp', SWAP)]
    ppermute x1, starting transfers between devices: 7.72 us -> 4.26 us  [per_device(): weights_other = lax.ppermute(weights, 'dp', SWAP)]
    all_to_all x4 -> x3, waiting for transfers between devices: 59.2 us -> 56 us  [exchange(): return lax.all_to_all(x, 'dp', 0, 0, axis_index_groups=among)]
  transfers between devices with their start and end apart: 8 -> 7, of which waited for: 5 -> 4; matrix products, arithmetic and copies ran while one was open for 7% -> 5% of each run, Pallas kernels for 3% -> 2%
where the time goes in v7:
time: 161 us; the launch traced here: 160 us
  waiting for transfers between devices  58.4 us (36%)
  blocking collectives  45.5 us (28%)
  starting transfers between devices  21.9 us (14%)
  Pallas kernels  21.2 us (13%)
  other arithmetic  6.91 us (4%)
  local copies, waits for them, and re-layouts  4.98 us (3%)
    all_to_all x3, waiting for transfers between devices, exchange(): return lax.all_to_all(x, 'dp', 0, 0, axis_index_groups=among)  56 us
    all_to_all x3, blocking collectives, exchange(): return lax.all_to_all(x, 'dp', 0, 0, axis_index_groups=among)  45.5 us
    all_to_all x3, starting transfers between devices, exchange(): return lax.all_to_all(x, 'dp', 0, 0, axis_index_groups=among)  12.9 us
    pallas_call x1, Pallas kernels, block_max(): pl.pallas_call(max_kernel, out_shape=(jax.ShapeDtypeStruct((8, 128, 128),...  7.27 us
    pallas_call x2, Pallas kernels, place_rows(): pl.pallas_call(rows_kernel, out_shape=jax.ShapeDtypeStruct((ROWS, W), BF1...  7.12 us
    pallas_call x1, Pallas kernels, quantise(): pl.pallas_call(quant_kernel, out_shape=jax.ShapeDtypeStruct((2, 2, 2, 2,...  6.85 us
    ppermute x1, starting transfers between devices, per_device(): weights_other = lax.ppermute(weights, 'dp', SWAP)  4.26 us
  transfers between devices with their start and end apart: 7, of which 4 were waited for; matrix products, arithmetic and copies ran while one was open for 5% of the time, Pallas kernels for 2%

profile of v7, /device:TPU:1, one launch (start us, length us, event | category | flops | bytes accessed | tf_op | source)
XLA Modules:
  0.0 159.9 jit_solution(13718972524211266210)
XLA Ops:
  0.6 7.3 %block_max.1 = (bf16[8,128,128]{2,1,0:T(8,128)(2,1)}, bf16[256,8192]{1,0:T(8,128)(2,1)}) custom-call(s32[1]{0:T(128)} %bitcast.3.core_ref, bf16[1,256,16384]{2,1,0:T(8,128)(2,1)} %x_ref.3), custom_call_target="tpu_custom_call" | custom-call | tf_op jit(solution)/shard_map/block_max/pallas_call | solution.py:102
  7.9 1.5 collective-permute-start.1
  9.4 11.2 %all_to_all.30 = bf16[8,128,128]{2,1,0:T(8,128)(2,1)S(1)} all-to-all(bf16[8,128,128]{2,1,0:T(8,128)(2,1)} %get-tuple-element.8), channel_id=1, replica_groups={{0,2,4,6,1,3,5,7},{8,10,12,14,9,11,13,15},{16,18,20,22,17,19,21,23},{24..., dimensions={0} | all-to-all | bytes 524288 | tf_op jit(solution)/shard_map/all_to_all | solution.py:50
  20.8 17.8 %all_to_all.31 = bf16[16,128,128]{2,1,0:T(8,128)(2,1)S(1)} all-to-all(bf16[16,128,128]{2,1,0:T(8,128)(2,1)S(1)} %broadcast_in_dim.60), channel_id=1, replica_groups={{0,8,16,24,32,40,48,56,64,72,80,88,96,104,112,120},{1,9,17,25,33,41,49,..., dimensions={0} | all-to-all | bytes 1048576 | tf_op jit(solution)/shard_map/all_to_all | solution.py:50
  38.5 0.7 reduce_max.28.amax_ref
  39.2 6.8 %quantise.1 = bf16[2,2,2,2,2,8,8192]{6,5,4,3,2,1,0:T(8,128)(2,1)} custom-call(s32[1]{0:T(128)} %bitcast.3.core_ref, bf16[1,256,16384]{2,1,0:T(8,128)(2,1)} %x_ref.3, bf16[256,8192]{1,0:T(8,128)(2,1)} %collective-permute-done.1.other_ref, bf16[128,128]{1,0:T(8,128)(2,1)} %reduce_max.28.amax_ref), custom_call_target="tpu_custom_call" | custom-call | tf_op jit(solution)/shard_map/quantise/pallas_call | solution.py:191
  46.1 4.7 %all-to-all-start.2 = ((bf16[8,32,8192]{2,1,0:T(8,128)(2,1)}), bf16[8,32,8192]{2,1,0:T(8,128)(2,1)}, u32[]{:S(2)}, u32[]{:S(2)}) async-start(bf16[8,32,8192]{2,1,0:T(8,128)(2,1)} %bitcast.58), calls=%async_computation.2 | async-start | bytes 8388608 | tf_op jit(solution)/shard_map/all_to_all | solution.py:50
  50.9 0.2 pad_maximum_fusion.1
  51.1 2.2 %collective-permute-start = (f32[3,2,8192]{2,1,0:T(2,128)S(1)}, f32[3,2,8192]{2,1,0:T(2,128)S(1)}, u32[]{:S(2)}, u32[]{:S(2)}) collective-permute-start(f32[3,2,8192]{2,1,0:T(2,128)S(1)} %get-tuple-element.24), channel_id=1, source_target_pairs={{0,1},{1,0},{2,3},{3,2},{4,5},{5,4},{6,7},{7,6},{8,9},{9,8},{10,11... | collective-permute-start | bytes 589832 | tf_op jit(solution)/shard_map/ppermute | solution.py:273
  53.3 26.1 %all-to-all-done.2 = bf16[8,32,8192]{2,1,0:T(8,128)(2,1)} async-done(((bf16[8,32,8192]{2,1,0:T(8,128)(2,1)}), bf16[8,32,8192]{2,1,0:T(8,128)(2,1)}, u32[]{:S(2)}, u32[]{:S(2)}) %all-to-all-start.2) | async-done | bytes 4194336 | tf_op jit(solution)/shard_map/all_to_all | solution.py:50
  79.3 2.9 %convert_reduce_fusion = f32[32,8192]{1,0:T(8,128)S(1)} fusion(bf16[8,32,8192]{2,1,0:T(8,128)(2,1)} %all-to-all-done.2), kind=kLoop, calls=%fused_computation | loop fusion | flops 3932160 | bytes 5242880 | tf_op jit(solution)/shard_map/reduce_sum | solution.py:282
  82.3 1.0 convert_element_type.32
  83.3 3.7 %all-to-all-start.3 = ((f16[8,4,8192]{2,1,0:T(4,128)(2,1)}), f16[8,4,8192]{2,1,0:T(4,128)(2,1)S(1)}, u32[]{:S(2)}, u32[]{:S(2)}) async-start(f16[8,4,8192]{2,1,0:T(4,128)(2,1)} %convert_element_type.32), calls=%async_computation.3 | async-start | bytes 1048576 | tf_op jit(solution)/shard_map/all_to_all | solution.py:50
  87.0 0.3 maximum_select_fusion.1
  87.4 0.8 select_multiply_fusion
  88.3 5.0 %all-to-all-done.3 = f16[8,4,8192]{2,1,0:T(4,128)(2,1)S(1)} async-done(((f16[8,4,8192]{2,1,0:T(4,128)(2,1)}), f16[8,4,8192]{2,1,0:T(4,128)(2,1)S(1)}, u32[]{:S(2)}, u32[]{:S(2)}) %all-to-all-start.3) | async-done | bytes 524320 | tf_op jit(solution)/shard_map/all_to_all | solution.py:50
  93.3 0.6 convert_reduce_fusion.1
  93.9 0.3 fusion.9
  94.4 0.3 fusion.12
  94.6 0.1 broadcast_in_dim.63
  94.8 16.5 %all_to_all.32 = bf16[8,4,8192]{2,1,0:T(4,128)(2,1)S(1)} all-to-all(bf16[8,4,8192]{2,1,0:T(4,128)(2,1)S(1)} %broadcast_in_dim.63), channel_id=1, replica_groups={{0,2,8,10,32,34,40,42},{6,4,14,12,38,36,46,44},{24,26,16,18,56,58,48,50..., dimensions={0} | all-to-all | bytes 1048576 | tf_op jit(solution)/shard_map/all_to_all | solution.py:50
  111.4 2.5 %broadcast_in_dim.65 = bf16[8,32,8192]{2,1,0:T(8,128)(2,1)} broadcast(bf16[32,8192]{1,0:T(8,128)(2,1)S(1)} %broadcast_in_dim.64), dimensions={1,2} | broadcast | bytes 4718592 | tf_op jit(solution)/shard_map/broadcast_in_dim | solution.py:54
  113.9 4.6 %all-to-all-start.5 = ((bf16[8,32,8192]{2,1,0:T(8,128)(2,1)}), bf16[8,32,8192]{2,1,0:T(8,128)(2,1)}, u32[]{:S(2)}, u32[]{:S(2)}) async-start(bf16[8,32,8192]{2,1,0:T(8,128)(2,1)} %broadcast_in_dim.65), calls=%async_computation.5 | async-start | bytes 8388608 | tf_op jit(solution)/shard_map/all_to_all | solution.py:50
  118.6 0.2 broadcast_select_fusion.1
  118.8 1.0 collective-permute-start.2
  119.8 25.0 %all-to-all-done.5 = bf16[8,32,8192]{2,1,0:T(8,128)(2,1)} async-done(((bf16[8,32,8192]{2,1,0:T(8,128)(2,1)}), bf16[8,32,8192]{2,1,0:T(8,128)(2,1)}, u32[]{:S(2)}, u32[]{:S(2)}) %all-to-all-start.5) | async-done | bytes 4194336 | tf_op jit(solution)/shard_map/all_to_all | solution.py:50
  144.8 4.3 %collective-permute-start.3 = (bf16[8,32,8192]{2,1,0:T(8,128)(2,1)}, bf16[8,32,8192]{2,1,0:T(8,128)(2,1)}, u32[]{:S(2)}, u32[]{:S(2)}) collective-permute-start(bf16[8,32,8192]{2,1,0:T(8,128)(2,1)} %all-to-all-done.5), channel_id=1, source_target_pairs={{0,1},{1,0},{2,3},{3,2},{4,5},{5,4},{6,7},{7,6},{8,9},{9,8},{10,11... | collective-permute-start | bytes 12582920 | tf_op jit(solution)/shard_map/ppermute | solution.py:311
  149.1 0.4 maximum_select_fusion
  149.5 0.8 slice_bitcast_fusion
  150.3 3.6 %place_rows.2.refs_0_ = bf16[256,16384]{1,0:T(8,128)(2,1)} custom-call(s32[1]{0:T(128)} %bitcast.3.core_ref, bf16[2,2,2,2,2,8,8192]{6,5,4,3,2,1,0:T(8,128)(2,1)} %bitcast.13.w_ref), custom_call_target="tpu_custom_call" | custom-call | tf_op jit(solution)/shard_map/place_rows/pallas_call | solution.py:241
  153.9 2.3 %collective-permute-done.3 = bf16[8,32,8192]{2,1,0:T(8,128)(2,1)} collective-permute-done((bf16[8,32,8192]{2,1,0:T(8,128)(2,1)}, bf16[8,32,8192]{2,1,0:T(8,128)(2,1)}, u32[]{:S(2)}, u32[]{:S(2)}) %collective-permute-start.3) | collective-permute-done | bytes 4194336 | tf_op jit(solution)/shard_map/ppermute | solution.py:311
  156.2 3.6 %place_rows.3 = bf16[256,16384]{1,0:T(8,128)(2,1)} custom-call(s32[1]{0:T(128)} %bitcast.10.core_ref, bf16[2,2,2,2,2,8,8192]{6,5,4,3,2,1,0:T(8,128)(2,1)} %bitcast.12.w_ref, bf16[256,16384]{1,0:T(8,128)(2,1)} %place_rows.2.refs_0_), custom_call_target="tpu_custom_call", output_to_operand_aliasing={{}: (2, {})} | custom-call | tf_op jit(solution)/shard_map/place_rows/pallas_call | solution.py:241
  (21 shorter events, 0.9 us)
Async XLA Ops:
  7.9 31.3 %collective-permute-start.1 = (bf16[256,8192]{1,0:T(8,128)(2,1)}, bf16[256,8192]{1,0:T(8,128)(2,1)}, u32[]{:S(2)}, u32[]{:S(2)}) collective-permute-start(bf16[256,8192]{1,0:T(8,128)(2,1)} %get-tuple-element.7), channel_id=1, source_target_pairs={{0,1},{1,0},{2,3},{3,2},{4,5},{5,4},{6,7},{7,6},{8,9},{9,8},{10,11... | collective-permute-start | bytes 12582920 | tf_op jit(solution)/shard_map/ppermute | solution.py:266
  46.1 4.7 %copy-start = (f32[2,16384]{1,0:T(2,128)S(1)}, f32[2,16384]{1,0:T(2,128)}, u32[]{:S(2)}) copy-start(f32[2,16384]{1,0:T(2,128)} %param.7) | copy-start | bytes 393220
  46.1 4.7 %copy-start.1 = (f32[2,16384]{1,0:T(2,128)S(1)}, f32[2,16384]{1,0:T(2,128)}, u32[]{:S(2)}) copy-start(f32[2,16384]{1,0:T(2,128)} %param.6) | copy-start | bytes 393220
  46.1 4.7 %copy-start.2 = (f32[2,16384]{1,0:T(2,128)S(1)}, f32[2,16384]{1,0:T(2,128)}, u32[]{:S(2)}) copy-start(f32[2,16384]{1,0:T(2,128)} %param.5) | copy-start | bytes 393220
  46.1 33.2 %all-to-all-start.2 = ((bf16[8,32,8192]{2,1,0:T(8,128)(2,1)}), bf16[8,32,8192]{2,1,0:T(8,128)(2,1)}, u32[]{:S(2)}, u32[]{:S(2)}) async-start(bf16[8,32,8192]{2,1,0:T(8,128)(2,1)} %bitcast.58), calls=%async_computation.2 | async-start | bytes 8388608 | tf_op jit(solution)/shard_map/all_to_all | solution.py:50
  51.1 35.9 %collective-permute-start = (f32[3,2,8192]{2,1,0:T(2,128)S(1)}, f32[3,2,8192]{2,1,0:T(2,128)S(1)}, u32[]{:S(2)}, u32[]{:S(2)}) collective-permute-start(f32[3,2,8192]{2,1,0:T(2,128)S(1)} %get-tuple-element.24), channel_id=1, source_target_pairs={{0,1},{1,0},{2,3},{3,2},{4,5},{5,4},{6,7},{7,6},{8,9},{9,8},{10,11... | collective-permute-start | bytes 589832 | tf_op jit(solution)/shard_map/ppermute | solution.py:273
  83.3 10.0 %all-to-all-start.3 = ((f16[8,4,8192]{2,1,0:T(4,128)(2,1)}), f16[8,4,8192]{2,1,0:T(4,128)(2,1)S(1)}, u32[]{:S(2)}, u32[]{:S(2)}) async-start(f16[8,4,8192]{2,1,0:T(4,128)(2,1)} %convert_element_type.32), calls=%async_computation.3 | async-start | bytes 1048576 | tf_op jit(solution)/shard_map/all_to_all | solution.py:50
  113.9 30.9 %all-to-all-start.5 = ((bf16[8,32,8192]{2,1,0:T(8,128)(2,1)}), bf16[8,32,8192]{2,1,0:T(8,128)(2,1)}, u32[]{:S(2)}, u32[]{:S(2)}) async-start(bf16[8,32,8192]{2,1,0:T(8,128)(2,1)} %broadcast_in_dim.65), calls=%async_computation.5 | async-start | bytes 8388608 | tf_op jit(solution)/shard_map/all_to_all | solution.py:50
  118.8 30.3 %collective-permute-start.2 = (f32[4,2,8192]{2,1,0:T(2,128)S(1)}, f32[4,2,8192]{2,1,0:T(2,128)S(1)}, u32[]{:S(2)}, u32[]{:S(2)}) collective-permute-start(f32[4,2,8192]{2,1,0:T(2,128)S(1)} %get-tuple-element.19), channel_id=1, source_target_pairs={{0,1},{1,0},{2,3},{3,2},{4,5},{5,4},{6,7},{7,6},{8,9},{9,8},{10,11... | collective-permute-start | bytes 786440 | tf_op jit(solution)/shard_map/ppermute | solution.py:302
  144.8 11.4 %collective-permute-start.3 = (bf16[8,32,8192]{2,1,0:T(8,128)(2,1)}, bf16[8,32,8192]{2,1,0:T(8,128)(2,1)}, u32[]{:S(2)}, u32[]{:S(2)}) collective-permute-start(bf16[8,32,8192]{2,1,0:T(8,128)(2,1)} %all-to-all-done.5), channel_id=1, source_target_pairs={{0,1},{1,0},{2,3},{3,2},{4,5},{5,4},{6,7},{7,6},{8,9},{9,8},{10,11... | collective-permute-start | bytes 12582920 | tf_op jit(solution)/shard_map/ppermute | solution.py:311

commit v8 on v7

--- a/solution.py
+++ b/solution.py
@@ -32,7 +32,7 @@
     return [
         [device(x, z, y, core) for x in px for z in pz for y in py]
         for core in (0, 1)
-        for px in pairs[core]
+        for px in pairs[1 - core]
         for pz in pairs[core]
         for py in pairs[core]
     ]
@@ -56,9 +56,9 @@
 
 def max_kernel(core_ref, x_ref, amax_ref, send_ref, buf, left, right, in_sem, out_sem):
     core = core_ref[0]
-    rows = ROWS // in_sem.shape[0]
     theirs = pl.ds(pl.multiple_of((1 - core) * HALF, HALF), HALF)
-    chunks = [pl.ds(i * rows, rows) for i in range(ROWS // rows)]
+    starts = (0, 32, 64, 128, 192, ROWS)
+    chunks = [pl.ds(i, j - i) for i, j in zip(starts, starts[1:])]
     loads = [
         pltpu.make_async_copy(x_ref.at[0, at], buf.at[at], in_sem.at[i])
         for i, at in enumerate(chunks)
@@ -69,18 +69,17 @@
     ]
     for load in loads:
         load.start()
-    lane = lax.broadcasted_iota(jnp.int32, (rows, 128), 1)
-    low = lane < NB
     for i, at in enumerate(chunks):
+        lane = lax.broadcasted_iota(jnp.int32, (at.size, 128), 1)
         loads[i].wait()
         stores[i].start()
-        acc = jnp.zeros((rows, 128), F32)
+        acc = jnp.zeros((at.size, 128), F32)
         for b in range(W // BLOCK):
             v = jnp.abs(buf[at, b * BLOCK : (b + 1) * BLOCK].astype(F32))
             acc = jnp.where(lane == b, jnp.max(v, axis=1, keepdims=True), acc)
-        rolled = pltpu.roll(acc, NB, 1)
-        to = pl.ds(i * rows % 128, rows)
-        if i * rows < 128:
+        rolled, low = pltpu.roll(acc, NB, 1), lane < NB
+        to = pl.ds(at.start % 128, at.size)
+        if at.start < 128:
             left[to, :], right[to, :] = acc, rolled
         else:
             left[to, :] = jnp.where(low, left[to, :], rolled)
@@ -98,7 +97,7 @@
 PARAMS = pltpu.CompilerParams(vmem_limit_bytes=60 << 20)
 
 
-def block_max(core, partials, chunks=4):
+def block_max(core, partials, chunks=5):
     return pl.pallas_call(
         max_kernel,
         out_shape=(
@@ -138,7 +137,7 @@
 
 
 def block_of(core, x, z, y):
-    px, pz = pick(core, PLACE, x), pick(core, PLACE, z)
+    px, pz = pick(1 - core, PLACE, x), pick(core, PLACE, z)
     return (px >> 1, pz >> 1, y, px & 1, pz & 1)
 
 
@@ -227,7 +226,7 @@
                 q = pltpu.roll(got[i, 1, jz, :, cols].astype(F32), 4, 0)
                 full[n, :8, cols] = jnp.where(keep, p, q).astype(BF16)
                 full[n, 8:, cols] = jnp.where(keep, q, p).astype(BF16)
-            x = pick(core_ref[0], ARRIVE, 2 * ox + jx)
+            x = pick(1 - core_ref[0], ARRIVE, 2 * ox + jx)
             z = pick(core_ref[0], ARRIVE, 2 * oz + jz)
             at = pl.ds(pl.multiple_of(x * 64 + z * 16, 16), 16)
             stores.append(pltpu.make_async_copy(full.at[n], out_ref.at[at, half], out_sem.at[n]))

time: 161 us -> 161 us (level)
  waiting for transfers between devices: 58.4 us -> 60.6 us
    all_to_all x3, waiting for transfers between devices: 56 us -> 58.2 us  [exchange(): return lax.all_to_all(x, 'dp', 0, 0, axis_index_groups=among)]
where the time goes in v8:
time: 161 us; the launch traced here: 160 us
  waiting for transfers between devices  60.6 us (38%)
  blocking collectives  44.6 us (28%)
  Pallas kernels  21 us (13%)
  starting transfers between devices  20.7 us (13%)
  other arithmetic  6.91 us (4%)
  local copies, waits for them, and re-layouts  4.98 us (3%)
    all_to_all x3, waiting for transfers between devices, exchange(): return lax.all_to_all(x, 'dp', 0, 0, axis_index_groups=among)  58.2 us
    all_to_all x3, blocking collectives, exchange(): return lax.all_to_all(x, 'dp', 0, 0, axis_index_groups=among)  44.6 us
    all_to_all x3, starting transfers between devices, exchange(): return lax.all_to_all(x, 'dp', 0, 0, axis_index_groups=among)  12.9 us
    pallas_call x2, Pallas kernels, place_rows(): pl.pallas_call(rows_kernel, out_shape=jax.ShapeDtypeStruct((ROWS, W), BF1...  7.12 us
    pallas_call x1, Pallas kernels, block_max(): pl.pallas_call(max_kernel, out_shape=(jax.ShapeDtypeStruct((8, 128, 128),...  7.07 us
    pallas_call x1, Pallas kernels, quantise(): pl.pallas_call(quant_kernel, out_shape=jax.ShapeDtypeStruct((2, 2, 2, 2,...  6.85 us
  transfers between devices with their start and end apart: 7, of which 4 were waited for; matrix products, arithmetic and copies ran while one was open for 5% of the time, Pallas kernels for 2%

profile of v8, /device:TPU:1, one launch (start us, length us, event | category | flops | bytes accessed | tf_op | source)
XLA Modules:
  0.0 159.9 jit_solution(15094682956255427603)
XLA Ops:
  0.6 7.1 %block_max.1 = (bf16[8,128,128]{2,1,0:T(8,128)(2,1)}, bf16[256,8192]{1,0:T(8,128)(2,1)}) custom-call(s32[1]{0:T(128)} %bitcast.3.core_ref, bf16[1,256,16384]{2,1,0:T(8,128)(2,1)} %x_ref.3), custom_call_target="tpu_custom_call" | custom-call | tf_op jit(solution)/shard_map/block_max/pallas_call | solution.py:101
  7.7 1.5 collective-permute-start.1
  9.2 11.2 %all_to_all.30 = bf16[8,128,128]{2,1,0:T(8,128)(2,1)S(1)} all-to-all(bf16[8,128,128]{2,1,0:T(8,128)(2,1)} %get-tuple-element.8), channel_id=1, replica_groups={{0,2,4,6,1,3,5,7},{8,10,12,14,9,11,13,15},{16,18,20,22,17,19,21,23},{24..., dimensions={0} | all-to-all | bytes 524288 | tf_op jit(solution)/shard_map/all_to_all | solution.py:50
  20.6 17.8 %all_to_all.31 = bf16[16,128,128]{2,1,0:T(8,128)(2,1)S(1)} all-to-all(bf16[16,128,128]{2,1,0:T(8,128)(2,1)S(1)} %broadcast_in_dim.60), channel_id=1, replica_groups={{0,8,16,24,32,40,48,56,64,72,80,88,96,104,112,120},{1,9,17,25,33,41,49,..., dimensions={0} | all-to-all | bytes 1048576 | tf_op jit(solution)/shard_map/all_to_all | solution.py:50
  38.3 0.7 reduce_max.28.amax_ref
  39.0 6.8 %quantise.1 = bf16[2,2,2,2,2,8,8192]{6,5,4,3,2,1,0:T(8,128)(2,1)} custom-call(s32[1]{0:T(128)} %bitcast.3.core_ref, bf16[1,256,16384]{2,1,0:T(8,128)(2,1)} %x_ref.3, bf16[256,8192]{1,0:T(8,128)(2,1)} %collective-permute-done.1.other_ref, bf16[128,128]{1,0:T(8,128)(2,1)} %reduce_max.28.amax_ref), custom_call_target="tpu_custom_call" | custom-call | tf_op jit(solution)/shard_map/quantise/pallas_call | solution.py:190
  45.9 4.7 %all-to-all-start.2 = ((bf16[8,32,8192]{2,1,0:T(8,128)(2,1)}), bf16[8,32,8192]{2,1,0:T(8,128)(2,1)}, u32[]{:S(2)}, u32[]{:S(2)}) async-start(bf16[8,32,8192]{2,1,0:T(8,128)(2,1)} %bitcast.58), calls=%async_computation.2 | async-start | bytes 8388608 | tf_op jit(solution)/shard_map/all_to_all | solution.py:50
  50.7 0.2 pad_maximum_fusion.1
  50.9 2.2 %collective-permute-start = (f32[3,2,8192]{2,1,0:T(2,128)S(1)}, f32[3,2,8192]{2,1,0:T(2,128)S(1)}, u32[]{:S(2)}, u32[]{:S(2)}) collective-permute-start(f32[3,2,8192]{2,1,0:T(2,128)S(1)} %get-tuple-element.24), channel_id=1, source_target_pairs={{0,1},{1,0},{2,3},{3,2},{4,5},{5,4},{6,7},{7,6},{8,9},{9,8},{10,11... | collective-permute-start | bytes 589832 | tf_op jit(solution)/shard_map/ppermute | solution.py:272
  53.1 26.0 %all-to-all-done.2 = bf16[8,32,8192]{2,1,0:T(8,128)(2,1)} async-done(((bf16[8,32,8192]{2,1,0:T(8,128)(2,1)}), bf16[8,32,8192]{2,1,0:T(8,128)(2,1)}, u32[]{:S(2)}, u32[]{:S(2)}) %all-to-all-start.2) | async-done | bytes 4194336 | tf_op jit(solution)/shard_map/all_to_all | solution.py:50
  79.0 2.9 %convert_reduce_fusion = f32[32,8192]{1,0:T(8,128)S(1)} fusion(bf16[8,32,8192]{2,1,0:T(8,128)(2,1)} %all-to-all-done.2), kind=kLoop, calls=%fused_computation | loop fusion | flops 3932160 | bytes 5242880 | tf_op jit(solution)/shard_map/reduce_sum | solution.py:281
  82.0 1.0 convert_element_type.32
  83.0 3.7 %all-to-all-start.3 = ((f16[8,4,8192]{2,1,0:T(4,128)(2,1)}), f16[8,4,8192]{2,1,0:T(4,128)(2,1)S(1)}, u32[]{:S(2)}, u32[]{:S(2)}) async-start(f16[8,4,8192]{2,1,0:T(4,128)(2,1)} %convert_element_type.32), calls=%async_computation.3 | async-start | bytes 1048576 | tf_op jit(solution)/shard_map/all_to_all | solution.py:50
  86.7 0.3 maximum_select_fusion.1
  87.1 0.8 select_multiply_fusion
  88.0 6.2 %all-to-all-done.3 = f16[8,4,8192]{2,1,0:T(4,128)(2,1)S(1)} async-done(((f16[8,4,8192]{2,1,0:T(4,128)(2,1)}), f16[8,4,8192]{2,1,0:T(4,128)(2,1)S(1)}, u32[]{:S(2)}, u32[]{:S(2)}) %all-to-all-start.3) | async-done | bytes 524320 | tf_op jit(solution)/shard_map/all_to_all | solution.py:50
  94.2 0.6 convert_reduce_fusion.1
  94.8 0.3 fusion.9
  95.3 0.3 fusion.12
  95.5 0.1 broadcast_in_dim.63
  95.7 15.6 %all_to_all.32 = bf16[8,4,8192]{2,1,0:T(4,128)(2,1)S(1)} all-to-all(bf16[8,4,8192]{2,1,0:T(4,128)(2,1)S(1)} %broadcast_in_dim.63), channel_id=1, replica_groups={{32,34,40,42,64,66,72,74},{38,36,46,44,70,68,78,76},{56,58,48,50,88,90,..., dimensions={0} | all-to-all | bytes 1048576 | tf_op jit(solution)/shard_map/all_to_all | solution.py:50
  111.4 2.5 %broadcast_in_dim.65 = bf16[8,32,8192]{2,1,0:T(8,128)(2,1)} broadcast(bf16[32,8192]{1,0:T(8,128)(2,1)S(1)} %broadcast_in_dim.64), dimensions={1,2} | broadcast | bytes 4718592 | tf_op jit(solution)/shard_map/broadcast_in_dim | solution.py:54
  113.9 4.6 %all-to-all-start.5 = ((bf16[8,32,8192]{2,1,0:T(8,128)(2,1)}), bf16[8,32,8192]{2,1,0:T(8,128)(2,1)}, u32[]{:S(2)}, u32[]{:S(2)}) async-start(bf16[8,32,8192]{2,1,0:T(8,128)(2,1)} %broadcast_in_dim.65), calls=%async_computation.5 | async-start | bytes 8388608 | tf_op jit(solution)/shard_map/all_to_all | solution.py:50
  118.6 0.2 broadcast_select_fusion.1
  118.8 1.1 collective-permute-start.2
  119.9 26.1 %all-to-all-done.5 = bf16[8,32,8192]{2,1,0:T(8,128)(2,1)} async-done(((bf16[8,32,8192]{2,1,0:T(8,128)(2,1)}), bf16[8,32,8192]{2,1,0:T(8,128)(2,1)}, u32[]{:S(2)}, u32[]{:S(2)}) %all-to-all-start.5) | async-done | bytes 4194336 | tf_op jit(solution)/shard_map/all_to_all | solution.py:50
  146.0 3.0 %collective-permute-start.3 = (bf16[8,32,8192]{2,1,0:T(8,128)(2,1)}, bf16[8,32,8192]{2,1,0:T(8,128)(2,1)}, u32[]{:S(2)}, u32[]{:S(2)}) collective-permute-start(bf16[8,32,8192]{2,1,0:T(8,128)(2,1)} %all-to-all-done.5), channel_id=1, source_target_pairs={{0,1},{1,0},{2,3},{3,2},{4,5},{5,4},{6,7},{7,6},{8,9},{9,8},{10,11... | collective-permute-start | bytes 12582920 | tf_op jit(solution)/shard_map/ppermute | solution.py:310
  149.0 0.4 maximum_select_fusion
  149.5 0.8 slice_bitcast_fusion
  150.3 3.6 %place_rows.2.refs_0_ = bf16[256,16384]{1,0:T(8,128)(2,1)} custom-call(s32[1]{0:T(128)} %bitcast.3.core_ref, bf16[2,2,2,2,2,8,8192]{6,5,4,3,2,1,0:T(8,128)(2,1)} %bitcast.13.w_ref), custom_call_target="tpu_custom_call" | custom-call | tf_op jit(solution)/shard_map/place_rows/pallas_call | solution.py:240
  153.8 2.3 %collective-permute-done.3 = bf16[8,32,8192]{2,1,0:T(8,128)(2,1)} collective-permute-done((bf16[8,32,8192]{2,1,0:T(8,128)(2,1)}, bf16[8,32,8192]{2,1,0:T(8,128)(2,1)}, u32[]{:S(2)}, u32[]{:S(2)}) %collective-permute-start.3) | collective-permute-done | bytes 4194336 | tf_op jit(solution)/shard_map/ppermute | solution.py:310
  156.2 3.6 %place_rows.3 = bf16[256,16384]{1,0:T(8,128)(2,1)} custom-call(s32[1]{0:T(128)} %bitcast.10.core_ref, bf16[2,2,2,2,2,8,8192]{6,5,4,3,2,1,0:T(8,128)(2,1)} %bitcast.12.w_ref, bf16[256,16384]{1,0:T(8,128)(2,1)} %place_rows.2.refs_0_), custom_call_target="tpu_custom_call", output_to_operand_aliasing={{}: (2, {})} | custom-call | tf_op jit(solution)/shard_map/place_rows/pallas_call | solution.py:240
  (21 shorter events, 0.9 us)
Async XLA Ops:
  7.7 31.3 %collective-permute-start.1 = (bf16[256,8192]{1,0:T(8,128)(2,1)}, bf16[256,8192]{1,0:T(8,128)(2,1)}, u32[]{:S(2)}, u32[]{:S(2)}) collective-permute-start(bf16[256,8192]{1,0:T(8,128)(2,1)} %get-tuple-element.7), channel_id=1, source_target_pairs={{0,1},{1,0},{2,3},{3,2},{4,5},{5,4},{6,7},{7,6},{8,9},{9,8},{10,11... | collective-permute-start | bytes 12582920 | tf_op jit(solution)/shard_map/ppermute | solution.py:265
  45.9 4.7 %copy-start = (f32[2,16384]{1,0:T(2,128)S(1)}, f32[2,16384]{1,0:T(2,128)}, u32[]{:S(2)}) copy-start(f32[2,16384]{1,0:T(2,128)} %param.7) | copy-start | bytes 393220
  45.9 4.7 %copy-start.1 = (f32[2,16384]{1,0:T(2,128)S(1)}, f32[2,16384]{1,0:T(2,128)}, u32[]{:S(2)}) copy-start(f32[2,16384]{1,0:T(2,128)} %param.6) | copy-start | bytes 393220
  45.9 4.7 %copy-start.2 = (f32[2,16384]{1,0:T(2,128)S(1)}, f32[2,16384]{1,0:T(2,128)}, u32[]{:S(2)}) copy-start(f32[2,16384]{1,0:T(2,128)} %param.5) | copy-start | bytes 393220
  45.9 33.1 %all-to-all-start.2 = ((bf16[8,32,8192]{2,1,0:T(8,128)(2,1)}), bf16[8,32,8192]{2,1,0:T(8,128)(2,1)}, u32[]{:S(2)}, u32[]{:S(2)}) async-start(bf16[8,32,8192]{2,1,0:T(8,128)(2,1)} %bitcast.58), calls=%async_computation.2 | async-start | bytes 8388608 | tf_op jit(solution)/shard_map/all_to_all | solution.py:50
  50.9 35.8 %collective-permute-start = (f32[3,2,8192]{2,1,0:T(2,128)S(1)}, f32[3,2,8192]{2,1,0:T(2,128)S(1)}, u32[]{:S(2)}, u32[]{:S(2)}) collective-permute-start(f32[3,2,8192]{2,1,0:T(2,128)S(1)} %get-tuple-element.24), channel_id=1, source_target_pairs={{0,1},{1,0},{2,3},{3,2},{4,5},{5,4},{6,7},{7,6},{8,9},{9,8},{10,11... | collective-permute-start | bytes 589832 | tf_op jit(solution)/shard_map/ppermute | solution.py:272
  83.0 11.2 %all-to-all-start.3 = ((f16[8,4,8192]{2,1,0:T(4,128)(2,1)}), f16[8,4,8192]{2,1,0:T(4,128)(2,1)S(1)}, u32[]{:S(2)}, u32[]{:S(2)}) async-start(f16[8,4,8192]{2,1,0:T(4,128)(2,1)} %convert_element_type.32), calls=%async_computation.3 | async-start | bytes 1048576 | tf_op jit(solution)/shard_map/all_to_all | solution.py:50
  113.9 32.1 %all-to-all-start.5 = ((bf16[8,32,8192]{2,1,0:T(8,128)(2,1)}), bf16[8,32,8192]{2,1,0:T(8,128)(2,1)}, u32[]{:S(2)}, u32[]{:S(2)}) async-start(bf16[8,32,8192]{2,1,0:T(8,128)(2,1)} %broadcast_in_dim.65), calls=%async_computation.5 | async-start | bytes 8388608 | tf_op jit(solution)/shard_map/all_to_all | solution.py:50
  118.8 30.2 %collective-permute-start.2 = (f32[4,2,8192]{2,1,0:T(2,128)S(1)}, f32[4,2,8192]{2,1,0:T(2,128)S(1)}, u32[]{:S(2)}, u32[]{:S(2)}) collective-permute-start(f32[4,2,8192]{2,1,0:T(2,128)S(1)} %get-tuple-element.19), channel_id=1, source_target_pairs={{0,1},{1,0},{2,3},{3,2},{4,5},{5,4},{6,7},{7,6},{8,9},{9,8},{10,11... | collective-permute-start | bytes 786440 | tf_op jit(solution)/shard_map/ppermute | solution.py:301
  146.0 10.2 %collective-permute-start.3 = (bf16[8,32,8192]{2,1,0:T(8,128)(2,1)}, bf16[8,32,8192]{2,1,0:T(8,128)(2,1)}, u32[]{:S(2)}, u32[]{:S(2)}) collective-permute-start(bf16[8,32,8192]{2,1,0:T(8,128)(2,1)} %all-to-all-done.5), channel_id=1, source_target_pairs={{0,1},{1,0},{2,3},{3,2},{4,5},{5,4},{6,7},{7,6},{8,9},{9,8},{10,11... | collective-permute-start | bytes 12582920 | tf_op jit(solution)/shard_map/ppermute | solution.py:310

commit v9 on v8

--- a/solution.py
+++ b/solution.py
@@ -42,7 +42,8 @@
 FAR_GROUPS = groups(FAR)
 BACK_GROUPS = groups(BACK)
 Y_CORES = [[device(x, z, y, core) for core in (0, 1) for y in range(4)] for x in range(4) for z in range(4)]
-X_Z = [[device(x, z, y, core) for x in range(4) for z in range(4)] for y in range(4) for core in (0, 1)]
+X_RING = [[device(x, z, y, core) for x in range(4)] for z in range(4) for y in range(4) for core in (0, 1)]
+Z_RING = [[device(x, z, y, core) for z in range(4)] for x in range(4) for y in range(4) for core in (0, 1)]
 SWAP = [(d, d ^ 1) for d in range(N_DP)]
 
 
@@ -207,23 +208,18 @@
 
 
 def rows_kernel(core_ref, w_ref, *refs):
-    out_ref, got, full, in_sem, out_sem = refs[-5:]
+    out_ref, full, out_sem = refs[-3:]
     half = pl.ds(pl.multiple_of(core_ref[0] * HALF, HALF), HALF)
     keep = rows_below(8 - 4 * core_ref[0])
     chunks = [(i >> 2, i >> 1 & 1, i & 1) for i in range(8)]
-    loads, stores = [], []
+    stores = []
     for i, (ox, oz, jx) in enumerate(chunks):
-        source, target = w_ref.at[ox, oz, :, jx], got.at[i]
-        loads.append(pltpu.make_async_copy(source, target, in_sem.at[i]))
-        loads[i].start()
-    for i, (ox, oz, jx) in enumerate(chunks):
-        loads[i].wait()
         for jz in (0, 1):
             n = 2 * i + jz
             for b in range(NB):
                 cols = slice(b * BLOCK, (b + 1) * BLOCK)
-                p = got[i, 0, jz, :, cols].astype(F32)
-                q = pltpu.roll(got[i, 1, jz, :, cols].astype(F32), 4, 0)
+                p = w_ref[ox, oz, 0, jx, jz, :, cols].astype(F32)
+                q = pltpu.roll(w_ref[ox, oz, 1, jx, jz, :, cols].astype(F32), 4, 0)
                 full[n, :8, cols] = jnp.where(keep, p, q).astype(BF16)
                 full[n, 8:, cols] = jnp.where(keep, q, p).astype(BF16)
             x = pick(1 - core_ref[0], ARRIVE, 2 * ox + jx)
@@ -240,16 +236,14 @@
     return pl.pallas_call(
         rows_kernel,
         out_shape=jax.ShapeDtypeStruct((ROWS, W), BF16),
-        in_specs=[SMEM, HBM, *(HBM for _ in more)],
+        in_specs=[SMEM, VMEM, *(HBM for _ in more)],
         out_specs=HBM,
         scratch_shapes=[
-            pltpu.VMEM((8, 2, 2, 8, HALF), BF16),
             pltpu.VMEM((16, 16, HALF), BF16),
-            pltpu.SemaphoreType.DMA((8,)),
             pltpu.SemaphoreType.DMA((16,)),
         ],
         input_output_aliases={2: 0} if more else {},
-        compiler_params=PARAMS,
+        compiler_params=pltpu.CompilerParams(vmem_limit_bytes=24 << 20),
         name="place_rows",
     )(core, w.reshape(2, 2, 2, 2, 2, 8, HALF), *more)
 
@@ -264,7 +258,8 @@
     amax, send = block_max(mine, partials)
     other = lax.ppermute(send, "dp", SWAP)
     amax = jnp.max(exchange(amax, Y_CORES), axis=0)
-    amax = jnp.max(spread(amax, X_Z), axis=0)
+    amax = jnp.max(spread(amax, X_RING), axis=0)
+    amax = jnp.max(spread(amax, Z_RING), axis=0)
 
     state = jnp.stack([master, moment_one, moment_two])
     state_own = lax.dynamic_slice_in_dim(state, core * HALF, HALF, 2)

time: 161 us -> 161 us (level)
  starting transfers between devices: 20.7 us -> 24.9 us
  waiting for transfers between devices: 60.6 us -> 57.1 us
    all_to_all x3, waiting for transfers between devices: 58.2 us -> 55.7 us  [exchange(): return lax.all_to_all(x, 'dp', 0, 0, axis_index_groups=among)]
    all_to_all x3 -> x4, blocking collectives: 44.6 us -> 45 us  [exchange(): return lax.all_to_all(x, 'dp', 0, 0, axis_index_groups=among)]
  transfers between devices with their start and end apart: 7 -> 7, of which waited for: 4 -> 4; matrix products, arithmetic and copies ran while one was open for 5% -> 5% of each run, Pallas kernels for 2% -> 3%
where the time goes in v9:
time: 161 us; the launch traced here: 160 us
  waiting for transfers between devices  57.1 us (35%)
  blocking collectives  45 us (28%)
  starting transfers between devices  24.9 us (15%)
  Pallas kernels  20.5 us (13%)
  other arithmetic  6.87 us (4%)
  local copies, waits for them, and re-layouts  4.93 us (3%)
    all_to_all x3, waiting for transfers between devices, exchange(): return lax.all_to_all(x, 'dp', 0, 0, axis_index_groups=among)  55.7 us
    all_to_all x4, blocking collectives, exchange(): return lax.all_to_all(x, 'dp', 0, 0, axis_index_groups=among)  45 us
    all_to_all x3, starting transfers between devices, exchange(): return lax.all_to_all(x, 'dp', 0, 0, axis_index_groups=among)  12.9 us
    pallas_call x1, Pallas kernels, block_max(): pl.pallas_call(max_kernel, out_shape=(jax.ShapeDtypeStruct((8, 128, 128),...  7.06 us
    pallas_call x1, Pallas kernels, quantise(): pl.pallas_call(quant_kernel, out_shape=jax.ShapeDtypeStruct((2, 2, 2, 2,...  6.85 us
    pallas_call x2, Pallas kernels, place_rows(): pl.pallas_call(rows_kernel, out_shape=jax.ShapeDtypeStruct((ROWS, W), BF1...  6.57 us
    ppermute x1, starting transfers between devices, per_device(): weights_other = lax.ppermute(weights, 'dp', SWAP)  4.61 us
    ppermute x1, starting transfers between devices, per_device(): state_other = lax.ppermute(state_other, 'dp', SWAP)  3.3 us
  transfers between devices with their start and end apart: 7, of which 4 were waited for; matrix products, arithmetic and copies ran while one was open for 5% of the time, Pallas kernels for 3%

profile of v9, /device:TPU:1, one launch (start us, length us, event | category | flops | bytes accessed | tf_op | source)
XLA Modules:
  0.0 160.4 jit_solution(3196176737559016614)
XLA Ops:
  0.6 7.1 %block_max.1 = (bf16[8,128,128]{2,1,0:T(8,128)(2,1)}, bf16[256,8192]{1,0:T(8,128)(2,1)}) custom-call(s32[1]{0:T(128)} %bitcast.3.core_ref, bf16[1,256,16384]{2,1,0:T(8,128)(2,1)} %x_ref.3), custom_call_target="tpu_custom_call" | custom-call | tf_op jit(solution)/shard_map/block_max/pallas_call | solution.py:102
  7.7 1.5 collective-permute-start.1
  9.2 11.2 %all_to_all.35 = bf16[8,128,128]{2,1,0:T(8,128)(2,1)S(1)} all-to-all(bf16[8,128,128]{2,1,0:T(8,128)(2,1)} %get-tuple-element.8), channel_id=1, replica_groups={{0,2,4,6,1,3,5,7},{8,10,12,14,9,11,13,15},{16,18,20,22,17,19,21,23},{24..., dimensions={0} | all-to-all | bytes 524288 | tf_op jit(solution)/shard_map/all_to_all | solution.py:51
  20.5 8.6 %all_to_all.36 = bf16[4,128,128]{2,1,0:T(8,128)(2,1)S(1)} all-to-all(bf16[4,128,128]{2,1,0:T(8,128)(2,1)S(1)} %broadcast_in_dim.66), channel_id=1, replica_groups={{0,32,64,96},{1,33,65,97},{2,34,66,98},{3,35,67,99},{4,36,68,100},{5,37..., dimensions={0} | all-to-all | bytes 262144 | tf_op jit(solution)/shard_map/all_to_all | solution.py:51
  29.2 9.7 %all_to_all.37 = bf16[4,128,128]{2,1,0:T(8,128)(2,1)S(1)} all-to-all(bf16[4,128,128]{2,1,0:T(8,128)(2,1)S(1)} %broadcast_in_dim.67), channel_id=1, replica_groups={{0,8,16,24},{1,9,17,25},{2,10,18,26},{3,11,19,27},{4,12,20,28},{5,13,21..., dimensions={0} | all-to-all | bytes 262144 | tf_op jit(solution)/shard_map/all_to_all | solution.py:51
  38.8 0.6 reduce_max.38.amax_ref
  39.5 6.8 %quantise.1 = bf16[2,2,2,2,2,8,8192]{6,5,4,3,2,1,0:T(8,128)(2,1)} custom-call(s32[1]{0:T(128)} %bitcast.3.core_ref, bf16[1,256,16384]{2,1,0:T(8,128)(2,1)} %x_ref.3, bf16[256,8192]{1,0:T(8,128)(2,1)} %collective-permute-done.1.other_ref, bf16[128,128]{1,0:T(8,128)(2,1)} %reduce_max.38.amax_ref), custom_call_target="tpu_custom_call" | custom-call | tf_op jit(solution)/shard_map/quantise/pallas_call | solution.py:191
  46.4 4.7 %all-to-all-start.3 = ((bf16[8,32,8192]{2,1,0:T(8,128)(2,1)}), bf16[8,32,8192]{2,1,0:T(8,128)(2,1)}, u32[]{:S(2)}, u32[]{:S(2)}) async-start(bf16[8,32,8192]{2,1,0:T(8,128)(2,1)} %bitcast.59), calls=%async_computation.3 | async-start | bytes 8388608 | tf_op jit(solution)/shard_map/all_to_all | solution.py:51
  51.1 0.2 pad_maximum_fusion.1
  51.3 3.3 %collective-permute-start = (f32[3,2,8192]{2,1,0:T(2,128)S(1)}, f32[3,2,8192]{2,1,0:T(2,128)S(1)}, u32[]{:S(2)}, u32[]{:S(2)}) collective-permute-start(f32[3,2,8192]{2,1,0:T(2,128)S(1)} %get-tuple-element.24), channel_id=1, source_target_pairs={{0,1},{1,0},{2,3},{3,2},{4,5},{5,4},{6,7},{7,6},{8,9},{9,8},{10,11... | collective-permute-start | bytes 589832 | tf_op jit(solution)/shard_map/ppermute | solution.py:267
  54.6 25.0 %all-to-all-done.3 = bf16[8,32,8192]{2,1,0:T(8,128)(2,1)} async-done(((bf16[8,32,8192]{2,1,0:T(8,128)(2,1)}), bf16[8,32,8192]{2,1,0:T(8,128)(2,1)}, u32[]{:S(2)}, u32[]{:S(2)}) %all-to-all-start.3) | async-done | bytes 4194336 | tf_op jit(solution)/shard_map/all_to_all | solution.py:51
  79.6 2.9 %convert_reduce_fusion = f32[32,8192]{1,0:T(8,128)S(1)} fusion(bf16[8,32,8192]{2,1,0:T(8,128)(2,1)} %all-to-all-done.3), kind=kLoop, calls=%fused_computation | loop fusion | flops 3932160 | bytes 5242880 | tf_op jit(solution)/shard_map/reduce_sum | solution.py:276
  82.6 1.0 convert_element_type.32
  83.6 3.7 %all-to-all-start.4 = ((f16[8,4,8192]{2,1,0:T(4,128)(2,1)}), f16[8,4,8192]{2,1,0:T(4,128)(2,1)S(1)}, u32[]{:S(2)}, u32[]{:S(2)}) async-start(f16[8,4,8192]{2,1,0:T(4,128)(2,1)} %convert_element_type.32), calls=%async_computation.4 | async-start | bytes 1048576 | tf_op jit(solution)/shard_map/all_to_all | solution.py:51
  87.2 0.3 maximum_select_fusion.1
  87.6 0.8 select_multiply_fusion
  88.6 6.2 %all-to-all-done.4 = f16[8,4,8192]{2,1,0:T(4,128)(2,1)S(1)} async-done(((f16[8,4,8192]{2,1,0:T(4,128)(2,1)}), f16[8,4,8192]{2,1,0:T(4,128)(2,1)S(1)}, u32[]{:S(2)}, u32[]{:S(2)}) %all-to-all-start.4) | async-done | bytes 524320 | tf_op jit(solution)/shard_map/all_to_all | solution.py:51
  94.7 0.6 convert_reduce_fusion.1
  95.4 0.3 fusion.9
  95.8 0.3 fusion.12
  96.2 15.5 %all_to_all.38 = bf16[8,4,8192]{2,1,0:T(4,128)(2,1)S(1)} all-to-all(bf16[8,4,8192]{2,1,0:T(4,128)(2,1)S(1)} %broadcast_in_dim.70), channel_id=1, replica_groups={{32,34,40,42,64,66,72,74},{38,36,46,44,70,68,78,76},{56,58,48,50,88,90,..., dimensions={0} | all-to-all | bytes 1048576 | tf_op jit(solution)/shard_map/all_to_all | solution.py:51
  111.9 2.5 %broadcast_in_dim.72 = bf16[8,32,8192]{2,1,0:T(8,128)(2,1)} broadcast(bf16[32,8192]{1,0:T(8,128)(2,1)S(1)} %broadcast_in_dim.71), dimensions={1,2} | broadcast | bytes 4718592 | tf_op jit(solution)/shard_map/broadcast_in_dim | solution.py:55
  114.4 4.5 %all-to-all-start.6 = ((bf16[8,32,8192]{2,1,0:T(8,128)(2,1)}), bf16[8,32,8192]{2,1,0:T(8,128)(2,1)}, u32[]{:S(2)}, u32[]{:S(2)}) async-start(bf16[8,32,8192]{2,1,0:T(8,128)(2,1)} %broadcast_in_dim.72), calls=%async_computation.6 | async-start | bytes 8388608 | tf_op jit(solution)/shard_map/all_to_all | solution.py:51
  119.1 0.2 broadcast_select_fusion.1
  119.3 2.6 %collective-permute-start.2 = (f32[4,2,8192]{2,1,0:T(2,128)S(1)}, f32[4,2,8192]{2,1,0:T(2,128)S(1)}, u32[]{:S(2)}, u32[]{:S(2)}) collective-permute-start(f32[4,2,8192]{2,1,0:T(2,128)S(1)} %get-tuple-element.19), channel_id=1, source_target_pairs={{0,1},{1,0},{2,3},{3,2},{4,5},{5,4},{6,7},{7,6},{8,9},{9,8},{10,11... | collective-permute-start | bytes 786440 | tf_op jit(solution)/shard_map/ppermute | solution.py:296
  121.9 24.5 %all-to-all-done.6 = bf16[8,32,8192]{2,1,0:T(8,128)(2,1)} async-done(((bf16[8,32,8192]{2,1,0:T(8,128)(2,1)}), bf16[8,32,8192]{2,1,0:T(8,128)(2,1)}, u32[]{:S(2)}, u32[]{:S(2)}) %all-to-all-start.6) | async-done | bytes 4194336 | tf_op jit(solution)/shard_map/all_to_all | solution.py:51
  146.4 4.6 %collective-permute-start.3 = (bf16[8,32,8192]{2,1,0:T(8,128)(2,1)}, bf16[8,32,8192]{2,1,0:T(8,128)(2,1)S(1)}, u32[]{:S(2)}, u32[]{:S(2)}) collective-permute-start(bf16[8,32,8192]{2,1,0:T(8,128)(2,1)} %all-to-all-done.6), channel_id=1, source_target_pairs={{0,1},{1,0},{2,3},{3,2},{4,5},{5,4},{6,7},{7,6},{8,9},{9,8},{10,11... | collective-permute-start | bytes 12582920 | tf_op jit(solution)/shard_map/ppermute | solution.py:305
  151.0 0.4 maximum_select_fusion
  151.4 0.8 slice_bitcast_fusion
  152.2 4.4 %place_rows.2.refs_0_ = bf16[256,16384]{1,0:T(8,128)(2,1)} custom-call(s32[1]{0:T(128)} %bitcast.3.core_ref, bf16[2,2,2,2,2,8,8192]{6,5,4,3,2,1,0:T(8,128)(2,1)} %bitcast.13.w_ref), custom_call_target="tpu_custom_call" | custom-call | tf_op jit(solution)/shard_map/place_rows/pallas_call | solution.py:236
  156.6 1.4 collective-permute-done.3
  158.0 2.2 %place_rows.3 = bf16[256,16384]{1,0:T(8,128)(2,1)} custom-call(s32[1]{0:T(128)} %bitcast.10.core_ref, bf16[2,2,2,2,2,8,8192]{6,5,4,3,2,1,0:T(8,128)(2,1)S(1)} %bitcast.58, bf16[256,16384]{1,0:T(8,128)(2,1)} %place_rows.2.refs_0_), custom_call_target="tpu_custom_call", output_to_operand_aliasing={{}: (2, {})} | custom-call | tf_op jit(solution)/shard_map/place_rows/pallas_call | solution.py:236
  (24 shorter events, 1.0 us)
Async XLA Ops:
  7.7 31.8 %collective-permute-start.1 = (bf16[256,8192]{1,0:T(8,128)(2,1)}, bf16[256,8192]{1,0:T(8,128)(2,1)}, u32[]{:S(2)}, u32[]{:S(2)}) collective-permute-start(bf16[256,8192]{1,0:T(8,128)(2,1)} %get-tuple-element.7), channel_id=1, source_target_pairs={{0,1},{1,0},{2,3},{3,2},{4,5},{5,4},{6,7},{7,6},{8,9},{9,8},{10,11... | collective-permute-start | bytes 12582920 | tf_op jit(solution)/shard_map/ppermute | solution.py:259
  46.3 4.7 %copy-start = (f32[2,16384]{1,0:T(2,128)S(1)}, f32[2,16384]{1,0:T(2,128)}, u32[]{:S(2)}) copy-start(f32[2,16384]{1,0:T(2,128)} %param.7) | copy-start | bytes 393220
  46.4 4.7 %copy-start.1 = (f32[2,16384]{1,0:T(2,128)S(1)}, f32[2,16384]{1,0:T(2,128)}, u32[]{:S(2)}) copy-start(f32[2,16384]{1,0:T(2,128)} %param.6) | copy-start | bytes 393220
  46.4 4.7 %copy-start.2 = (f32[2,16384]{1,0:T(2,128)S(1)}, f32[2,16384]{1,0:T(2,128)}, u32[]{:S(2)}) copy-start(f32[2,16384]{1,0:T(2,128)} %param.5) | copy-start | bytes 393220
  46.4 33.2 %all-to-all-start.3 = ((bf16[8,32,8192]{2,1,0:T(8,128)(2,1)}), bf16[8,32,8192]{2,1,0:T(8,128)(2,1)}, u32[]{:S(2)}, u32[]{:S(2)}) async-start(bf16[8,32,8192]{2,1,0:T(8,128)(2,1)} %bitcast.59), calls=%async_computation.3 | async-start | bytes 8388608 | tf_op jit(solution)/shard_map/all_to_all | solution.py:51
  51.3 35.9 %collective-permute-start = (f32[3,2,8192]{2,1,0:T(2,128)S(1)}, f32[3,2,8192]{2,1,0:T(2,128)S(1)}, u32[]{:S(2)}, u32[]{:S(2)}) collective-permute-start(f32[3,2,8192]{2,1,0:T(2,128)S(1)} %get-tuple-element.24), channel_id=1, source_target_pairs={{0,1},{1,0},{2,3},{3,2},{4,5},{5,4},{6,7},{7,6},{8,9},{9,8},{10,11... | collective-permute-start | bytes 589832 | tf_op jit(solution)/shard_map/ppermute | solution.py:267
  83.6 11.2 %all-to-all-start.4 = ((f16[8,4,8192]{2,1,0:T(4,128)(2,1)}), f16[8,4,8192]{2,1,0:T(4,128)(2,1)S(1)}, u32[]{:S(2)}, u32[]{:S(2)}) async-start(f16[8,4,8192]{2,1,0:T(4,128)(2,1)} %convert_element_type.32), calls=%async_computation.4 | async-start | bytes 1048576 | tf_op jit(solution)/shard_map/all_to_all | solution.py:51
  114.4 32.0 %all-to-all-start.6 = ((bf16[8,32,8192]{2,1,0:T(8,128)(2,1)}), bf16[8,32,8192]{2,1,0:T(8,128)(2,1)}, u32[]{:S(2)}, u32[]{:S(2)}) async-start(bf16[8,32,8192]{2,1,0:T(8,128)(2,1)} %broadcast_in_dim.72), calls=%async_computation.6 | async-start | bytes 8388608 | tf_op jit(solution)/shard_map/all_to_all | solution.py:51
  119.3 31.8 %collective-permute-start.2 = (f32[4,2,8192]{2,1,0:T(2,128)S(1)}, f32[4,2,8192]{2,1,0:T(2,128)S(1)}, u32[]{:S(2)}, u32[]{:S(2)}) collective-permute-start(f32[4,2,8192]{2,1,0:T(2,128)S(1)} %get-tuple-element.19), channel_id=1, source_target_pairs={{0,1},{1,0},{2,3},{3,2},{4,5},{5,4},{6,7},{7,6},{8,9},{9,8},{10,11... | collective-permute-start | bytes 786440 | tf_op jit(solution)/shard_map/ppermute | solution.py:296
  146.4 11.6 %collective-permute-start.3 = (bf16[8,32,8192]{2,1,0:T(8,128)(2,1)}, bf16[8,32,8192]{2,1,0:T(8,128)(2,1)S(1)}, u32[]{:S(2)}, u32[]{:S(2)}) collective-permute-start(bf16[8,32,8192]{2,1,0:T(8,128)(2,1)} %all-to-all-done.6), channel_id=1, source_target_pairs={{0,1},{1,0},{2,3},{3,2},{4,5},{5,4},{6,7},{7,6},{8,9},{9,8},{10,11... | collective-permute-start | bytes 12582920 | tf_op jit(solution)/shard_map/ppermute | solution.py:305

commit v10 on v9

--- a/solution.py
+++ b/solution.py
@@ -42,8 +42,7 @@
 FAR_GROUPS = groups(FAR)
 BACK_GROUPS = groups(BACK)
 Y_CORES = [[device(x, z, y, core) for core in (0, 1) for y in range(4)] for x in range(4) for z in range(4)]
-X_RING = [[device(x, z, y, core) for x in range(4)] for z in range(4) for y in range(4) for core in (0, 1)]
-Z_RING = [[device(x, z, y, core) for z in range(4)] for x in range(4) for y in range(4) for core in (0, 1)]
+X_Z = [[device(x, z, y, core) for x in range(4) for z in range(4)] for y in range(4) for core in (0, 1)]
 SWAP = [(d, d ^ 1) for d in range(N_DP)]
 
 
@@ -258,8 +257,7 @@
     amax, send = block_max(mine, partials)
     other = lax.ppermute(send, "dp", SWAP)
     amax = jnp.max(exchange(amax, Y_CORES), axis=0)
-    amax = jnp.max(spread(amax, X_RING), axis=0)
-    amax = jnp.max(spread(amax, Z_RING), axis=0)
+    amax = jnp.max(spread(amax, X_Z), axis=0)
 
     state = jnp.stack([master, moment_one, moment_two])
     state_own = lax.dynamic_slice_in_dim(state, core * HALF, HALF, 2)

time: 161 us -> 159 us (0.988)
  starting transfers between devices: 24.9 us -> 20.7 us
  waiting for transfers between devices: 57.1 us -> 59.6 us
    all_to_all x3, waiting for transfers between devices: 55.7 us -> 58.2 us  [exchange(): return lax.all_to_all(x, 'dp', 0, 0, axis_index_groups=among)]
    all_to_all x4 -> x3, blocking collectives: 45 us -> 44.6 us  [exchange(): return lax.all_to_all(x, 'dp', 0, 0, axis_index_groups=among)]
where the time goes in v10:
time: 159 us; the launch traced here: 158 us
  waiting for transfers between devices  59.6 us (37%)
  blocking collectives  44.6 us (28%)
  starting transfers between devices  20.7 us (13%)
  Pallas kernels  20.5 us (13%)
  other arithmetic  6.91 us (4%)
  local copies, waits for them, and re-layouts  4.98 us (3%)
    all_to_all x3, waiting for transfers between devices, exchange(): return lax.all_to_all(x, 'dp', 0, 0, axis_index_groups=among)  58.2 us
    all_to_all x3, blocking collectives, exchange(): return lax.all_to_all(x, 'dp', 0, 0, axis_index_groups=among)  44.6 us
    all_to_all x3, starting transfers between devices, exchange(): return lax.all_to_all(x, 'dp', 0, 0, axis_index_groups=among)  12.9 us
    pallas_call x1, Pallas kernels, block_max(): pl.pallas_call(max_kernel, out_shape=(jax.ShapeDtypeStruct((8, 128, 128),...  7.07 us
    pallas_call x1, Pallas kernels, quantise(): pl.pallas_call(quant_kernel, out_shape=jax.ShapeDtypeStruct((2, 2, 2, 2,...  6.85 us
    pallas_call x2, Pallas kernels, place_rows(): pl.pallas_call(rows_kernel, out_shape=jax.ShapeDtypeStruct((ROWS, W), BF1...  6.57 us
  transfers between devices with their start and end apart: 7, of which 4 were waited for; matrix products, arithmetic and copies ran while one was open for 5% of the time, Pallas kernels for 3%

profile of v10, /device:TPU:1, one launch (start us, length us, event | category | flops | bytes accessed | tf_op | source)
XLA Modules:
  0.0 158.4 jit_solution(5021639354216751550)
XLA Ops:
  0.6 7.1 %block_max.1 = (bf16[8,128,128]{2,1,0:T(8,128)(2,1)}, bf16[256,8192]{1,0:T(8,128)(2,1)}) custom-call(s32[1]{0:T(128)} %bitcast.3.core_ref, bf16[1,256,16384]{2,1,0:T(8,128)(2,1)} %x_ref.3), custom_call_target="tpu_custom_call" | custom-call | tf_op jit(solution)/shard_map/block_max/pallas_call | solution.py:101
  7.7 1.5 collective-permute-start.1
  9.2 11.2 %all_to_all.30 = bf16[8,128,128]{2,1,0:T(8,128)(2,1)S(1)} all-to-all(bf16[8,128,128]{2,1,0:T(8,128)(2,1)} %get-tuple-element.8), channel_id=1, replica_groups={{0,2,4,6,1,3,5,7},{8,10,12,14,9,11,13,15},{16,18,20,22,17,19,21,23},{24..., dimensions={0} | all-to-all | bytes 524288 | tf_op jit(solution)/shard_map/all_to_all | solution.py:50
  20.6 17.8 %all_to_all.31 = bf16[16,128,128]{2,1,0:T(8,128)(2,1)S(1)} all-to-all(bf16[16,128,128]{2,1,0:T(8,128)(2,1)S(1)} %broadcast_in_dim.60), channel_id=1, replica_groups={{0,8,16,24,32,40,48,56,64,72,80,88,96,104,112,120},{1,9,17,25,33,41,49,..., dimensions={0} | all-to-all | bytes 1048576 | tf_op jit(solution)/shard_map/all_to_all | solution.py:50
  38.3 0.7 reduce_max.28.amax_ref
  39.0 6.8 %quantise.1 = bf16[2,2,2,2,2,8,8192]{6,5,4,3,2,1,0:T(8,128)(2,1)} custom-call(s32[1]{0:T(128)} %bitcast.3.core_ref, bf16[1,256,16384]{2,1,0:T(8,128)(2,1)} %x_ref.3, bf16[256,8192]{1,0:T(8,128)(2,1)} %collective-permute-done.1.other_ref, bf16[128,128]{1,0:T(8,128)(2,1)} %reduce_max.28.amax_ref), custom_call_target="tpu_custom_call" | custom-call | tf_op jit(solution)/shard_map/quantise/pallas_call | solution.py:190
  45.9 4.7 %all-to-all-start.2 = ((bf16[8,32,8192]{2,1,0:T(8,128)(2,1)}), bf16[8,32,8192]{2,1,0:T(8,128)(2,1)}, u32[]{:S(2)}, u32[]{:S(2)}) async-start(bf16[8,32,8192]{2,1,0:T(8,128)(2,1)} %bitcast.59), calls=%async_computation.2 | async-start | bytes 8388608 | tf_op jit(solution)/shard_map/all_to_all | solution.py:50
  50.7 0.2 pad_maximum_fusion.1
  50.9 2.2 %collective-permute-start = (f32[3,2,8192]{2,1,0:T(2,128)S(1)}, f32[3,2,8192]{2,1,0:T(2,128)S(1)}, u32[]{:S(2)}, u32[]{:S(2)}) collective-permute-start(f32[3,2,8192]{2,1,0:T(2,128)S(1)} %get-tuple-element.24), channel_id=1, source_target_pairs={{0,1},{1,0},{2,3},{3,2},{4,5},{5,4},{6,7},{7,6},{8,9},{9,8},{10,11... | collective-permute-start | bytes 589832 | tf_op jit(solution)/shard_map/ppermute | solution.py:265
  53.1 26.0 %all-to-all-done.2 = bf16[8,32,8192]{2,1,0:T(8,128)(2,1)} async-done(((bf16[8,32,8192]{2,1,0:T(8,128)(2,1)}), bf16[8,32,8192]{2,1,0:T(8,128)(2,1)}, u32[]{:S(2)}, u32[]{:S(2)}) %all-to-all-start.2) | async-done | bytes 4194336 | tf_op jit(solution)/shard_map/all_to_all | solution.py:50
  79.0 2.9 %convert_reduce_fusion = f32[32,8192]{1,0:T(8,128)S(1)} fusion(bf16[8,32,8192]{2,1,0:T(8,128)(2,1)} %all-to-all-done.2), kind=kLoop, calls=%fused_computation | loop fusion | flops 3932160 | bytes 5242880 | tf_op jit(solution)/shard_map/reduce_sum | solution.py:274
  82.0 1.0 convert_element_type.32
  83.0 3.7 %all-to-all-start.3 = ((f16[8,4,8192]{2,1,0:T(4,128)(2,1)}), f16[8,4,8192]{2,1,0:T(4,128)(2,1)S(1)}, u32[]{:S(2)}, u32[]{:S(2)}) async-start(f16[8,4,8192]{2,1,0:T(4,128)(2,1)} %convert_element_type.32), calls=%async_computation.3 | async-start | bytes 1048576 | tf_op jit(solution)/shard_map/all_to_all | solution.py:50
  86.7 0.3 maximum_select_fusion.1
  87.1 0.8 select_multiply_fusion
  88.0 6.2 %all-to-all-done.3 = f16[8,4,8192]{2,1,0:T(4,128)(2,1)S(1)} async-done(((f16[8,4,8192]{2,1,0:T(4,128)(2,1)}), f16[8,4,8192]{2,1,0:T(4,128)(2,1)S(1)}, u32[]{:S(2)}, u32[]{:S(2)}) %all-to-all-start.3) | async-done | bytes 524320 | tf_op jit(solution)/shard_map/all_to_all | solution.py:50
  94.2 0.6 convert_reduce_fusion.1
  94.8 0.3 fusion.9
  95.3 0.3 fusion.12
  95.5 0.1 broadcast_in_dim.63
  95.7 15.6 %all_to_all.32 = bf16[8,4,8192]{2,1,0:T(4,128)(2,1)S(1)} all-to-all(bf16[8,4,8192]{2,1,0:T(4,128)(2,1)S(1)} %broadcast_in_dim.63), channel_id=1, replica_groups={{32,34,40,42,64,66,72,74},{38,36,46,44,70,68,78,76},{56,58,48,50,88,90,..., dimensions={0} | all-to-all | bytes 1048576 | tf_op jit(solution)/shard_map/all_to_all | solution.py:50
  111.4 2.5 %broadcast_in_dim.65 = bf16[8,32,8192]{2,1,0:T(8,128)(2,1)} broadcast(bf16[32,8192]{1,0:T(8,128)(2,1)S(1)} %broadcast_in_dim.64), dimensions={1,2} | broadcast | bytes 4718592 | tf_op jit(solution)/shard_map/broadcast_in_dim | solution.py:54
  113.9 4.6 %all-to-all-start.5 = ((bf16[8,32,8192]{2,1,0:T(8,128)(2,1)}), bf16[8,32,8192]{2,1,0:T(8,128)(2,1)}, u32[]{:S(2)}, u32[]{:S(2)}) async-start(bf16[8,32,8192]{2,1,0:T(8,128)(2,1)} %broadcast_in_dim.65), calls=%async_computation.5 | async-start | bytes 8388608 | tf_op jit(solution)/shard_map/all_to_all | solution.py:50
  118.6 0.2 broadcast_select_fusion.1
  118.8 1.1 collective-permute-start.2
  119.9 26.1 %all-to-all-done.5 = bf16[8,32,8192]{2,1,0:T(8,128)(2,1)} async-done(((bf16[8,32,8192]{2,1,0:T(8,128)(2,1)}), bf16[8,32,8192]{2,1,0:T(8,128)(2,1)}, u32[]{:S(2)}, u32[]{:S(2)}) %all-to-all-start.5) | async-done | bytes 4194336 | tf_op jit(solution)/shard_map/all_to_all | solution.py:50
  146.0 3.0 %collective-permute-start.3 = (bf16[8,32,8192]{2,1,0:T(8,128)(2,1)}, bf16[8,32,8192]{2,1,0:T(8,128)(2,1)S(1)}, u32[]{:S(2)}, u32[]{:S(2)}) collective-permute-start(bf16[8,32,8192]{2,1,0:T(8,128)(2,1)} %all-to-all-done.5), channel_id=1, source_target_pairs={{0,1},{1,0},{2,3},{3,2},{4,5},{5,4},{6,7},{7,6},{8,9},{9,8},{10,11... | collective-permute-start | bytes 12582920 | tf_op jit(solution)/shard_map/ppermute | solution.py:303
  149.0 0.4 maximum_select_fusion
  149.4 0.8 slice_bitcast_fusion
  150.2 4.4 %place_rows.2.refs_0_ = bf16[256,16384]{1,0:T(8,128)(2,1)} custom-call(s32[1]{0:T(128)} %bitcast.3.core_ref, bf16[2,2,2,2,2,8,8192]{6,5,4,3,2,1,0:T(8,128)(2,1)} %bitcast.13.w_ref), custom_call_target="tpu_custom_call" | custom-call | tf_op jit(solution)/shard_map/place_rows/pallas_call | solution.py:235
  154.6 1.4 collective-permute-done.3
  156.0 2.2 %place_rows.3 = bf16[256,16384]{1,0:T(8,128)(2,1)} custom-call(s32[1]{0:T(128)} %bitcast.10.core_ref, bf16[2,2,2,2,2,8,8192]{6,5,4,3,2,1,0:T(8,128)(2,1)S(1)} %bitcast.58, bf16[256,16384]{1,0:T(8,128)(2,1)} %place_rows.2.refs_0_), custom_call_target="tpu_custom_call", output_to_operand_aliasing={{}: (2, {})} | custom-call | tf_op jit(solution)/shard_map/place_rows/pallas_call | solution.py:235
  (21 shorter events, 0.9 us)
Async XLA Ops:
  7.7 31.3 %collective-permute-start.1 = (bf16[256,8192]{1,0:T(8,128)(2,1)}, bf16[256,8192]{1,0:T(8,128)(2,1)}, u32[]{:S(2)}, u32[]{:S(2)}) collective-permute-start(bf16[256,8192]{1,0:T(8,128)(2,1)} %get-tuple-element.7), channel_id=1, source_target_pairs={{0,1},{1,0},{2,3},{3,2},{4,5},{5,4},{6,7},{7,6},{8,9},{9,8},{10,11... | collective-permute-start | bytes 12582920 | tf_op jit(solution)/shard_map/ppermute | solution.py:258
  45.9 4.7 %copy-start = (f32[2,16384]{1,0:T(2,128)S(1)}, f32[2,16384]{1,0:T(2,128)}, u32[]{:S(2)}) copy-start(f32[2,16384]{1,0:T(2,128)} %param.7) | copy-start | bytes 393220
  45.9 4.7 %copy-start.1 = (f32[2,16384]{1,0:T(2,128)S(1)}, f32[2,16384]{1,0:T(2,128)}, u32[]{:S(2)}) copy-start(f32[2,16384]{1,0:T(2,128)} %param.6) | copy-start | bytes 393220
  45.9 4.7 %copy-start.2 = (f32[2,16384]{1,0:T(2,128)S(1)}, f32[2,16384]{1,0:T(2,128)}, u32[]{:S(2)}) copy-start(f32[2,16384]{1,0:T(2,128)} %param.5) | copy-start | bytes 393220
  45.9 33.1 %all-to-all-start.2 = ((bf16[8,32,8192]{2,1,0:T(8,128)(2,1)}), bf16[8,32,8192]{2,1,0:T(8,128)(2,1)}, u32[]{:S(2)}, u32[]{:S(2)}) async-start(bf16[8,32,8192]{2,1,0:T(8,128)(2,1)} %bitcast.59), calls=%async_computation.2 | async-start | bytes 8388608 | tf_op jit(solution)/shard_map/all_to_all | solution.py:50
  50.9 35.8 %collective-permute-start = (f32[3,2,8192]{2,1,0:T(2,128)S(1)}, f32[3,2,8192]{2,1,0:T(2,128)S(1)}, u32[]{:S(2)}, u32[]{:S(2)}) collective-permute-start(f32[3,2,8192]{2,1,0:T(2,128)S(1)} %get-tuple-element.24), channel_id=1, source_target_pairs={{0,1},{1,0},{2,3},{3,2},{4,5},{5,4},{6,7},{7,6},{8,9},{9,8},{10,11... | collective-permute-start | bytes 589832 | tf_op jit(solution)/shard_map/ppermute | solution.py:265
  83.0 11.2 %all-to-all-start.3 = ((f16[8,4,8192]{2,1,0:T(4,128)(2,1)}), f16[8,4,8192]{2,1,0:T(4,128)(2,1)S(1)}, u32[]{:S(2)}, u32[]{:S(2)}) async-start(f16[8,4,8192]{2,1,0:T(4,128)(2,1)} %convert_element_type.32), calls=%async_computation.3 | async-start | bytes 1048576 | tf_op jit(solution)/shard_map/all_to_all | solution.py:50
  113.9 32.1 %all-to-all-start.5 = ((bf16[8,32,8192]{2,1,0:T(8,128)(2,1)}), bf16[8,32,8192]{2,1,0:T(8,128)(2,1)}, u32[]{:S(2)}, u32[]{:S(2)}) async-start(bf16[8,32,8192]{2,1,0:T(8,128)(2,1)} %broadcast_in_dim.65), calls=%async_computation.5 | async-start | bytes 8388608 | tf_op jit(solution)/shard_map/all_to_all | solution.py:50
  118.8 30.2 %collective-permute-start.2 = (f32[4,2,8192]{2,1,0:T(2,128)S(1)}, f32[4,2,8192]{2,1,0:T(2,128)S(1)}, u32[]{:S(2)}, u32[]{:S(2)}) collective-permute-start(f32[4,2,8192]{2,1,0:T(2,128)S(1)} %get-tuple-element.19), channel_id=1, source_target_pairs={{0,1},{1,0},{2,3},{3,2},{4,5},{5,4},{6,7},{7,6},{8,9},{9,8},{10,11... | collective-permute-start | bytes 786440 | tf_op jit(solution)/shard_map/ppermute | solution.py:294
  146.0 10.0 %collective-permute-start.3 = (bf16[8,32,8192]{2,1,0:T(8,128)(2,1)}, bf16[8,32,8192]{2,1,0:T(8,128)(2,1)S(1)}, u32[]{:S(2)}, u32[]{:S(2)}) collective-permute-start(bf16[8,32,8192]{2,1,0:T(8,128)(2,1)} %all-to-all-done.5), channel_id=1, source_target_pairs={{0,1},{1,0},{2,3},{3,2},{4,5},{5,4},{6,7},{7,6},{8,9},{9,8},{10,11... | collective-permute-start | bytes 12582920 | tf_op jit(solution)/shard_map/ppermute | solution.py:303
